TPU v7x, 32 devices: a whole 2x2x4 slice. The times are simulated.
32 devices in a mesh: row: 8 (over z, core), rep: 4 (over y, x).
Axes of the slice: x: 2, y: 2, z: 4, core: 2. Of those that a mesh axis runs over, the one named last changes fastest.
Arguments:
- features: bfloat16 [1024, 512], P('row', 'rep'), may hold values from -6 to 6
- edge_tiles: bfloat16 [8, 8, 128, 128], P('row'), may hold values from -0.3125 to 0.3125
- sources: int32 [8, 8], P('row'), may hold values from 0 to 7, as said below
- counts: int32 [8], P('row'), may hold values from 1 to 8, as said below
- w_first: bfloat16 [512, 512], P('rep'), may hold values from -0.25 to 0.25
- w_second: bfloat16 [512, 512], P('rep'), may hold values from -0.25 to 0.25
- cotangent: bfloat16 [1024, 512], P('row', 'rep'), may hold values from -6 to 6
Outputs:
- embeddings: bfloat16 [1024, 512], P('row', 'rep')
- grad_first: float32 [512, 512], P('rep')
- grad_second: float32 [512, 512], P('rep')
Inputs may be any that keep to these rules, and one draw needn't show every extreme that they name: `sources`: the 8 source blocks of one block row are distinct. `counts`: some block row has all 8 slots live.
All inputs are finite; a program needn't handle non-finite values.
Results may differ from a plain program's by a relative error of at most 0.0065.
Values may be sent and summed in bfloat16 or wider, within the bound.
No kernel may reach another device: no remote copies, remote signals or barrier semaphores. Data moves between devices by JAX's collectives and lax.ppermute only.
A program may use at most 64 MiB of HBM per device.

v0:
```python
import math

import jax
import jax.numpy as jnp
from jax import lax
from jax.sharding import PartitionSpec as P


def silu_slope(value):
    sig = jax.nn.sigmoid(value)
    return sig * (1.0 + value * (1.0 - sig))


def gather_blocks(local, block):
    height, width = local.shape
    packed = local.reshape(height * width // 128, 128)
    whole = lax.all_gather(packed, "row", axis=0, tiled=True)
    return whole.reshape(-1, block, width)


def aggregate(local, live_tiles, sources):
    height, width = local.shape
    group_rows, slots, block, _ = live_tiles.shape
    blocks = gather_blocks(local, block)
    total = jnp.einsum(
        "bkij,bkjf->bif", live_tiles, blocks[sources], preferred_element_type=jnp.float32
    )
    return total.reshape(height, width).astype(jnp.bfloat16)


def spread_back(back_agg, live_tiles):
    group_rows, slots, block, _ = live_tiles.shape
    width = back_agg.shape[1]
    block_rows = back_agg.reshape(group_rows, block, width)
    return jnp.einsum("bkij,bif->bkjf", live_tiles, block_rows, preferred_element_type=jnp.float32)


def mix_columns(agg, weight):
    partial_terms = jnp.dot(agg, weight, preferred_element_type=jnp.float32)
    return lax.psum_scatter(partial_terms, "rep", scatter_dimension=1, tiled=True)


def widen(local):
    return lax.all_gather(local, "rep", axis=1, tiled=True)


def body(features, edge_tiles, sources, counts, w_first, w_second, cotangent):
    group_rows, slots, block, _ = edge_tiles.shape
    height, width = features.shape
    live = jnp.arange(slots, dtype=jnp.int32)[None, :] < counts[:, None]
    live_tiles = edge_tiles * live[:, :, None, None].astype(edge_tiles.dtype)
    scale = 1.0 / math.sqrt(height * lax.axis_size("row"))
    agg_first = aggregate(features, live_tiles, sources)
    pre_first = mix_columns(agg_first, w_first)
    hidden = jax.nn.silu(pre_first).astype(jnp.bfloat16)
    agg_second = aggregate(hidden, live_tiles, sources)
    embeddings = mix_columns(agg_second, w_second).astype(jnp.bfloat16)
    full_cotangent = widen(cotangent)
    second_part = jnp.dot(agg_second.T, full_cotangent, preferred_element_type=jnp.float32) * scale
    back_agg = jnp.dot(full_cotangent, w_second.T, preferred_element_type=jnp.float32).astype(
        jnp.bfloat16
    )
    contrib = spread_back(back_agg, live_tiles)
    flat_sources = sources.reshape(-1)
    flat_contrib = contrib.reshape(group_rows * slots, block * width)
    count = height * lax.axis_size("row")
    wanted = count // block
    inside = (flat_sources >= 0) & (flat_sources < wanted)
    target = jnp.where(inside, flat_sources, wanted)
    summed = jax.ops.segment_sum(flat_contrib, target, num_segments=wanted + 1)
    back_hidden = lax.psum_scatter(
        summed[:wanted].reshape(count, width), "row", scatter_dimension=0, tiled=True
    )
    back_pre = (back_hidden * silu_slope(pre_first)).astype(jnp.bfloat16)
    first_part = jnp.dot(agg_first.T, widen(back_pre), preferred_element_type=jnp.float32) * scale
    grad_second, grad_first = lax.psum((second_part, first_part), "row")
    return (embeddings, grad_first, grad_second)


def solution(mesh):
    placed = (
        P("row", "rep"),
        P("row", None, None, None),
        P("row", None),
        P("row"),
        P("rep", None),
        P("rep", None),
        P("row", "rep"),
    )
    return jax.shard_map(
        body,
        mesh=mesh,
        in_specs=placed,
        out_specs=(P("row", "rep"), P("rep", None), P("rep", None)),
        check_vma=False,
    )
```

profile of v0, /device:TPU:0, one launch (start us, length us, event | category | flops | bytes accessed | tf_op | source)
XLA Modules:
  0.0 194.0 jit_solution(15451476026461485404)
XLA Ops:
  7.9 16.1 %all_gather.12 = bf16[1024,128]{1,0:T(8,128)(2,1)S(1)} all-gather(bf16[128,128]{1,0:T(8,128)(2,1)} %param.7), channel_id=1, replica_groups=mesh['row'=8,'rep'=4] {'row'}, dimensions={0}, use_global_device_ids=true | all-gather | bytes 294912 | tf_op jit(solution)/shard_map/all_gather | solution.py:17
  24.1 0.6 gather_fusion
  24.7 0.3 copy-done.2
  25.3 0.6 copy-done.3
  25.9 0.9 fusion.18
  26.9 0.7 copy-done.4
  27.6 8.5 %all_gather.14 = bf16[128,512]{1,0:T(8,128)(2,1)S(1)} all-gather(bf16[128,128]{1,0:T(8,128)(2,1)S(1)} %copy-done.4), channel_id=1, replica_groups=mesh['row'=8,'rep'=4] {'rep'}, dimensions={1}, use_global_device_ids=true | all-gather | bytes 163840 | tf_op jit(solution)/shard_map/all_gather | solution.py:44
  36.0 0.4 convolution_bitcast_fusion
  36.5 1.7 scatter_custom_fusion
  38.2 0.9 reshape.96
  39.2 13.2 %reduce-scatter.4.cloned.1.call-done = f32[128,128]{1,0:T(8,128)} async-done(((f32[128,512]{1,0:T(8,128)}), f32[128,128]{1,0:T(8,128)}) %reduce-scatter.4.cloned.1.call-update) | async-done | bytes 65552 | tf_op jit(solution)/shard_map/reduce_scatter | solution.py:40
  52.4 33.7 %reduce-scatter.8.cloned.1.call-done = f32[128,128]{1,0:T(8,128)} async-done(((f32[1024,128]{1,0:T(8,128)}), f32[128,128]{1,0:T(8,128)}) %reduce-scatter.8.cloned.1.call-update) | async-done | bytes 65552 | tf_op jit(solution)/shard_map/reduce_scatter | solution.py:71
  86.1 0.9 multiply_convert_fusion
  87.0 14.2 %all_gather.13 = bf16[1024,128]{1,0:T(8,128)(2,1)S(1)} all-gather(bf16[128,128]{1,0:T(8,128)(2,1)S(1)} %get-tuple-element.6), channel_id=1, replica_groups=mesh['row'=8,'rep'=4] {'row'}, dimensions={0}, use_global_device_ids=true | all-gather | bytes 294912 | tf_op jit(solution)/shard_map/all_gather | solution.py:17
  101.2 0.6 gather_fusion.1
  102.1 0.9 fusion.19
  103.0 8.3 %all_gather.15 = bf16[128,512]{1,0:T(8,128)(2,1)S(1)} all-gather(bf16[128,128]{1,0:T(8,128)(2,1)S(1)} %get-tuple-element.5), channel_id=1, replica_groups=mesh['row'=8,'rep'=4] {'rep'}, dimensions={1}, use_global_device_ids=true | all-gather | bytes 163840 | tf_op jit(solution)/shard_map/all_gather | solution.py:44
  111.3 0.9 convolution_multiply_fusion
  112.3 0.9 convolution_multiply_fusion.1
  113.2 12.4 %reduce-scatter.6.cloned.1.call-done = f32[128,128]{1,0:T(8,128)} async-done(((f32[128,512]{1,0:T(8,128)}), f32[128,128]{1,0:T(8,128)}) %reduce-scatter.6.cloned.1.call-update) | async-done | bytes 65552 | tf_op jit(solution)/shard_map/reduce_scatter | solution.py:40
  125.6 1.5 convert_element_type.30
  127.1 58.0 %all-reduce.3.cloned.1.call-done = (f32[128,512]{1,0:T(8,128)}, f32[128,512]{1,0:T(8,128)}) async-done(((f32[128,512]{1,0:T(8,128)}, f32[128,512]{1,0:T(8,128)}), (f32[128,512]{1,0:T(8,128)}, f32[128,512]{1,0:T(8,128)})) %all-reduce.3.cloned.1.call-update) | async-done | bytes 524304 | tf_op jit(solution)/shard_map/psum | solution.py:76
  185.1 1.7 copy.20
  186.8 0.7 copy.21
  (24 shorter events, 0.8 us)
Async XLA Ops:
  7.2 28.8 %copy-start = (bf16[128,512]{1,0:T(8,128)(2,1)S(1)}, bf16[128,512]{1,0:T(8,128)(2,1)}, u32[]{:S(2)}) copy-start(bf16[128,512]{1,0:T(8,128)(2,1)} %param.12) | copy-start | bytes 393220
  7.2 45.2 %reduce-scatter.4.cloned.1.call-start = ((), (), s32[]{:S(2)}) async-start(), calls=%async_computation.3 | async-start | bytes 327680 | tf_op jit(solution)/shard_map/reduce_scatter | solution.py:40
  7.9 16.1 %copy-start.5 = (s32[1,8]{1,0:T(1,128)S(1)}, s32[1,8]{1,0:T(1,128)}, u32[]{:S(2)}) copy-start(s32[1,8]{1,0:T(1,128)} %param.9) | copy-start | bytes 100
  24.1 1.0 copy-start.2
  25.0 0.9 copy-start.3
  26.8 0.8 copy-start.4
  26.8 59.3 %reduce-scatter.8.cloned.1.call-start = ((), (), s32[]{:S(2)}) async-start(), calls=%async_computation.5 | async-start | bytes 589824 | tf_op jit(solution)/shard_map/reduce_scatter | solution.py:71
  39.1 86.5 %reduce-scatter.6.cloned.1.call-start = ((), (), s32[]{:S(2)}) async-start(), calls=%async_computation.4 | async-start | bytes 327680 | tf_op jit(solution)/shard_map/reduce_scatter | solution.py:40
  103.0 82.1 %all-reduce.3.cloned.1.call-start = ((), (), s32[]{:S(2)}) async-start(), calls=%async_computation.6 | async-start | bytes 1048576 | tf_op jit(solution)/shard_map/psum | solution.py:76
  185.1 1.7 copy-start.1
Sparse Core Ops, SparseCore 0:
  26.9 25.4 reduce-scatter.3
  54.7 31.3 reduce-scatter.7
  103.1 22.4 reduce-scatter.5
  128.4 56.6 all-reduce.2
where the time goes:
time: 194 us
  waiting for transfers between devices  117 us (60%)
  blocking collectives  47.1 us (24%)
  between operations  14.5 us (7%)
  local copies, waits for them, and re-layouts  6.2 us (3%)
  matrix products  4.55 us (2%)
  other arithmetic  4.11 us (2%)
    psum x1, waiting for transfers between devices, body(): grad_second, grad_first = lax.psum((second_part, first_part), 'row')  58 us
    reduce_scatter x1, waiting for transfers between devices, body(): lax.psum_scatter(summed[:wanted].reshape(count, width), 'row', scatter_di...  33.7 us
    all_gather x2, blocking collectives, gather_blocks(): whole = lax.all_gather(packed, 'row', axis=0, tiled=True)  30.3 us
    reduce_scatter x2, waiting for transfers between devices, mix_columns(): lax.psum_scatter(partial_terms, 'rep', scatter_dimension=1, tiled=True)  25.6 us
    all_gather x2, blocking collectives, widen(): return lax.all_gather(local, 'rep', axis=1, tiled=True)  16.8 us
    unnamed x14, local copies, waits for them, and re-layouts  4.09 us
  transfers between devices with their start and end apart: 4, of which 4 were waited for; matrix products, arithmetic and copies ran while one was open for 3% of the time, Pallas kernels for 0%

commit v1 on v0

--- a/solution.py
+++ b/solution.py
@@ -1,9 +1,17 @@
+import functools
 import math
 
 import jax
 import jax.numpy as jnp
 from jax import lax
+from jax.experimental import pallas as pl
+from jax.experimental.pallas import tpu as pltpu
 from jax.sharding import PartitionSpec as P
+
+BF16 = jnp.bfloat16
+F32 = jnp.float32
+CORES = 2
+REPLICATED_BYTES = 16 * 2**20
 
 
 def silu_slope(value):
@@ -20,7 +28,7 @@
 
 def aggregate(local, live_tiles, sources):
     height, width = local.shape
-    group_rows, slots, block, _ = live_tiles.shape
+    _, _, block, _ = live_tiles.shape
     blocks = gather_blocks(local, block)
     total = jnp.einsum(
         "bkij,bkjf->bif", live_tiles, blocks[sources], preferred_element_type=jnp.float32
@@ -29,7 +37,7 @@
 
 
 def spread_back(back_agg, live_tiles):
-    group_rows, slots, block, _ = live_tiles.shape
+    group_rows, _, block, _ = live_tiles.shape
     width = back_agg.shape[1]
     block_rows = back_agg.reshape(group_rows, block, width)
     return jnp.einsum("bkij,bif->bkjf", live_tiles, block_rows, preferred_element_type=jnp.float32)
@@ -44,7 +52,7 @@
     return lax.all_gather(local, "rep", axis=1, tiled=True)
 
 
-def body(features, edge_tiles, sources, counts, w_first, w_second, cotangent):
+def split_body(features, edge_tiles, sources, counts, w_first, w_second, cotangent):
     group_rows, slots, block, _ = edge_tiles.shape
     height, width = features.shape
     live = jnp.arange(slots, dtype=jnp.int32)[None, :] < counts[:, None]
@@ -77,6 +85,233 @@
     return (embeddings, grad_first, grad_second)
 
 
+def dot(a, b, contract):
+    return lax.dot_general(a, b, (contract, ((), ())), preferred_element_type=F32)
+
+
+def pack_kernel(
+    chips, parts, sources_ref, counts_ref, feat_ref, cot_ref, tiles_ref, w1_ref, w2_ref, *outs
+):
+    for_chips, for_reps, row_ref, sems = outs
+    _, slots, block, _ = tiles_ref.shape
+    width = feat_ref.shape[1]
+    core = lax.rem(lax.axis_index("row"), CORES)
+    moves = [
+        (feat_ref, for_reps.at[0, :, pl.ds(0, width)]),
+        (cot_ref, for_reps.at[0, :, pl.ds(width, width)]),
+    ]
+    copies = [pltpu.make_async_copy(*move, sems.at[slots + n]) for n, move in enumerate(moves)]
+    for copy in copies:
+        copy.start()
+    step = for_reps.shape[2]
+    halves = w1_ref.shape[1] // step
+
+    def weight_copy(ref, n):
+        lanes = pl.ds(n * step, step)
+        return pltpu.make_async_copy(ref.at[:, lanes], for_reps.at[1 + n], sems.at[slots + 2 + n])
+
+    for c, ref in enumerate((w1_ref, w2_ref)):
+        for n in range(halves):
+            pl.when(core == c)(lambda ref=ref, n=n: weight_copy(ref, n).start())
+    row_ref[...] = jnp.zeros_like(row_ref)
+
+    def tile_copy(k):
+        source = sources_ref[0, k]
+        position = lax.rem(source, CORES) * chips + lax.div(source, CORES)
+        columns = pl.ds(pl.multiple_of(position * block, block), block)
+        return pltpu.make_async_copy(tiles_ref.at[0, k], row_ref.at[:, columns], sems.at[k])
+
+    for k in range(slots):
+        pl.when(k < counts_ref[0])(lambda k=k: tile_copy(k).start())
+    for copy in copies:
+        copy.wait()
+    for_chips[0] = for_reps[0]
+    for k in range(slots):
+        pl.when(k < counts_ref[0])(lambda k=k: tile_copy(k).wait())
+    share = parts * block
+    start = pl.multiple_of(lax.axis_index("rep") * share, share)
+    for_chips[1] = row_ref[:, pl.ds(start, share)]
+    for c, ref in enumerate((w1_ref, w2_ref)):
+        for n in range(halves):
+            pl.when(core == c)(lambda ref=ref, n=n: weight_copy(ref, n).wait())
+
+
+def join_kernel(*refs):
+    out_ref = refs[-1]
+    size = refs[0].shape[0]
+    for n, ref in enumerate(refs[:-1]):
+        out_ref[pl.ds(n * size, size)] = ref[...]
+
+
+def layers_kernel(chips, reps, scale, *refs):
+    count = CORES * reps
+    locals_, nears, fars, refs = (*(refs[n * count :][:count] for n in range(3)), refs[3 * count :])
+    own_rows, refs = refs[:CORES], refs[CORES:]
+    emb_ref, gf_ref, gs_ref, a_s, f_s, c_s, w_s, af_s, hid_s, slope_s, ba_s = refs
+    row, rep = lax.axis_index("row"), lax.axis_index("rep")
+    core, chip = lax.rem(row, CORES), lax.div(row, CORES)
+    height, width = emb_ref.shape
+    nodes, wide = f_s.shape
+    share = nodes // reps
+
+    def at(index, size):
+        return pl.ds(pl.multiple_of(index * size, size), size)
+
+    for d in range(reps):
+        q = rep ^ d
+        for dc in range(CORES):
+            n, c = dc * reps + d, core ^ dc
+
+            def place(ref, first, dz, q=q, c=c):
+                rows = at(c * chips + (chip ^ dz), height)
+                f_s[rows, at(q, width)] = ref[first, :, :width]
+                c_s[rows, at(q, width)] = ref[first, :, width:]
+                if dz:
+                    a_s[rows, at(q, share)] = ref[first + 1]
+
+            place(locals_[n], 0, 0)
+            place(nears[n], 0, 1)
+            for dz in range(2, chips):
+                place(fars[n], 2 * (dz - 2), dz)
+            step = locals_[n].shape[2]
+            for h in range(wide // step):
+                w_s[c, at(q, width), h * step : (h + 1) * step] = locals_[n][1 + h]
+    for dc in range(CORES):
+        a_s[at((core ^ dc) * chips + chip, height)] = own_rows[dc][...]
+
+    my_cols = at(rep, width)
+    step = 2 * height
+
+    def forward(i, _):
+        rows = at(i, step)
+        agg = dot(a_s[rows, :], f_s[...], ((1,), (0,))).astype(BF16)
+        af_s[rows, :] = agg
+        pre = dot(agg, w_s[0], ((1,), (0,)))
+        sig = jax.nn.sigmoid(pre)
+        hid_s[rows, :] = (pre * sig).astype(BF16)
+        slope_s[rows, :] = sig * (1.0 + pre * (1.0 - sig))
+        ba_s[rows, :] = dot(c_s[rows, :], w_s[1], ((1,), (1,))).astype(BF16)
+        return 0
+
+    lax.fori_loop(0, nodes // step, forward, 0)
+
+    gf_ref[...] = jnp.zeros_like(gf_ref)
+    gs_ref[...] = jnp.zeros_like(gs_ref)
+
+    def backward(i, _):
+        rows = at(i, step)
+        back_hidden = dot(a_s[:, rows], ba_s[...], ((0,), (0,)))
+        back_pre = (back_hidden * slope_s[rows, :]).astype(BF16)
+        gf_ref[...] += dot(af_s[rows, my_cols], back_pre, ((0,), (0,)))
+        agg = dot(a_s[rows, :], hid_s[:, my_cols], ((1,), (0,))).astype(BF16)
+        gs_ref[...] += dot(agg, c_s[rows, :], ((0,), (0,)))
+        return 0
+
+    lax.fori_loop(0, nodes // step, backward, 0)
+    gf_ref[...] = gf_ref[...] * scale
+    gs_ref[...] = gs_ref[...] * scale
+
+    agg_mine = dot(a_s[at(core * chips + chip, height), :], hid_s[...], ((1,), (0,))).astype(BF16)
+    emb_ref[...] = dot(agg_mine, w_s[1, :, my_cols], ((1,), (0,))).astype(BF16)
+
+
+def whole_body(features, edge_tiles, sources, counts, w_first, w_second, cotangent):
+    _, slots, block, _ = edge_tiles.shape
+    height, width = features.shape
+    rows, reps = lax.axis_size("row"), lax.axis_size("rep")
+    chips = rows // CORES
+    nodes = height * rows
+    share = nodes // reps
+    wide = width * reps
+    vmem = pl.BlockSpec(memory_space=pltpu.VMEM)
+    smem = pl.BlockSpec(memory_space=pltpu.SMEM)
+    hbm = pl.BlockSpec(memory_space=pltpu.HBM)
+    shape = jax.ShapeDtypeStruct
+    limit = pltpu.CompilerParams(vmem_limit_bytes=24 * 2**20)
+
+    in_hbm = [
+        pltpu.with_memory_space_constraint(v, pltpu.HBM)
+        for v in (features, cotangent, edge_tiles, w_first, w_second)
+    ]
+    for_chips, for_reps, my_row = pl.pallas_call(
+        functools.partial(pack_kernel, chips, share // block),
+        out_shape=(
+            shape((2, height, share), BF16),
+            shape((1 + wide // share, height, share), BF16),
+            shape((height, nodes), BF16),
+        ),
+        in_specs=[smem, smem] + [hbm] * 5,
+        out_specs=(vmem,) * 3,
+        scratch_shapes=[pltpu.SemaphoreType.DMA((slots + 2 + wide // share,))],
+        compiler_params=limit,
+        name="pack",
+    )(sources, counts, *in_hbm)
+
+    def swap(value, axis, size, d):
+        return lax.ppermute(value, axis, [(i, i ^ d) for i in range(size)])
+
+    def spread(value):
+        far_first = range(reps - 1, 0, -1)
+        got = {d: swap(value, "rep", reps, d) for d in far_first}
+        values = [value] + [got[d] for d in range(1, reps)]
+        return values + [swap(v, "row", rows, 1) for v in values]
+
+    near, *far = [swap(for_chips, "row", rows, CORES * d) for d in range(1, chips)]
+    joined = pl.pallas_call(
+        join_kernel,
+        out_shape=shape((2 * (chips - 2), height, share), BF16),
+        in_specs=[vmem] * (chips - 2),
+        out_specs=vmem,
+        compiler_params=limit,
+        name="join",
+    )(*far)
+    pieces = spread(for_reps) + spread(near) + spread(joined)
+    own_rows = [my_row, swap(my_row, "row", rows, 1)]
+
+    return tuple(
+        pl.pallas_call(
+            functools.partial(layers_kernel, chips, reps, 1.0 / math.sqrt(nodes)),
+            out_shape=(
+                shape((height, width), BF16),
+                shape((width, wide), F32),
+                shape((width, wide), F32),
+            ),
+            in_specs=[vmem] * (3 * CORES * reps + CORES),
+            out_specs=(vmem, vmem, vmem),
+            scratch_shapes=[
+                pltpu.VMEM((nodes, nodes), BF16),
+                pltpu.VMEM((nodes, wide), BF16),
+                pltpu.VMEM((nodes, wide), BF16),
+                pltpu.VMEM((2, wide, wide), BF16),
+                pltpu.VMEM((nodes, wide), BF16),
+                pltpu.VMEM((nodes, wide), BF16),
+                pltpu.VMEM((nodes, wide), F32),
+                pltpu.VMEM((nodes, wide), BF16),
+            ],
+            compiler_params=limit,
+            name="layers",
+        )(*pieces, *own_rows)
+    )
+
+
+def fits_whole(features, edge_tiles, rows, reps):
+    nodes, wide = features.shape
+    block = edge_tiles.shape[2]
+    powers = all(n & (n - 1) == 0 for n in (rows, reps))
+    held = 2 * (nodes * nodes + 2 * nodes * wide + 2 * wide * wide)
+    width, share = wide // reps, nodes // reps
+    return (
+        held <= REPLICATED_BYTES
+        and powers
+        and rows % CORES == 0
+        and nodes // rows == block == width
+        and share % block == 0
+        and share == 2 * width
+        and wide % share == 0
+        and rows // CORES > 2
+    )
+
+
 def solution(mesh):
     placed = (
         P("row", "rep"),
@@ -87,10 +322,17 @@
         P("rep", None),
         P("row", "rep"),
     )
-    return jax.shard_map(
-        body,
-        mesh=mesh,
-        in_specs=placed,
-        out_specs=(P("row", "rep"), P("rep", None), P("rep", None)),
-        check_vma=False,
-    )
+
+    rows, reps = mesh.shape["row"], mesh.shape["rep"]
+    outs = (P("row", "rep"), P("rep", None), P("rep", None))
+
+    def run(features, edge_tiles, *rest):
+        whole = fits_whole(features, edge_tiles, rows, reps)
+
+        def body(*args):
+            return (whole_body if whole else split_body)(*args)
+
+        step = jax.shard_map(body, mesh=mesh, in_specs=placed, out_specs=outs, check_vma=False)
+        return step(features, edge_tiles, *rest)
+
+    return run

time: 194 us -> 57.5 us (0.30)
  waiting for transfers between devices: 117 us -> 23.3 us
  blocking collectives: 47.1 us -> 0 us
  starting transfers between devices: 0.16 us -> 22 us
  between operations: 14.5 us -> 1.36 us
  Pallas kernels: 0 us -> 10.6 us
  local copies, waits for them, and re-layouts: 6.2 us -> 0.01 us
  matrix products: 4.55 us -> 0 us
  other arithmetic: 4.11 us -> 0 us
    reduce_scatter x3 -> x0, waiting for transfers between devices: 59.3 us -> none  [the longest x1 33.7 us: body(): lax.psum_scatter(summed[:wanted].reshape(count, width), 'row', scatter_di...]
    psum x1 -> x0, waiting for transfers between devices: 58 us -> none  [body(): grad_second, grad_first = lax.psum((second_part, first_part), 'row')]
    all_gather x4 -> x0, blocking collectives: 47.1 us -> none  [the longest x2 30.3 us: gather_blocks(): whole = lax.all_gather(packed, 'row', axis=0, tiled=True)]
    ppermute x0 -> x25, waiting for transfers between devices: none -> 23.3 us  [swap(): return lax.ppermute(value, axis, [(i, i ^ d) for i in range(size)])]
    ppermute x0 -> x25, starting transfers between devices: none -> 22 us  [swap(): return lax.ppermute(value, axis, [(i, i ^ d) for i in range(size)])]
    pallas_call x0 -> x3, Pallas kernels: none -> 10.6 us  [the longest x1 9.04 us: whole_body(): pl.pallas_call(functools.partial(layers_kernel, chips, reps, 1.0 / math.s...]
    dot_general x7 -> x0, matrix products: 4.55 us -> none  [the longest x2 1.75 us: mix_columns(): partial_terms = jnp.dot(agg, weight, preferred_element_type=jnp.float32)]
    unnamed x14 -> x2, local copies, waits for them, and re-layouts: 4.09 us -> 0.01 us
  transfers between devices with their start and end apart: 4 -> 25, of which waited for: 4 -> 8; matrix products, arithmetic and copies ran while one was open for 3% -> 0% of each run, Pallas kernels for 0% -> 0%
where the time goes in v1:
time: 57.5 us; the launch traced here: 57.3 us
  waiting for transfers between devices  23.3 us (41%)
  starting transfers between devices  22 us (38%)
  Pallas kernels  10.6 us (18%)
  between operations  1.36 us (2%)
    ppermute x25, waiting for transfers between devices, swap(): return lax.ppermute(value, axis, [(i, i ^ d) for i in range(size)])  23.3 us
    ppermute x25, starting transfers between devices, swap(): return lax.ppermute(value, axis, [(i, i ^ d) for i in range(size)])  22 us
    pallas_call x1, Pallas kernels, whole_body(): pl.pallas_call(functools.partial(layers_kernel, chips, reps, 1.0 / math.s...  9.04 us
    pallas_call x1, Pallas kernels, whole_body(): pl.pallas_call(functools.partial(pack_kernel, chips, share // block), out...  1.57 us
  transfers between devices with their start and end apart: 25, of which 8 were waited for; matrix products, arithmetic and copies ran while one was open for 0% of the time, Pallas kernels for 0%

profile of v1, /device:TPU:0, one launch (start us, length us, event | category | flops | bytes accessed | tf_op | source)
XLA Modules:
  0.0 57.3 jit_solution(12658579061786326364)
XLA Ops:
  1.3 1.6 %pack.1 = (bf16[2,128,256]{2,1,0:T(8,128)(2,1)S(1)}, bf16[3,128,256]{2,1,0:T(8,128)(2,1)S(1)}, bf16[128,1024]{1,0:T(8,128)(2,1)S(1)}) custom-call(s32[1,8]{1,0:T(1,128)S(1)} %copy-done, s32[1]{0:T(128)S(6)} %copy.10.counts_ref, bf16[128,128]{1,0:T(8,128)(2,1)} %feat_ref.1, bf16[128,128]{1,0:T(8,128)(2,1)} %cot_ref.1, bf16[1,8,128,128]{3,2,1,0:T(8,128)(2,1)} %tiles_ref.1, ...), custom_call_target="tpu_custom_call" | custom-call | tf_op jit(solution)/shard_map/pack/pallas_call | solution.py:236
  2.9 5.2 %collective-permute-start.16 = (bf16[2,128,256]{2,1,0:T(8,128)(2,1)S(1)}, bf16[2,128,256]{2,1,0:T(8,128)(2,1)S(1)}, u32[]{:S(2)}, u32[]{:S(2)}) collective-permute-start(bf16[2,128,256]{2,1,0:T(8,128)(2,1)S(1)} %get-tuple-element.7), channel_id=1, source_target_pairs={{0,24},{4,28},{8,16},{12,20},{16,8},{20,12},{24,0},{28,4},{1,25},{... | collective-permute-start | bytes 393224 | tf_op jit(solution)/shard_map/ppermute | solution.py:251
  8.1 2.4 %collective-permute-start.2 = (bf16[3,128,256]{2,1,0:T(8,128)(2,1)S(1)}, bf16[3,128,256]{2,1,0:T(8,128)(2,1)S(1)}, u32[]{:S(2)}, u32[]{:S(2)}) collective-permute-start(bf16[3,128,256]{2,1,0:T(8,128)(2,1)S(1)} %get-tuple-element.6.refs_0_), channel_id=1, source_target_pairs={{0,3},{1,2},{2,1},{3,0},{4,7},{5,6},{6,5},{7,4},{8,11},{9,10},{10,... | collective-permute-start | bytes 589832 | tf_op jit(solution)/shard_map/ppermute | solution.py:251
  10.6 0.7 %collective-permute-start.7 = (bf16[2,128,256]{2,1,0:T(8,128)(2,1)S(1)}, bf16[2,128,256]{2,1,0:T(8,128)(2,1)S(1)}, u32[]{:S(2)}, u32[]{:S(2)}) collective-permute-start(bf16[2,128,256]{2,1,0:T(8,128)(2,1)S(1)} %get-tuple-element.7), channel_id=1, source_target_pairs={{0,8},{4,12},{8,0},{12,4},{16,24},{20,28},{24,16},{28,20},{1,9},{5... | collective-permute-start | bytes 393224 | tf_op jit(solution)/shard_map/ppermute | solution.py:251
  11.3 1.3 %collective-permute-done.16.refs_1_ = bf16[2,128,256]{2,1,0:T(8,128)(2,1)S(1)} collective-permute-done((bf16[2,128,256]{2,1,0:T(8,128)(2,1)S(1)}, bf16[2,128,256]{2,1,0:T(8,128)(2,1)S(1)}, u32[]{:S(2)}, u32[]{:S(2)}) %collective-permute-start.16) | collective-permute-done | bytes 131104 | tf_op jit(solution)/shard_map/ppermute | solution.py:251
  12.6 1.6 %collective-permute-start.1 = (bf16[3,128,256]{2,1,0:T(8,128)(2,1)S(1)}, bf16[3,128,256]{2,1,0:T(8,128)(2,1)S(1)}, u32[]{:S(2)}, u32[]{:S(2)}) collective-permute-start(bf16[3,128,256]{2,1,0:T(8,128)(2,1)S(1)} %get-tuple-element.6.refs_0_), channel_id=1, source_target_pairs={{0,2},{1,3},{2,0},{3,1},{4,6},{5,7},{6,4},{7,5},{8,10},{9,11},{10,... | collective-permute-start | bytes 589832 | tf_op jit(solution)/shard_map/ppermute | solution.py:251
  14.2 5.0 %collective-permute-done.15.refs_0_ = bf16[2,128,256]{2,1,0:T(8,128)(2,1)S(1)} collective-permute-done((bf16[2,128,256]{2,1,0:T(8,128)(2,1)S(1)}, bf16[2,128,256]{2,1,0:T(8,128)(2,1)S(1)}, u32[]{:S(2)}, u32[]{:S(2)}) %collective-permute-start.15) | collective-permute-done | bytes 131104 | tf_op jit(solution)/shard_map/ppermute | solution.py:251
  19.2 1.5 %collective-permute-start = (bf16[3,128,256]{2,1,0:T(8,128)(2,1)S(1)}, bf16[3,128,256]{2,1,0:T(8,128)(2,1)S(1)}, u32[]{:S(2)}, u32[]{:S(2)}) collective-permute-start(bf16[3,128,256]{2,1,0:T(8,128)(2,1)S(1)} %get-tuple-element.6.refs_0_), channel_id=1, source_target_pairs={{0,1},{1,0},{2,3},{3,2},{4,5},{5,4},{6,7},{7,6},{8,9},{9,8},{10,11... | collective-permute-start | bytes 589832 | tf_op jit(solution)/shard_map/ppermute | solution.py:251
  20.7 1.6 %collective-permute-start.10 = (bf16[2,128,256]{2,1,0:T(8,128)(2,1)S(1)}, bf16[2,128,256]{2,1,0:T(8,128)(2,1)S(1)}, u32[]{:S(2)}, u32[]{:S(2)}) collective-permute-start(bf16[2,128,256]{2,1,0:T(8,128)(2,1)S(1)} %collective-permute-done.7.refs_8_), channel_id=1, source_target_pairs={{0,3},{1,2},{2,1},{3,0},{4,7},{5,6},{6,5},{7,4},{8,11},{9,10},{10,... | collective-permute-start | bytes 393224 | tf_op jit(solution)/shard_map/ppermute | solution.py:251
  22.2 0.5 collective-permute-start.9
  22.7 2.9 %collective-permute-done.refs_1_ = bf16[3,128,256]{2,1,0:T(8,128)(2,1)S(1)} collective-permute-done((bf16[3,128,256]{2,1,0:T(8,128)(2,1)S(1)}, bf16[3,128,256]{2,1,0:T(8,128)(2,1)S(1)}, u32[]{:S(2)}, u32[]{:S(2)}) %collective-permute-start) | collective-permute-done | bytes 196640 | tf_op jit(solution)/shard_map/ppermute | solution.py:251
  25.7 2.4 %collective-permute-start.8 = (bf16[2,128,256]{2,1,0:T(8,128)(2,1)S(1)}, bf16[2,128,256]{2,1,0:T(8,128)(2,1)S(1)}, u32[]{:S(2)}, u32[]{:S(2)}) collective-permute-start(bf16[2,128,256]{2,1,0:T(8,128)(2,1)S(1)} %collective-permute-done.7.refs_8_), channel_id=1, source_target_pairs={{0,1},{1,0},{2,3},{3,2},{4,5},{5,4},{6,7},{7,6},{8,9},{9,8},{10,11... | collective-permute-start | bytes 393224 | tf_op jit(solution)/shard_map/ppermute | solution.py:251
  28.1 2.3 %collective-permute-done.10.refs_11_ = bf16[2,128,256]{2,1,0:T(8,128)(2,1)S(1)} collective-permute-done((bf16[2,128,256]{2,1,0:T(8,128)(2,1)S(1)}, bf16[2,128,256]{2,1,0:T(8,128)(2,1)S(1)}, u32[]{:S(2)}, u32[]{:S(2)}) %collective-permute-start.10) | collective-permute-done | bytes 131104 | tf_op jit(solution)/shard_map/ppermute | solution.py:251
  30.5 0.5 collective-permute-start.13
  31.0 1.5 %collective-permute-start.19 = (bf16[4,128,256]{2,1,0:T(8,128)(2,1)S(1)}, bf16[4,128,256]{2,1,0:T(8,128)(2,1)S(1)}, u32[]{:S(2)}, u32[]{:S(2)}) collective-permute-start(bf16[4,128,256]{2,1,0:T(8,128)(2,1)S(1)} %join.1.refs_16_), channel_id=1, source_target_pairs={{0,3},{1,2},{2,1},{3,0},{4,7},{5,6},{6,5},{7,4},{8,11},{9,10},{10,... | collective-permute-start | bytes 786440 | tf_op jit(solution)/shard_map/ppermute | solution.py:251
  32.5 1.5 %collective-permute-start.18 = (bf16[4,128,256]{2,1,0:T(8,128)(2,1)S(1)}, bf16[4,128,256]{2,1,0:T(8,128)(2,1)S(1)}, u32[]{:S(2)}, u32[]{:S(2)}) collective-permute-start(bf16[4,128,256]{2,1,0:T(8,128)(2,1)S(1)} %join.1.refs_16_), channel_id=1, source_target_pairs={{0,2},{1,3},{2,0},{3,1},{4,6},{5,7},{6,4},{7,5},{8,10},{9,11},{10,... | collective-permute-start | bytes 786440 | tf_op jit(solution)/shard_map/ppermute | solution.py:251
  34.0 0.9 %collective-permute-start.17 = (bf16[4,128,256]{2,1,0:T(8,128)(2,1)S(1)}, bf16[4,128,256]{2,1,0:T(8,128)(2,1)S(1)}, u32[]{:S(2)}, u32[]{:S(2)}) collective-permute-start(bf16[4,128,256]{2,1,0:T(8,128)(2,1)S(1)} %join.1.refs_16_), channel_id=1, source_target_pairs={{0,1},{1,0},{2,3},{3,2},{4,5},{5,4},{6,7},{7,6},{8,9},{9,8},{10,11... | collective-permute-start | bytes 786440 | tf_op jit(solution)/shard_map/ppermute | solution.py:251
  34.9 0.5 collective-permute-start.6
  35.5 5.7 %collective-permute-done.19.refs_19_ = bf16[4,128,256]{2,1,0:T(8,128)(2,1)S(1)} collective-permute-done((bf16[4,128,256]{2,1,0:T(8,128)(2,1)S(1)}, bf16[4,128,256]{2,1,0:T(8,128)(2,1)S(1)}, u32[]{:S(2)}, u32[]{:S(2)}) %collective-permute-start.19) | collective-permute-done | bytes 262176 | tf_op jit(solution)/shard_map/ppermute | solution.py:251
  41.2 4.6 %collective-permute-done.18.refs_18_ = bf16[4,128,256]{2,1,0:T(8,128)(2,1)S(1)} collective-permute-done((bf16[4,128,256]{2,1,0:T(8,128)(2,1)S(1)}, bf16[4,128,256]{2,1,0:T(8,128)(2,1)S(1)}, u32[]{:S(2)}, u32[]{:S(2)}) %collective-permute-start.18) | collective-permute-done | bytes 262176 | tf_op jit(solution)/shard_map/ppermute | solution.py:251
  45.9 0.4 collective-permute-start.21
  46.4 0.4 collective-permute-start.4
  46.8 1.2 %collective-permute-done.5.refs_6_ = bf16[3,128,256]{2,1,0:T(8,128)(2,1)S(1)} collective-permute-done((bf16[3,128,256]{2,1,0:T(8,128)(2,1)S(1)}, bf16[3,128,256]{2,1,0:T(8,128)(2,1)S(1)}, u32[]{:S(2)}, u32[]{:S(2)}) %collective-permute-start.5) | collective-permute-done | bytes 196640 | tf_op jit(solution)/shard_map/ppermute | solution.py:251
  48.3 9.0 %layers.1 = (bf16[128,128]{1,0:T(8,128)(2,1)}, f32[128,512]{1,0:T(8,128)}, f32[128,512]{1,0:T(8,128)}) custom-call(bf16[3,128,256]{2,1,0:T(8,128)(2,1)S(1)} %get-tuple-element.6.refs_0_, bf16[3,128,256]{2,1,0:T(8,128)(2,1)S(1)} %collective-permute-done.refs_1_, bf16[3,128,256]{2,1,0:T(8,128)(2,1)S(1)} %collective-permute-done.1.refs_2_, ...), custom_call_target="tpu_custom_call" | custom-call | tf_op jit(solution)/shard_map/layers/pallas_call | solution.py:272
  (31 shorter events, 0.5 us)
Async XLA Ops:
  2.9 9.7 %collective-permute-start.16 = (bf16[2,128,256]{2,1,0:T(8,128)(2,1)S(1)}, bf16[2,128,256]{2,1,0:T(8,128)(2,1)S(1)}, u32[]{:S(2)}, u32[]{:S(2)}) collective-permute-start(bf16[2,128,256]{2,1,0:T(8,128)(2,1)S(1)} %get-tuple-element.7), channel_id=1, source_target_pairs={{0,24},{4,28},{8,16},{12,20},{16,8},{20,12},{24,0},{28,4},{1,25},{... | collective-permute-start | bytes 393224 | tf_op jit(solution)/shard_map/ppermute | solution.py:251
  8.1 11.1 %collective-permute-start.15 = (bf16[2,128,256]{2,1,0:T(8,128)(2,1)S(1)}, bf16[2,128,256]{2,1,0:T(8,128)(2,1)S(1)}, u32[]{:S(2)}, u32[]{:S(2)}) collective-permute-start(bf16[2,128,256]{2,1,0:T(8,128)(2,1)S(1)} %get-tuple-element.7), channel_id=1, source_target_pairs={{0,16},{4,20},{8,24},{12,28},{16,0},{20,4},{24,8},{28,12},{1,17},{... | collective-permute-start | bytes 393224 | tf_op jit(solution)/shard_map/ppermute | solution.py:251
  8.1 12.6 %collective-permute-start.3 = (bf16[3,128,256]{2,1,0:T(8,128)(2,1)S(1)}, bf16[3,128,256]{2,1,0:T(8,128)(2,1)S(1)}, u32[]{:S(2)}, u32[]{:S(2)}) collective-permute-start(bf16[3,128,256]{2,1,0:T(8,128)(2,1)S(1)} %get-tuple-element.6.refs_0_), channel_id=1, source_target_pairs={{0,4},{4,0},{8,12},{12,8},{16,20},{20,16},{24,28},{28,24},{1,5},{5... | collective-permute-start | bytes 589832 | tf_op jit(solution)/shard_map/ppermute | solution.py:251
  8.1 14.1 %collective-permute-start.2 = (bf16[3,128,256]{2,1,0:T(8,128)(2,1)S(1)}, bf16[3,128,256]{2,1,0:T(8,128)(2,1)S(1)}, u32[]{:S(2)}, u32[]{:S(2)}) collective-permute-start(bf16[3,128,256]{2,1,0:T(8,128)(2,1)S(1)} %get-tuple-element.6.refs_0_), channel_id=1, source_target_pairs={{0,3},{1,2},{2,1},{3,0},{4,7},{5,6},{6,5},{7,4},{8,11},{9,10},{10,... | collective-permute-start | bytes 589832 | tf_op jit(solution)/shard_map/ppermute | solution.py:251
  10.6 10.1 %collective-permute-start.7 = (bf16[2,128,256]{2,1,0:T(8,128)(2,1)S(1)}, bf16[2,128,256]{2,1,0:T(8,128)(2,1)S(1)}, u32[]{:S(2)}, u32[]{:S(2)}) collective-permute-start(bf16[2,128,256]{2,1,0:T(8,128)(2,1)S(1)} %get-tuple-element.7), channel_id=1, source_target_pairs={{0,8},{4,12},{8,0},{12,4},{16,24},{20,28},{24,16},{28,20},{1,9},{5... | collective-permute-start | bytes 393224 | tf_op jit(solution)/shard_map/ppermute | solution.py:251
  12.6 10.2 %collective-permute-start.1 = (bf16[3,128,256]{2,1,0:T(8,128)(2,1)S(1)}, bf16[3,128,256]{2,1,0:T(8,128)(2,1)S(1)}, u32[]{:S(2)}, u32[]{:S(2)}) collective-permute-start(bf16[3,128,256]{2,1,0:T(8,128)(2,1)S(1)} %get-tuple-element.6.refs_0_), channel_id=1, source_target_pairs={{0,2},{1,3},{2,0},{3,1},{4,6},{5,7},{6,4},{7,5},{8,10},{9,11},{10,... | collective-permute-start | bytes 589832 | tf_op jit(solution)/shard_map/ppermute | solution.py:251
  19.2 6.5 %collective-permute-start = (bf16[3,128,256]{2,1,0:T(8,128)(2,1)S(1)}, bf16[3,128,256]{2,1,0:T(8,128)(2,1)S(1)}, u32[]{:S(2)}, u32[]{:S(2)}) collective-permute-start(bf16[3,128,256]{2,1,0:T(8,128)(2,1)S(1)} %get-tuple-element.6.refs_0_), channel_id=1, source_target_pairs={{0,1},{1,0},{2,3},{3,2},{4,5},{5,4},{6,7},{7,6},{8,9},{9,8},{10,11... | collective-permute-start | bytes 589832 | tf_op jit(solution)/shard_map/ppermute | solution.py:251
  20.7 11.9 %collective-permute-start.24 = (bf16[128,1024]{1,0:T(8,128)(2,1)S(1)}, bf16[128,1024]{1,0:T(8,128)(2,1)S(1)}, u32[]{:S(2)}, u32[]{:S(2)}) collective-permute-start(bf16[128,1024]{1,0:T(8,128)(2,1)S(1)} %get-tuple-element.8.refs_24_), channel_id=1, source_target_pairs={{0,4},{4,0},{8,12},{12,8},{16,20},{20,16},{24,28},{28,24},{1,5},{5... | collective-permute-start | bytes 786440 | tf_op jit(solution)/shard_map/ppermute | solution.py:251
  20.7 9.8 %collective-permute-start.10 = (bf16[2,128,256]{2,1,0:T(8,128)(2,1)S(1)}, bf16[2,128,256]{2,1,0:T(8,128)(2,1)S(1)}, u32[]{:S(2)}, u32[]{:S(2)}) collective-permute-start(bf16[2,128,256]{2,1,0:T(8,128)(2,1)S(1)} %collective-permute-done.7.refs_8_), channel_id=1, source_target_pairs={{0,3},{1,2},{2,1},{3,0},{4,7},{5,6},{6,5},{7,4},{8,11},{9,10},{10,... | collective-permute-start | bytes 393224 | tf_op jit(solution)/shard_map/ppermute | solution.py:251
  22.2 8.2 %collective-permute-start.9 = (bf16[2,128,256]{2,1,0:T(8,128)(2,1)S(1)}, bf16[2,128,256]{2,1,0:T(8,128)(2,1)S(1)}, u32[]{:S(2)}, u32[]{:S(2)}) collective-permute-start(bf16[2,128,256]{2,1,0:T(8,128)(2,1)S(1)} %collective-permute-done.7.refs_8_), channel_id=1, source_target_pairs={{0,2},{1,3},{2,0},{3,1},{4,6},{5,7},{6,4},{7,5},{8,10},{9,11},{10,... | collective-permute-start | bytes 393224 | tf_op jit(solution)/shard_map/ppermute | solution.py:251
  22.7 8.2 %collective-permute-start.11 = (bf16[2,128,256]{2,1,0:T(8,128)(2,1)S(1)}, bf16[2,128,256]{2,1,0:T(8,128)(2,1)S(1)}, u32[]{:S(2)}, u32[]{:S(2)}) collective-permute-start(bf16[2,128,256]{2,1,0:T(8,128)(2,1)S(1)} %collective-permute-done.7.refs_8_), channel_id=1, source_target_pairs={{0,4},{4,0},{8,12},{12,8},{16,20},{20,16},{24,28},{28,24},{1,5},{5... | collective-permute-start | bytes 393224 | tf_op jit(solution)/shard_map/ppermute | solution.py:251
  25.7 6.9 %collective-permute-start.8 = (bf16[2,128,256]{2,1,0:T(8,128)(2,1)S(1)}, bf16[2,128,256]{2,1,0:T(8,128)(2,1)S(1)}, u32[]{:S(2)}, u32[]{:S(2)}) collective-permute-start(bf16[2,128,256]{2,1,0:T(8,128)(2,1)S(1)} %collective-permute-done.7.refs_8_), channel_id=1, source_target_pairs={{0,1},{1,0},{2,3},{3,2},{4,5},{5,4},{6,7},{7,6},{8,9},{9,8},{10,11... | collective-permute-start | bytes 393224 | tf_op jit(solution)/shard_map/ppermute | solution.py:251
  30.4 3.6 %collective-permute-start.14 = (bf16[2,128,256]{2,1,0:T(8,128)(2,1)S(1)}, bf16[2,128,256]{2,1,0:T(8,128)(2,1)S(1)}, u32[]{:S(2)}, u32[]{:S(2)}) collective-permute-start(bf16[2,128,256]{2,1,0:T(8,128)(2,1)S(1)} %collective-permute-done.10.refs_11_), channel_id=1, source_target_pairs={{0,4},{4,0},{8,12},{12,8},{16,20},{20,16},{24,28},{28,24},{1,5},{5... | collective-permute-start | bytes 393224 | tf_op jit(solution)/shard_map/ppermute | solution.py:251
  30.5 4.5 %collective-permute-start.13 = (bf16[2,128,256]{2,1,0:T(8,128)(2,1)S(1)}, bf16[2,128,256]{2,1,0:T(8,128)(2,1)S(1)}, u32[]{:S(2)}, u32[]{:S(2)}) collective-permute-start(bf16[2,128,256]{2,1,0:T(8,128)(2,1)S(1)} %collective-permute-done.9.refs_10_), channel_id=1, source_target_pairs={{0,4},{4,0},{8,12},{12,8},{16,20},{20,16},{24,28},{28,24},{1,5},{5... | collective-permute-start | bytes 393224 | tf_op jit(solution)/shard_map/ppermute | solution.py:251
  31.0 10.2 %collective-permute-start.19 = (bf16[4,128,256]{2,1,0:T(8,128)(2,1)S(1)}, bf16[4,128,256]{2,1,0:T(8,128)(2,1)S(1)}, u32[]{:S(2)}, u32[]{:S(2)}) collective-permute-start(bf16[4,128,256]{2,1,0:T(8,128)(2,1)S(1)} %join.1.refs_16_), channel_id=1, source_target_pairs={{0,3},{1,2},{2,1},{3,0},{4,7},{5,6},{6,5},{7,4},{8,11},{9,10},{10,... | collective-permute-start | bytes 786440 | tf_op jit(solution)/shard_map/ppermute | solution.py:251
  32.5 2.4 %collective-permute-start.12 = (bf16[2,128,256]{2,1,0:T(8,128)(2,1)S(1)}, bf16[2,128,256]{2,1,0:T(8,128)(2,1)S(1)}, u32[]{:S(2)}, u32[]{:S(2)}) collective-permute-start(bf16[2,128,256]{2,1,0:T(8,128)(2,1)S(1)} %collective-permute-done.8.refs_9_), channel_id=1, source_target_pairs={{0,4},{4,0},{8,12},{12,8},{16,20},{20,16},{24,28},{28,24},{1,5},{5... | collective-permute-start | bytes 393224 | tf_op jit(solution)/shard_map/ppermute | solution.py:251
  32.5 13.3 %collective-permute-start.18 = (bf16[4,128,256]{2,1,0:T(8,128)(2,1)S(1)}, bf16[4,128,256]{2,1,0:T(8,128)(2,1)S(1)}, u32[]{:S(2)}, u32[]{:S(2)}) collective-permute-start(bf16[4,128,256]{2,1,0:T(8,128)(2,1)S(1)} %join.1.refs_16_), channel_id=1, source_target_pairs={{0,2},{1,3},{2,0},{3,1},{4,6},{5,7},{6,4},{7,5},{8,10},{9,11},{10,... | collective-permute-start | bytes 786440 | tf_op jit(solution)/shard_map/ppermute | solution.py:251
  34.0 11.8 %collective-permute-start.17 = (bf16[4,128,256]{2,1,0:T(8,128)(2,1)S(1)}, bf16[4,128,256]{2,1,0:T(8,128)(2,1)S(1)}, u32[]{:S(2)}, u32[]{:S(2)}) collective-permute-start(bf16[4,128,256]{2,1,0:T(8,128)(2,1)S(1)} %join.1.refs_16_), channel_id=1, source_target_pairs={{0,1},{1,0},{2,3},{3,2},{4,5},{5,4},{6,7},{7,6},{8,9},{9,8},{10,11... | collective-permute-start | bytes 786440 | tf_op jit(solution)/shard_map/ppermute | solution.py:251
  34.9 11.4 %collective-permute-start.20 = (bf16[4,128,256]{2,1,0:T(8,128)(2,1)S(1)}, bf16[4,128,256]{2,1,0:T(8,128)(2,1)S(1)}, u32[]{:S(2)}, u32[]{:S(2)}) collective-permute-start(bf16[4,128,256]{2,1,0:T(8,128)(2,1)S(1)} %join.1.refs_16_), channel_id=1, source_target_pairs={{0,4},{4,0},{8,12},{12,8},{16,20},{20,16},{24,28},{28,24},{1,5},{5... | collective-permute-start | bytes 786440 | tf_op jit(solution)/shard_map/ppermute | solution.py:251
  34.9 11.4 %collective-permute-start.6 = (bf16[3,128,256]{2,1,0:T(8,128)(2,1)S(1)}, bf16[3,128,256]{2,1,0:T(8,128)(2,1)S(1)}, u32[]{:S(2)}, u32[]{:S(2)}) collective-permute-start(bf16[3,128,256]{2,1,0:T(8,128)(2,1)S(1)} %collective-permute-done.2.refs_3_), channel_id=1, source_target_pairs={{0,4},{4,0},{8,12},{12,8},{16,20},{20,16},{24,28},{28,24},{1,5},{5... | collective-permute-start | bytes 589832 | tf_op jit(solution)/shard_map/ppermute | solution.py:251
  41.2 7.1 %collective-permute-start.23 = (bf16[4,128,256]{2,1,0:T(8,128)(2,1)S(1)}, bf16[4,128,256]{2,1,0:T(8,128)(2,1)S(1)}, u32[]{:S(2)}, u32[]{:S(2)}) collective-permute-start(bf16[4,128,256]{2,1,0:T(8,128)(2,1)S(1)} %collective-permute-done.19.refs_19_), channel_id=1, source_target_pairs={{0,4},{4,0},{8,12},{12,8},{16,20},{20,16},{24,28},{28,24},{1,5},{5... | collective-permute-start | bytes 786440 | tf_op jit(solution)/shard_map/ppermute | solution.py:251
  45.8 2.5 %collective-permute-start.22 = (bf16[4,128,256]{2,1,0:T(8,128)(2,1)S(1)}, bf16[4,128,256]{2,1,0:T(8,128)(2,1)S(1)}, u32[]{:S(2)}, u32[]{:S(2)}) collective-permute-start(bf16[4,128,256]{2,1,0:T(8,128)(2,1)S(1)} %collective-permute-done.18.refs_18_), channel_id=1, source_target_pairs={{0,4},{4,0},{8,12},{12,8},{16,20},{20,16},{24,28},{28,24},{1,5},{5... | collective-permute-start | bytes 786440 | tf_op jit(solution)/shard_map/ppermute | solution.py:251
  45.9 2.4 %collective-permute-start.21 = (bf16[4,128,256]{2,1,0:T(8,128)(2,1)S(1)}, bf16[4,128,256]{2,1,0:T(8,128)(2,1)S(1)}, u32[]{:S(2)}, u32[]{:S(2)}) collective-permute-start(bf16[4,128,256]{2,1,0:T(8,128)(2,1)S(1)} %collective-permute-done.17.refs_17_), channel_id=1, source_target_pairs={{0,4},{4,0},{8,12},{12,8},{16,20},{20,16},{24,28},{28,24},{1,5},{5... | collective-permute-start | bytes 786440 | tf_op jit(solution)/shard_map/ppermute | solution.py:251
  46.4 1.9 %collective-permute-start.4 = (bf16[3,128,256]{2,1,0:T(8,128)(2,1)S(1)}, bf16[3,128,256]{2,1,0:T(8,128)(2,1)S(1)}, u32[]{:S(2)}, u32[]{:S(2)}) collective-permute-start(bf16[3,128,256]{2,1,0:T(8,128)(2,1)S(1)} %collective-permute-done.refs_1_), channel_id=1, source_target_pairs={{0,4},{4,0},{8,12},{12,8},{16,20},{20,16},{24,28},{28,24},{1,5},{5... | collective-permute-start | bytes 589832 | tf_op jit(solution)/shard_map/ppermute | solution.py:251
  (2 other events, 2.3 us)

commit v2 on v0

--- a/solution.py
+++ b/solution.py
@@ -1,9 +1,17 @@
+import functools
 import math
 
 import jax
 import jax.numpy as jnp
 from jax import lax
+from jax.experimental import pallas as pl
+from jax.experimental.pallas import tpu as pltpu
 from jax.sharding import PartitionSpec as P
+
+BF16 = jnp.bfloat16
+F32 = jnp.float32
+CORES = 2
+REPLICATED_BYTES = 16 * 2**20
 
 
 def silu_slope(value):
@@ -20,7 +28,7 @@
 
 def aggregate(local, live_tiles, sources):
     height, width = local.shape
-    group_rows, slots, block, _ = live_tiles.shape
+    _, _, block, _ = live_tiles.shape
     blocks = gather_blocks(local, block)
     total = jnp.einsum(
         "bkij,bkjf->bif", live_tiles, blocks[sources], preferred_element_type=jnp.float32
@@ -29,7 +37,7 @@
 
 
 def spread_back(back_agg, live_tiles):
-    group_rows, slots, block, _ = live_tiles.shape
+    group_rows, _, block, _ = live_tiles.shape
     width = back_agg.shape[1]
     block_rows = back_agg.reshape(group_rows, block, width)
     return jnp.einsum("bkij,bif->bkjf", live_tiles, block_rows, preferred_element_type=jnp.float32)
@@ -44,7 +52,7 @@
     return lax.all_gather(local, "rep", axis=1, tiled=True)
 
 
-def body(features, edge_tiles, sources, counts, w_first, w_second, cotangent):
+def split_body(features, edge_tiles, sources, counts, w_first, w_second, cotangent):
     group_rows, slots, block, _ = edge_tiles.shape
     height, width = features.shape
     live = jnp.arange(slots, dtype=jnp.int32)[None, :] < counts[:, None]
@@ -77,6 +85,358 @@
     return (embeddings, grad_first, grad_second)
 
 
+def dot(a, b, contract):
+    return lax.dot_general(a, b, (contract, ((), ())), preferred_element_type=F32)
+
+
+def pack_kernel(
+    chips, parts, counts_ref, sources_hbm, feat_ref, cot_ref, tiles_ref, w1_ref, w2_ref, *outs
+):
+    for_chips, for_reps, for_next, sems, sources_ref, index_sem = outs
+    index_copy = pltpu.make_async_copy(sources_hbm, sources_ref, index_sem)
+    index_copy.start()
+    _, slots, block, _ = tiles_ref.shape
+    width = feat_ref.shape[1]
+    core = lax.rem(lax.axis_index("row"), CORES)
+    moves = [
+        (feat_ref, for_reps.at[0, :, pl.ds(0, width)]),
+        (cot_ref, for_reps.at[0, :, pl.ds(width, width)]),
+    ]
+    copies = [pltpu.make_async_copy(*move, sems.at[slots + n]) for n, move in enumerate(moves)]
+    for copy in copies:
+        copy.start()
+    step = for_reps.shape[2]
+
+    def weight_copy(ref, n):
+        lanes = pl.ds(n * step, step)
+        return pltpu.make_async_copy(ref.at[:, lanes], for_reps.at[1 + n], sems.at[slots + 2 + n])
+
+    for c, ref in enumerate((w1_ref, w2_ref)):
+        for n in range(2):
+            pl.when(core == c)(lambda ref=ref, n=n: weight_copy(ref, n).start())
+    for_next[1:] = jnp.zeros_like(for_next[1:])
+    index_copy.wait()
+
+    def tile_copy(k):
+        source = sources_ref[0, k]
+        position = lax.rem(source, CORES) * chips + lax.div(source, CORES)
+        columns = pl.ds(pl.multiple_of(lax.rem(position, parts) * block, block), block)
+        target = for_next.at[1 + lax.div(position, parts), :, columns]
+        return pltpu.make_async_copy(tiles_ref.at[0, k], target, sems.at[k])
+
+    for k in range(slots):
+        pl.when(k < counts_ref[0])(lambda k=k: tile_copy(k).start())
+    for copy in copies:
+        copy.wait()
+    for_chips[0] = for_reps[0]
+    for_next[0] = for_reps[0]
+    for k in range(slots):
+        pl.when(k < counts_ref[0])(lambda k=k: tile_copy(k).wait())
+    for_chips[1] = for_next[1 + lax.axis_index("rep")]
+    for c, ref in enumerate((w1_ref, w2_ref)):
+        for n in range(2):
+            pl.when(core == c)(lambda ref=ref, n=n: weight_copy(ref, n).wait())
+
+
+def at(index, size, start=0):
+    return pl.ds(pl.multiple_of(start + index * size, size), size)
+
+
+def place_features(out_ref, rows, rep, blocks):
+    reps = len(blocks)
+    width = blocks[0].shape[1] // 2
+    for d, block in enumerate(blocks):
+        out_ref[rows, at(rep ^ d, width)] = block[:, :width]
+        out_ref[rows, at(rep ^ d, width, width * reps)] = block[:, width:]
+
+
+def place_adjacency(out_ref, for_next):
+    share = for_next.shape[2]
+    count = for_next.shape[0] - 1
+    start = out_ref.shape[1] - count * share
+    for j in range(count):
+        out_ref[:, start + j * share : start + (j + 1) * share] = for_next[1 + j]
+
+
+def own_kernel(*refs):
+    *own, for_next, rows_ref, weight_ref, peers_ref = refs
+    rep = lax.axis_index("rep")
+    _, height, share = for_next.shape
+    everything = pl.ds(0, height)
+    place_features(rows_ref, everything, rep, [ref[0] for ref in own])
+    place_adjacency(rows_ref, for_next)
+    width = weight_ref.shape[0] // len(own)
+    for d, ref in enumerate(own):
+        for n in range(2):
+            weight_ref[at(rep ^ d, width), n * share : (n + 1) * share] = ref[1 + n]
+        if d:
+            peers_ref[d - 1] = ref[0]
+
+
+def next_kernel(from_next, peers, rows_ref):
+    rep = lax.axis_index("rep")
+    everything = pl.ds(0, from_next.shape[1])
+    blocks = [from_next[0]] + [peers[d] for d in range(peers.shape[0])]
+    place_features(rows_ref, everything, rep, blocks)
+    place_adjacency(rows_ref, from_next)
+
+
+def far_kernel(*refs):
+    *blocks, out_ref = refs
+    reps = len(blocks) // 2
+    rep = lax.axis_index("rep")
+    half = lax.rem(lax.div(lax.axis_index("row"), CORES), 2)
+    _, height, share = blocks[0].shape
+    for parity, chunk in ((half, blocks[:reps]), (1 - half, blocks[reps:])):
+        rows = at(parity, height)
+        place_features(out_ref, rows, rep, [ref[0] for ref in chunk])
+        for d, ref in enumerate(chunk):
+            out_ref[rows, at(rep ^ d, share, share * reps)] = ref[1]
+
+
+def place_of(b):
+    row = lax.axis_index("row")
+    core, chip = lax.rem(row, CORES), lax.div(row, CORES)
+    dh, dc = divmod(b, CORES)
+    return (core ^ dc) * 2 + (lax.div(chip, 2) ^ dh)
+
+
+def parts_of(bundle, wide, step):
+    return (
+        bundle[:, :wide],
+        bundle[:, wide : 2 * wide],
+        lambda b: bundle[:, at(place_of(b), step, 2 * wide)],
+    )
+
+
+def total_of(terms):
+    total = None
+    for term in terms:
+        total = term if total is None else total + term
+    return total
+
+
+def back_aggregates(cotangent, weight):
+    return dot(cotangent, weight, ((1,), (1,))).astype(BF16)
+
+
+def early_kernel(*refs):
+    own_rows, next_rows, weights, refs = refs[:2], refs[2:4], refs[4:6], refs[6:]
+    first_bundle, second_bundle, w_ref, back_ref, agg_ref, ba_s = refs
+    bundles = first_bundle, second_bundle
+    row = lax.axis_index("row")
+    core, half = lax.rem(row, CORES), lax.rem(lax.div(row, CORES), 2)
+    height = own_rows[0].shape[0]
+    wide = w_ref.shape[1]
+    for c in range(CORES):
+        bundles[c][at(half, height), :] = own_rows[c][...]
+        bundles[c][at(1 - half, height), :] = next_rows[c][...]
+        w_ref[core ^ c] = weights[c][...]
+    parts = [parts_of(bundle, wide, 2 * height) for bundle in bundles]
+    for k, (_, cotangent, _) in enumerate(parts):
+        ba_s[k] = back_aggregates(cotangent[...], w_ref[1])
+    for b in range(2 * CORES):
+        terms = (dot(a(b), ba_s[k], ((0,), (0,))) for k, (_, _, a) in enumerate(parts))
+        back_ref[b] = total_of(terms)
+    for b, (_, _, a) in enumerate(parts):
+        terms = (dot(a(k), feats, ((1,), (0,))) for k, (feats, _, _) in enumerate(parts))
+        agg_ref[b] = total_of(terms)
+
+
+def middle_kernel(*refs):
+    bundles, (w_ref, back_in, agg_in), (back_ref, agg_ref) = refs[:3], refs[3:6], refs[6:]
+    step = bundles[0].shape[0]
+    parts = [parts_of(bundle, w_ref.shape[1], step) for bundle in bundles]
+    feats, cotangent, a = parts[CORES]
+    back_agg = back_aggregates(cotangent, w_ref[1])
+    for b in range(2 * CORES):
+        back_ref[b] = back_in[b] + dot(a(b), back_agg, ((0,), (0,)))
+    for b in range(CORES):
+        agg_ref[b] = agg_in[b] + dot(parts[b][2](CORES), feats, ((1,), (0,)))
+    agg_ref[CORES] = total_of(dot(a(k), parts[k][0], ((1,), (0,))) for k in range(CORES + 1))
+
+
+def layers_kernel(reps, scale, *refs):
+    bundles, (w_ref, back_ref, early_agg_ref), refs = refs[:4], refs[4:7], refs[7:]
+    emb_ref, gf_ref, gs_ref, af_s, hid_s, slope_s = refs
+    row, rep = lax.axis_index("row"), lax.axis_index("rep")
+    chip = lax.div(row, CORES)
+    height, width = emb_ref.shape
+    wide = width * reps
+    step = 2 * height
+    count = len(bundles)
+    my_cols = at(rep, width)
+    parts = [parts_of(bundle, wide, step) for bundle in bundles]
+
+    last = count - 1
+    back_agg = back_aggregates(parts[last][1], w_ref[1])
+    for b in range(count):
+        a = parts[b][2]
+        if b < last:
+            total = early_agg_ref[b] + dot(a(last), parts[last][0], ((1,), (0,)))
+        else:
+            total = total_of(dot(a(k), parts[k][0], ((1,), (0,))) for k in range(count))
+        agg = total.astype(BF16)
+        af_s[b] = agg
+        pre = dot(agg, w_ref[0], ((1,), (0,)))
+        sig = jax.nn.sigmoid(pre)
+        hid_s[b] = (pre * sig).astype(BF16)
+        slope_s[b] = sig * (1.0 + pre * (1.0 - sig))
+
+    for b in range(count):
+        _, cotangent, a = parts[b]
+        back_hidden = back_ref[b] + dot(parts[last][2](b), back_agg, ((0,), (0,)))
+        back_pre = (back_hidden * slope_s[b]).astype(BF16)
+        agg = total_of(dot(a(k), hid_s[k, :, my_cols], ((1,), (0,))) for k in range(count))
+        gf = dot(af_s[b, :, my_cols], back_pre, ((0,), (0,)))
+        gs = dot(agg.astype(BF16), cotangent, ((0,), (0,)))
+        gf_ref[...] = gf if b == 0 else gf_ref[...] + gf
+        gs_ref[...] = gs if b == 0 else gs_ref[...] + gs
+    gf_ref[...] = gf_ref[...] * scale
+    gs_ref[...] = gs_ref[...] * scale
+
+    mine = at(lax.rem(chip, 2), height)
+    agg = total_of(
+        dot(bundles[0][mine, at(place_of(k), step, 2 * wide)], hid_s[k], ((1,), (0,)))
+        for k in range(count)
+    )
+    emb_ref[...] = dot(agg.astype(BF16), w_ref[1, :, my_cols], ((1,), (0,))).astype(BF16)
+
+
+def whole_body(features, edge_tiles, sources, counts, w_first, w_second, cotangent):
+    _, slots, block, _ = edge_tiles.shape
+    height, width = features.shape
+    rows, reps = lax.axis_size("row"), lax.axis_size("rep")
+    chips = rows // CORES
+    nodes = height * rows
+    share = nodes // reps
+    wide = width * reps
+    vmem = pl.BlockSpec(memory_space=pltpu.VMEM)
+    hbm = pl.BlockSpec(memory_space=pltpu.HBM)
+    shape = jax.ShapeDtypeStruct
+    step = 2 * height
+    rows_shape = shape((height, 2 * wide + nodes), BF16)
+    bundle_shape = shape((step, 2 * wide + nodes), BF16)
+    limit = pltpu.CompilerParams(vmem_limit_bytes=24 * 2**20)
+
+    in_hbm = [
+        pltpu.with_memory_space_constraint(v, pltpu.HBM)
+        for v in (sources, features, cotangent, edge_tiles, w_first, w_second)
+    ]
+    for_chips, for_reps, for_next = pl.pallas_call(
+        functools.partial(pack_kernel, chips, share // block),
+        out_shape=(
+            shape((2, height, share), BF16),
+            shape((3, height, share), BF16),
+            shape((1 + reps, height, share), BF16),
+        ),
+        in_specs=[pl.BlockSpec(memory_space=pltpu.SMEM)] + [hbm] * 6,
+        out_specs=(vmem,) * 3,
+        scratch_shapes=[
+            pltpu.SemaphoreType.DMA((slots + 4,)),
+            pltpu.SMEM(sources.shape, sources.dtype),
+            pltpu.SemaphoreType.DMA,
+        ],
+        compiler_params=limit,
+        name="pack",
+    )(counts, *in_hbm)
+
+    def swap(value, axis, size, d):
+        return lax.ppermute(value, axis, [(i, i ^ d) for i in range(size)])
+
+    def spread(value, name):
+        values = [value]
+        for d in range(1, reps):
+            via, hop = hop_of(name, d)
+            values.append(swap(values[via], "rep", reps, hop))
+        return values
+
+    def local(kernel, outs, *operands, scratch=()):
+        return pl.pallas_call(
+            kernel,
+            out_shape=outs,
+            in_specs=[vmem] * len(operands),
+            out_specs=(vmem,) * len(outs),
+            scratch_shapes=scratch,
+            compiler_params=limit,
+        )(*operands)
+
+    def pair(value):
+        return value, swap(value, "row", rows, 1)
+
+    third = swap(for_chips, "row", rows, CORES * 3)
+    second = swap(for_chips, "row", rows, CORES * 2)
+    from_next = swap(for_next, "row", rows, CORES)
+    own, third, second = spread(for_reps, "own"), spread(third, "third"), spread(second, "second")
+
+    outs = (rows_shape, shape((wide, wide), BF16), shape((reps - 1, height, share), BF16))
+    own_rows, weight, peers = local(own_kernel, outs, *own, for_next)
+    peers = swap(peers, "row", rows, CORES)
+    (next_rows,) = local(next_kernel, (rows_shape,), from_next, peers)
+    (far_bundle,) = local(far_kernel, (bundle_shape,), *second, *third)
+    outs = (
+        *(bundle_shape, bundle_shape),
+        shape((2, wide, wide), BF16),
+        shape((2 * CORES, step, wide), F32),
+        shape((CORES, step, wide), F32),
+    )
+    *near_bundles, weights, back, agg = local(
+        early_kernel,
+        outs,
+        *pair(own_rows),
+        *pair(next_rows),
+        *pair(weight),
+        scratch=[pltpu.VMEM((CORES, step, wide), BF16)],
+    )
+    far_pair = pair(far_bundle)
+    back, agg = local(
+        middle_kernel,
+        (shape((2 * CORES, step, wide), F32), shape((CORES + 1, step, wide), F32)),
+        *near_bundles,
+        far_bundle,
+        *(weights, back, agg),
+    )
+    outs = (shape((height, width), BF16), shape((width, wide), F32), shape((width, wide), F32))
+    return local(
+        functools.partial(layers_kernel, reps, 1.0 / math.sqrt(nodes)),
+        outs,
+        *near_bundles,
+        *far_pair,
+        *(weights, back, agg),
+        scratch=[
+            pltpu.VMEM((2 * CORES, step, wide), BF16),
+            pltpu.VMEM((2 * CORES, step, wide), BF16),
+            pltpu.VMEM((2 * CORES, step, wide), F32),
+        ],
+    )
+
+
+RELAYED = {}
+
+
+def hop_of(name, d):
+    hop = RELAYED.get(name, 0) & d
+    return (d ^ hop, hop) if hop and hop != d else (0, d)
+
+
+def fits_whole(features, edge_tiles, rows, reps):
+    nodes, wide = features.shape
+    block = edge_tiles.shape[2]
+    powers = all(n & (n - 1) == 0 for n in (rows, reps))
+    held = 2 * (nodes * nodes + 2 * nodes * wide + 2 * wide * wide)
+    width, share = wide // reps, nodes // reps
+    return (
+        held <= REPLICATED_BYTES
+        and powers
+        and rows % CORES == 0
+        and nodes // rows == block == width
+        and share % block == 0
+        and share == 2 * width
+        and wide == 2 * share
+        and rows == 4 * CORES
+    )
+
+
 def solution(mesh):
     placed = (
         P("row", "rep"),
@@ -87,10 +447,17 @@
         P("rep", None),
         P("row", "rep"),
     )
-    return jax.shard_map(
-        body,
-        mesh=mesh,
-        in_specs=placed,
-        out_specs=(P("row", "rep"), P("rep", None), P("rep", None)),
-        check_vma=False,
-    )
+
+    rows, reps = mesh.shape["row"], mesh.shape["rep"]
+    outs = (P("row", "rep"), P("rep", None), P("rep", None))
+
+    def run(features, edge_tiles, *rest):
+        whole = fits_whole(features, edge_tiles, rows, reps)
+
+        def body(*args):
+            return (whole_body if whole else split_body)(*args)
+
+        step = jax.shard_map(body, mesh=mesh, in_specs=placed, out_specs=outs, check_vma=False)
+        return step(features, edge_tiles, *rest)
+
+    return run

time: 194 us -> 60.6 us (0.31)
  waiting for transfers between devices: 117 us -> 31.2 us
  blocking collectives: 47.1 us -> 0 us
  starting transfers between devices: 0.16 us -> 18.3 us
  between operations: 14.5 us -> 1.38 us
  Pallas kernels: 0 us -> 9.51 us
  local copies, waits for them, and re-layouts: 6.2 us -> 0 us
  matrix products: 4.55 us -> 0 us
  other arithmetic: 4.11 us -> 0 us
    reduce_scatter x3 -> x0, waiting for transfers between devices: 59.3 us -> none  [the longest x1 33.7 us: body(): lax.psum_scatter(summed[:wanted].reshape(count, width), 'row', scatter_di...]
    psum x1 -> x0, waiting for transfers between devices: 58 us -> none  [body(): grad_second, grad_first = lax.psum((second_part, first_part), 'row')]
    all_gather x4 -> x0, blocking collectives: 47.1 us -> none  [the longest x2 30.3 us: gather_blocks(): whole = lax.all_gather(packed, 'row', axis=0, tiled=True)]
    ppermute x0 -> x17, waiting for transfers between devices: none -> 31.2 us  [swap(): return lax.ppermute(value, axis, [(i, i ^ d) for i in range(size)])]
    ppermute x0 -> x17, starting transfers between devices: none -> 18.3 us  [swap(): return lax.ppermute(value, axis, [(i, i ^ d) for i in range(size)])]
    pallas_call x0 -> x7, Pallas kernels: none -> 9.51 us  [the longest x6 7.76 us: local(): pl.pallas_call(kernel, out_shape=outs, in_specs=[vmem] * len(operands), o...]
    dot_general x7 -> x0, matrix products: 4.55 us -> none  [the longest x2 1.75 us: mix_columns(): partial_terms = jnp.dot(agg, weight, preferred_element_type=jnp.float32)]
    unnamed x14 -> x0, local copies, waits for them, and re-layouts: 4.09 us -> none
  transfers between devices with their start and end apart: 4 -> 17, of which waited for: 4 -> 8; matrix products, arithmetic and copies ran while one was open for 3% -> 0% of each run, Pallas kernels for 0% -> 5%
where the time goes in v2:
time: 60.6 us; the launch traced here: 60.3 us
  waiting for transfers between devices  31.2 us (51%)
  starting transfers between devices  18.3 us (30%)
  Pallas kernels  9.51 us (16%)
  between operations  1.38 us (2%)
    ppermute x17, waiting for transfers between devices, swap(): return lax.ppermute(value, axis, [(i, i ^ d) for i in range(size)])  31.2 us
    ppermute x17, starting transfers between devices, swap(): return lax.ppermute(value, axis, [(i, i ^ d) for i in range(size)])  18.3 us
    pallas_call x6, Pallas kernels, local(): pl.pallas_call(kernel, out_shape=outs, in_specs=[vmem] * len(operands), o...  7.76 us
    pallas_call x1, Pallas kernels, whole_body(): pl.pallas_call(functools.partial(pack_kernel, chips, share // block), out...  1.76 us
  transfers between devices with their start and end apart: 17, of which 8 were waited for; matrix products, arithmetic and copies ran while one was open for 0% of the time, Pallas kernels for 5%

profile of v2, /device:TPU:0, one launch (start us, length us, event | category | flops | bytes accessed | tf_op | source)
XLA Modules:
  0.0 60.3 jit_solution(14318573066395025708)
XLA Ops:
  1.3 1.8 %pack.1 = (bf16[2,128,256]{2,1,0:T(8,128)(2,1)S(1)}, bf16[3,128,256]{2,1,0:T(8,128)(2,1)S(1)}, bf16[5,128,256]{2,1,0:T(8,128)(2,1)S(1)}) custom-call(s32[1]{0:T(128)S(6)} %copy.10.counts_ref, s32[1,8]{1,0:T(1,128)} %sources_hbm.1, bf16[128,128]{1,0:T(8,128)(2,1)} %feat_ref.1, bf16[128,128]{1,0:T(8,128)(2,1)} %cot_ref.1, bf16[1,8,128,128]{3,2,1,0:T(8,128)(2,1)} %tiles_ref.1, ...), custom_call_target="tpu_custom_call" | custom-call | tf_op jit(solution)/shard_map/pack/pallas_call | solution.py:326
  3.0 4.1 %collective-permute-start.8 = (bf16[2,128,256]{2,1,0:T(8,128)(2,1)S(1)}, bf16[2,128,256]{2,1,0:T(8,128)(2,1)S(1)}, u32[]{:S(2)}, u32[]{:S(2)}) collective-permute-start(bf16[2,128,256]{2,1,0:T(8,128)(2,1)S(1)} %get-tuple-element.23), channel_id=1, source_target_pairs={{0,16},{4,20},{8,24},{12,28},{16,0},{20,4},{24,8},{28,12},{1,17},{... | collective-permute-start | bytes 393224 | tf_op jit(solution)/shard_map/ppermute | solution.py:345
  7.1 1.3 %collective-permute-start.12 = (bf16[2,128,256]{2,1,0:T(8,128)(2,1)S(1)}, bf16[2,128,256]{2,1,0:T(8,128)(2,1)S(1)}, u32[]{:S(2)}, u32[]{:S(2)}) collective-permute-start(bf16[2,128,256]{2,1,0:T(8,128)(2,1)S(1)} %get-tuple-element.23), channel_id=1, source_target_pairs={{0,24},{4,28},{8,16},{12,20},{16,8},{20,12},{24,0},{28,4},{1,25},{... | collective-permute-start | bytes 393224 | tf_op jit(solution)/shard_map/ppermute | solution.py:345
  8.5 8.6 %collective-permute-done.8.refs_0_ = bf16[2,128,256]{2,1,0:T(8,128)(2,1)S(1)} collective-permute-done((bf16[2,128,256]{2,1,0:T(8,128)(2,1)S(1)}, bf16[2,128,256]{2,1,0:T(8,128)(2,1)S(1)}, u32[]{:S(2)}, u32[]{:S(2)}) %collective-permute-start.8) | collective-permute-done | bytes 131104 | tf_op jit(solution)/shard_map/ppermute | solution.py:345
  17.1 1.9 %collective-permute-start.10 = (bf16[2,128,256]{2,1,0:T(8,128)(2,1)S(1)}, bf16[2,128,256]{2,1,0:T(8,128)(2,1)S(1)}, u32[]{:S(2)}, u32[]{:S(2)}) collective-permute-start(bf16[2,128,256]{2,1,0:T(8,128)(2,1)S(1)} %collective-permute-done.8.refs_0_), channel_id=1, source_target_pairs={{0,2},{1,3},{2,0},{3,1},{4,6},{5,7},{6,4},{7,5},{8,10},{9,11},{10,... | collective-permute-start | bytes 393224 | tf_op jit(solution)/shard_map/ppermute | solution.py:345
  19.0 1.4 %collective-permute-start.11 = (bf16[2,128,256]{2,1,0:T(8,128)(2,1)S(1)}, bf16[2,128,256]{2,1,0:T(8,128)(2,1)S(1)}, u32[]{:S(2)}, u32[]{:S(2)}) collective-permute-start(bf16[2,128,256]{2,1,0:T(8,128)(2,1)S(1)} %collective-permute-done.8.refs_0_), channel_id=1, source_target_pairs={{0,3},{1,2},{2,1},{3,0},{4,7},{5,6},{6,5},{7,4},{8,11},{9,10},{10,... | collective-permute-start | bytes 393224 | tf_op jit(solution)/shard_map/ppermute | solution.py:345
  20.6 1.9 %collective-permute-start.14 = (bf16[2,128,256]{2,1,0:T(8,128)(2,1)S(1)}, bf16[2,128,256]{2,1,0:T(8,128)(2,1)S(1)}, u32[]{:S(2)}, u32[]{:S(2)}) collective-permute-start(bf16[2,128,256]{2,1,0:T(8,128)(2,1)S(1)} %collective-permute-done.12.refs_4_), channel_id=1, source_target_pairs={{0,2},{1,3},{2,0},{3,1},{4,6},{5,7},{6,4},{7,5},{8,10},{9,11},{10,... | collective-permute-start | bytes 393224 | tf_op jit(solution)/shard_map/ppermute | solution.py:345
  22.5 1.4 %collective-permute-start.15 = (bf16[2,128,256]{2,1,0:T(8,128)(2,1)S(1)}, bf16[2,128,256]{2,1,0:T(8,128)(2,1)S(1)}, u32[]{:S(2)}, u32[]{:S(2)}) collective-permute-start(bf16[2,128,256]{2,1,0:T(8,128)(2,1)S(1)} %collective-permute-done.12.refs_4_), channel_id=1, source_target_pairs={{0,3},{1,2},{2,1},{3,0},{4,7},{5,6},{6,5},{7,4},{8,11},{9,10},{10,... | collective-permute-start | bytes 393224 | tf_op jit(solution)/shard_map/ppermute | solution.py:345
  23.9 3.1 %collective-permute-done.10.refs_2_ = bf16[2,128,256]{2,1,0:T(8,128)(2,1)S(1)} collective-permute-done((bf16[2,128,256]{2,1,0:T(8,128)(2,1)S(1)}, bf16[2,128,256]{2,1,0:T(8,128)(2,1)S(1)}, u32[]{:S(2)}, u32[]{:S(2)}) %collective-permute-start.10) | collective-permute-done | bytes 131104 | tf_op jit(solution)/shard_map/ppermute | solution.py:345
  27.0 1.5 %collective-permute-start.9 = (bf16[2,128,256]{2,1,0:T(8,128)(2,1)S(1)}, bf16[2,128,256]{2,1,0:T(8,128)(2,1)S(1)}, u32[]{:S(2)}, u32[]{:S(2)}) collective-permute-start(bf16[2,128,256]{2,1,0:T(8,128)(2,1)S(1)} %collective-permute-done.8.refs_0_), channel_id=1, source_target_pairs={{0,1},{1,0},{2,3},{3,2},{4,5},{5,4},{6,7},{7,6},{8,9},{9,8},{10,11... | collective-permute-start | bytes 393224 | tf_op jit(solution)/shard_map/ppermute | solution.py:345
  28.6 1.3 %collective-permute-done.15.refs_7_ = bf16[2,128,256]{2,1,0:T(8,128)(2,1)S(1)} collective-permute-done((bf16[2,128,256]{2,1,0:T(8,128)(2,1)S(1)}, bf16[2,128,256]{2,1,0:T(8,128)(2,1)S(1)}, u32[]{:S(2)}, u32[]{:S(2)}) %collective-permute-start.15) | collective-permute-done | bytes 131104 | tf_op jit(solution)/shard_map/ppermute | solution.py:345
  29.9 2.1 %collective-permute-done.9.refs_1_ = bf16[2,128,256]{2,1,0:T(8,128)(2,1)S(1)} collective-permute-done((bf16[2,128,256]{2,1,0:T(8,128)(2,1)S(1)}, bf16[2,128,256]{2,1,0:T(8,128)(2,1)S(1)}, u32[]{:S(2)}, u32[]{:S(2)}) %collective-permute-start.9) | collective-permute-done | bytes 131104 | tf_op jit(solution)/shard_map/ppermute | solution.py:345
  32.2 1.6 %collective-permute-start = (bf16[3,128,256]{2,1,0:T(8,128)(2,1)S(1)}, bf16[3,128,256]{2,1,0:T(8,128)(2,1)S(1)}, u32[]{:S(2)}, u32[]{:S(2)}) collective-permute-start(bf16[3,128,256]{2,1,0:T(8,128)(2,1)S(1)} %get-tuple-element.16.refs_0_), channel_id=1, source_target_pairs={{0,1},{1,0},{2,3},{3,2},{4,5},{5,4},{6,7},{7,6},{8,9},{9,8},{10,11... | collective-permute-start | bytes 589832 | tf_op jit(solution)/shard_map/ppermute | solution.py:345
  33.8 0.8 %collective-permute-start.1 = (bf16[3,128,256]{2,1,0:T(8,128)(2,1)S(1)}, bf16[3,128,256]{2,1,0:T(8,128)(2,1)S(1)}, u32[]{:S(2)}, u32[]{:S(2)}) collective-permute-start(bf16[3,128,256]{2,1,0:T(8,128)(2,1)S(1)} %get-tuple-element.16.refs_0_), channel_id=1, source_target_pairs={{0,2},{1,3},{2,0},{3,1},{4,6},{5,7},{6,4},{7,5},{8,10},{9,11},{10,... | collective-permute-start | bytes 589832 | tf_op jit(solution)/shard_map/ppermute | solution.py:345
  34.6 1.2 %collective-permute-start.2 = (bf16[3,128,256]{2,1,0:T(8,128)(2,1)S(1)}, bf16[3,128,256]{2,1,0:T(8,128)(2,1)S(1)}, u32[]{:S(2)}, u32[]{:S(2)}) collective-permute-start(bf16[3,128,256]{2,1,0:T(8,128)(2,1)S(1)} %get-tuple-element.16.refs_0_), channel_id=1, source_target_pairs={{0,3},{1,2},{2,1},{3,0},{4,7},{5,6},{6,5},{7,4},{8,11},{9,10},{10,... | collective-permute-start | bytes 589832 | tf_op jit(solution)/shard_map/ppermute | solution.py:345
  35.9 4.2 %collective-permute-done.refs_1_ = bf16[3,128,256]{2,1,0:T(8,128)(2,1)S(1)} collective-permute-done((bf16[3,128,256]{2,1,0:T(8,128)(2,1)S(1)}, bf16[3,128,256]{2,1,0:T(8,128)(2,1)S(1)}, u32[]{:S(2)}, u32[]{:S(2)}) %collective-permute-start) | collective-permute-done | bytes 196640 | tf_op jit(solution)/shard_map/ppermute | solution.py:345
  40.1 4.9 %collective-permute-done.1.refs_2_ = bf16[3,128,256]{2,1,0:T(8,128)(2,1)S(1)} collective-permute-done((bf16[3,128,256]{2,1,0:T(8,128)(2,1)S(1)}, bf16[3,128,256]{2,1,0:T(8,128)(2,1)S(1)}, u32[]{:S(2)}, u32[]{:S(2)}) %collective-permute-start.1) | collective-permute-done | bytes 196640 | tf_op jit(solution)/shard_map/ppermute | solution.py:345
  45.1 0.2 collective-permute-start.5
  45.4 0.5 collective-permute-start.7
  45.9 5.0 %collective-permute-done.5.peers = bf16[3,128,256]{2,1,0:T(8,128)(2,1)S(1)} collective-permute-done((bf16[3,128,256]{2,1,0:T(8,128)(2,1)S(1)}, bf16[3,128,256]{2,1,0:T(8,128)(2,1)S(1)}, u32[]{:S(2)}, u32[]{:S(2)}) %collective-permute-start.5) | collective-permute-done | bytes 196640 | tf_op jit(solution)/shard_map/ppermute | solution.py:345
  51.1 1.9 %collective-permute-done.6.refs_3_ = bf16[128,2048]{1,0:T(8,128)(2,1)S(1)} collective-permute-done((bf16[128,2048]{1,0:T(8,128)(2,1)S(1)}, bf16[128,2048]{1,0:T(8,128)(2,1)S(1)}, u32[]{:S(2)}, u32[]{:S(2)}) %collective-permute-start.6) | collective-permute-done | bytes 524320 | tf_op jit(solution)/shard_map/ppermute | solution.py:345
  52.9 1.6 %shard_map.96 = (bf16[256,2048]{1,0:T(8,128)(2,1)S(1)}, bf16[256,2048]{1,0:T(8,128)(2,1)S(1)}, bf16[2,512,512]{2,1,0:T(8,128)(2,1)S(1)}, f32[4,256,512]{2,1,0:T(8,128)S(1)}, f32[2,256,512]{2,1,0:T(8,128)S(1)}) custom-call(bf16[128,2048]{1,0:T(8,128)(2,1)S(1)} %get-tuple-element.18.refs_0_, bf16[128,2048]{1,0:T(8,128)(2,1)S(1)} %collective-permute-done.3.refs_1_, ...), custom_call_target="tpu_custom_call" | custom-call | tf_op jit(solution)/shard_map/pallas_call | solution.py:355
  54.5 1.1 %shard_map.98 = (f32[4,256,512]{2,1,0:T(8,128)S(1)}, f32[3,256,512]{2,1,0:T(8,128)S(1)}) custom-call(bf16[256,2048]{1,0:T(8,128)(2,1)S(1)} %get-tuple-element.21.refs_0_, bf16[256,2048]{1,0:T(8,128)(2,1)S(1)} %get-tuple-element.22.refs_1_, bf16[256,2048]{1,0:T(8,128)(2,1)S(1)} %shard_map.97.refs_2_, ...), custom_call_target="tpu_custom_call" | custom-call | tf_op jit(solution)/shard_map/pallas_call | solution.py:355
  55.6 4.7 %shard_map.99 = (bf16[128,128]{1,0:T(8,128)(2,1)}, f32[128,512]{1,0:T(8,128)}, f32[128,512]{1,0:T(8,128)}) custom-call(bf16[256,2048]{1,0:T(8,128)(2,1)S(1)} %get-tuple-element.21.refs_0_, bf16[256,2048]{1,0:T(8,128)(2,1)S(1)} %get-tuple-element.22.refs_1_, bf16[256,2048]{1,0:T(8,128)(2,1)S(1)} %shard_map.97.refs_2_, ...), custom_call_target="tpu_custom_call" | custom-call | tf_op jit(solution)/shard_map/pallas_call | solution.py:355
  (17 shorter events, 0.9 us)
Async XLA Ops:
  3.0 14.1 %collective-permute-start.8 = (bf16[2,128,256]{2,1,0:T(8,128)(2,1)S(1)}, bf16[2,128,256]{2,1,0:T(8,128)(2,1)S(1)}, u32[]{:S(2)}, u32[]{:S(2)}) collective-permute-start(bf16[2,128,256]{2,1,0:T(8,128)(2,1)S(1)} %get-tuple-element.23), channel_id=1, source_target_pairs={{0,16},{4,20},{8,24},{12,28},{16,0},{20,4},{24,8},{28,12},{1,17},{... | collective-permute-start | bytes 393224 | tf_op jit(solution)/shard_map/ppermute | solution.py:345
  7.1 13.3 %collective-permute-start.12 = (bf16[2,128,256]{2,1,0:T(8,128)(2,1)S(1)}, bf16[2,128,256]{2,1,0:T(8,128)(2,1)S(1)}, u32[]{:S(2)}, u32[]{:S(2)}) collective-permute-start(bf16[2,128,256]{2,1,0:T(8,128)(2,1)S(1)} %get-tuple-element.23), channel_id=1, source_target_pairs={{0,24},{4,28},{8,16},{12,20},{16,8},{20,12},{24,0},{28,4},{1,25},{... | collective-permute-start | bytes 393224 | tf_op jit(solution)/shard_map/ppermute | solution.py:345
  17.1 9.9 %collective-permute-start.10 = (bf16[2,128,256]{2,1,0:T(8,128)(2,1)S(1)}, bf16[2,128,256]{2,1,0:T(8,128)(2,1)S(1)}, u32[]{:S(2)}, u32[]{:S(2)}) collective-permute-start(bf16[2,128,256]{2,1,0:T(8,128)(2,1)S(1)} %collective-permute-done.8.refs_0_), channel_id=1, source_target_pairs={{0,2},{1,3},{2,0},{3,1},{4,6},{5,7},{6,4},{7,5},{8,10},{9,11},{10,... | collective-permute-start | bytes 393224 | tf_op jit(solution)/shard_map/ppermute | solution.py:345
  19.0 9.6 %collective-permute-start.11 = (bf16[2,128,256]{2,1,0:T(8,128)(2,1)S(1)}, bf16[2,128,256]{2,1,0:T(8,128)(2,1)S(1)}, u32[]{:S(2)}, u32[]{:S(2)}) collective-permute-start(bf16[2,128,256]{2,1,0:T(8,128)(2,1)S(1)} %collective-permute-done.8.refs_0_), channel_id=1, source_target_pairs={{0,3},{1,2},{2,1},{3,0},{4,7},{5,6},{6,5},{7,4},{8,11},{9,10},{10,... | collective-permute-start | bytes 393224 | tf_op jit(solution)/shard_map/ppermute | solution.py:345
  20.4 8.1 %collective-permute-start.13 = (bf16[2,128,256]{2,1,0:T(8,128)(2,1)S(1)}, bf16[2,128,256]{2,1,0:T(8,128)(2,1)S(1)}, u32[]{:S(2)}, u32[]{:S(2)}) collective-permute-start(bf16[2,128,256]{2,1,0:T(8,128)(2,1)S(1)} %collective-permute-done.12.refs_4_), channel_id=1, source_target_pairs={{0,1},{1,0},{2,3},{3,2},{4,5},{5,4},{6,7},{7,6},{8,9},{9,8},{10,11... | collective-permute-start | bytes 393224 | tf_op jit(solution)/shard_map/ppermute | solution.py:345
  20.6 8.0 %collective-permute-start.14 = (bf16[2,128,256]{2,1,0:T(8,128)(2,1)S(1)}, bf16[2,128,256]{2,1,0:T(8,128)(2,1)S(1)}, u32[]{:S(2)}, u32[]{:S(2)}) collective-permute-start(bf16[2,128,256]{2,1,0:T(8,128)(2,1)S(1)} %collective-permute-done.12.refs_4_), channel_id=1, source_target_pairs={{0,2},{1,3},{2,0},{3,1},{4,6},{5,7},{6,4},{7,5},{8,10},{9,11},{10,... | collective-permute-start | bytes 393224 | tf_op jit(solution)/shard_map/ppermute | solution.py:345
  22.5 7.4 %collective-permute-start.15 = (bf16[2,128,256]{2,1,0:T(8,128)(2,1)S(1)}, bf16[2,128,256]{2,1,0:T(8,128)(2,1)S(1)}, u32[]{:S(2)}, u32[]{:S(2)}) collective-permute-start(bf16[2,128,256]{2,1,0:T(8,128)(2,1)S(1)} %collective-permute-done.12.refs_4_), channel_id=1, source_target_pairs={{0,3},{1,2},{2,1},{3,0},{4,7},{5,6},{6,5},{7,4},{8,11},{9,10},{10,... | collective-permute-start | bytes 393224 | tf_op jit(solution)/shard_map/ppermute | solution.py:345
  27.0 5.0 %collective-permute-start.9 = (bf16[2,128,256]{2,1,0:T(8,128)(2,1)S(1)}, bf16[2,128,256]{2,1,0:T(8,128)(2,1)S(1)}, u32[]{:S(2)}, u32[]{:S(2)}) collective-permute-start(bf16[2,128,256]{2,1,0:T(8,128)(2,1)S(1)} %collective-permute-done.8.refs_0_), channel_id=1, source_target_pairs={{0,1},{1,0},{2,3},{3,2},{4,5},{5,4},{6,7},{7,6},{8,9},{9,8},{10,11... | collective-permute-start | bytes 393224 | tf_op jit(solution)/shard_map/ppermute | solution.py:345
  32.2 23.5 %collective-permute-start.16 = (bf16[256,2048]{1,0:T(8,128)(2,1)S(1)}, bf16[256,2048]{1,0:T(8,128)(2,1)S(1)}, u32[]{:S(2)}, u32[]{:S(2)}) collective-permute-start(bf16[256,2048]{1,0:T(8,128)(2,1)S(1)} %shard_map.97.refs_2_), channel_id=1, source_target_pairs={{0,4},{4,0},{8,12},{12,8},{16,20},{20,16},{24,28},{28,24},{1,5},{5... | collective-permute-start | bytes 3145736 | tf_op jit(solution)/shard_map/ppermute | solution.py:345
  32.2 7.8 %collective-permute-start = (bf16[3,128,256]{2,1,0:T(8,128)(2,1)S(1)}, bf16[3,128,256]{2,1,0:T(8,128)(2,1)S(1)}, u32[]{:S(2)}, u32[]{:S(2)}) collective-permute-start(bf16[3,128,256]{2,1,0:T(8,128)(2,1)S(1)} %get-tuple-element.16.refs_0_), channel_id=1, source_target_pairs={{0,1},{1,0},{2,3},{3,2},{4,5},{5,4},{6,7},{7,6},{8,9},{9,8},{10,11... | collective-permute-start | bytes 589832 | tf_op jit(solution)/shard_map/ppermute | solution.py:345
  33.8 11.2 %collective-permute-start.1 = (bf16[3,128,256]{2,1,0:T(8,128)(2,1)S(1)}, bf16[3,128,256]{2,1,0:T(8,128)(2,1)S(1)}, u32[]{:S(2)}, u32[]{:S(2)}) collective-permute-start(bf16[3,128,256]{2,1,0:T(8,128)(2,1)S(1)} %get-tuple-element.16.refs_0_), channel_id=1, source_target_pairs={{0,2},{1,3},{2,0},{3,1},{4,6},{5,7},{6,4},{7,5},{8,10},{9,11},{10,... | collective-permute-start | bytes 589832 | tf_op jit(solution)/shard_map/ppermute | solution.py:345
  34.6 10.4 %collective-permute-start.2 = (bf16[3,128,256]{2,1,0:T(8,128)(2,1)S(1)}, bf16[3,128,256]{2,1,0:T(8,128)(2,1)S(1)}, u32[]{:S(2)}, u32[]{:S(2)}) collective-permute-start(bf16[3,128,256]{2,1,0:T(8,128)(2,1)S(1)} %get-tuple-element.16.refs_0_), channel_id=1, source_target_pairs={{0,3},{1,2},{2,1},{3,0},{4,7},{5,6},{6,5},{7,4},{8,11},{9,10},{10,... | collective-permute-start | bytes 589832 | tf_op jit(solution)/shard_map/ppermute | solution.py:345
  35.8 10.1 %collective-permute-start.4 = (bf16[5,128,256]{2,1,0:T(8,128)(2,1)S(1)}, bf16[5,128,256]{2,1,0:T(8,128)(2,1)S(1)}, u32[]{:S(2)}, u32[]{:S(2)}) collective-permute-start(bf16[5,128,256]{2,1,0:T(8,128)(2,1)S(1)} %get-tuple-element.17.refs_4_), channel_id=1, source_target_pairs={{0,8},{4,12},{8,0},{12,4},{16,24},{20,28},{24,16},{28,20},{1,9},{5... | collective-permute-start | bytes 983048 | tf_op jit(solution)/shard_map/ppermute | solution.py:345
  45.1 5.7 %collective-permute-start.5 = (bf16[3,128,256]{2,1,0:T(8,128)(2,1)S(1)}, bf16[3,128,256]{2,1,0:T(8,128)(2,1)S(1)}, u32[]{:S(2)}, u32[]{:S(2)}) collective-permute-start(bf16[3,128,256]{2,1,0:T(8,128)(2,1)S(1)} %get-tuple-element.19), channel_id=1, source_target_pairs={{0,8},{4,12},{8,0},{12,4},{16,24},{20,28},{24,16},{28,20},{1,9},{5... | collective-permute-start | bytes 589832 | tf_op jit(solution)/shard_map/ppermute | solution.py:345
  45.3 5.7 %collective-permute-start.3 = (bf16[128,2048]{1,0:T(8,128)(2,1)S(1)}, bf16[128,2048]{1,0:T(8,128)(2,1)S(1)}, u32[]{:S(2)}, u32[]{:S(2)}) collective-permute-start(bf16[128,2048]{1,0:T(8,128)(2,1)S(1)} %get-tuple-element.18.refs_0_), channel_id=1, source_target_pairs={{0,4},{4,0},{8,12},{12,8},{16,20},{20,16},{24,28},{28,24},{1,5},{5... | collective-permute-start | bytes 1572872 | tf_op jit(solution)/shard_map/ppermute | solution.py:345
  45.4 5.7 %collective-permute-start.7 = (bf16[512,512]{1,0:T(8,128)(2,1)S(1)}, bf16[512,512]{1,0:T(8,128)(2,1)S(1)}, u32[]{:S(2)}, u32[]{:S(2)}) collective-permute-start(bf16[512,512]{1,0:T(8,128)(2,1)S(1)} %get-tuple-element.20.refs_4_), channel_id=1, source_target_pairs={{0,4},{4,0},{8,12},{12,8},{16,20},{20,16},{24,28},{28,24},{1,5},{5... | collective-permute-start | bytes 1572872 | tf_op jit(solution)/shard_map/ppermute | solution.py:345
  51.0 2.0 %collective-permute-start.6 = (bf16[128,2048]{1,0:T(8,128)(2,1)S(1)}, bf16[128,2048]{1,0:T(8,128)(2,1)S(1)}, u32[]{:S(2)}, u32[]{:S(2)}) collective-permute-start(bf16[128,2048]{1,0:T(8,128)(2,1)S(1)} %shard_map.95.refs_2_), channel_id=1, source_target_pairs={{0,4},{4,0},{8,12},{12,8},{16,20},{20,16},{24,28},{28,24},{1,5},{5... | collective-permute-start | bytes 1572872 | tf_op jit(solution)/shard_map/ppermute | solution.py:345

commit v3 on v2

--- a/solution.py
+++ b/solution.py
@@ -182,16 +182,18 @@
 
 
 def far_kernel(*refs):
-    *blocks, out_ref = refs
+    *blocks, feats_ref, rest_ref = refs
     reps = len(blocks) // 2
     rep = lax.axis_index("rep")
     half = lax.rem(lax.div(lax.axis_index("row"), CORES), 2)
     _, height, share = blocks[0].shape
+    width = share // 2
     for parity, chunk in ((half, blocks[:reps]), (1 - half, blocks[reps:])):
         rows = at(parity, height)
-        place_features(out_ref, rows, rep, [ref[0] for ref in chunk])
         for d, ref in enumerate(chunk):
-            out_ref[rows, at(rep ^ d, share, share * reps)] = ref[1]
+            feats_ref[rows, at(rep ^ d, width)] = ref[0, :, :width]
+            rest_ref[rows, at(rep ^ d, width)] = ref[0, :, width:]
+            rest_ref[rows, at(rep ^ d, share, width * reps)] = ref[1]
 
 
 def place_of(b):
@@ -202,10 +204,11 @@
 
 
 def parts_of(bundle, wide, step):
+    feats, rest, start = (*bundle, 0) if isinstance(bundle, tuple) else (bundle, bundle, wide)
     return (
-        bundle[:, :wide],
-        bundle[:, wide : 2 * wide],
-        lambda b: bundle[:, at(place_of(b), step, 2 * wide)],
+        feats[:, :wide],
+        rest[:, start : start + wide],
+        lambda b: rest[:, at(place_of(b), step, start + wide)],
     )
 
 
@@ -234,7 +237,7 @@
         w_ref[core ^ c] = weights[c][...]
     parts = [parts_of(bundle, wide, 2 * height) for bundle in bundles]
     for k, (_, cotangent, _) in enumerate(parts):
-        ba_s[k] = back_aggregates(cotangent[...], w_ref[1])
+        ba_s[k] = back_aggregates(cotangent, w_ref[1])
     for b in range(2 * CORES):
         terms = (dot(a(b), ba_s[k], ((0,), (0,))) for k, (_, _, a) in enumerate(parts))
         back_ref[b] = total_of(terms)
@@ -244,8 +247,9 @@
 
 
 def middle_kernel(*refs):
-    bundles, (w_ref, back_in, agg_in), (back_ref, agg_ref) = refs[:3], refs[3:6], refs[6:]
-    step = bundles[0].shape[0]
+    first, second, *far, w_ref, back_in, agg_in, back_ref, agg_ref = refs
+    bundles = first, second, tuple(far)
+    step = first.shape[0]
     parts = [parts_of(bundle, w_ref.shape[1], step) for bundle in bundles]
     feats, cotangent, a = parts[CORES]
     back_agg = back_aggregates(cotangent, w_ref[1])
@@ -256,39 +260,59 @@
     agg_ref[CORES] = total_of(dot(a(k), parts[k][0], ((1,), (0,))) for k in range(CORES + 1))
 
 
+def activate(total, weight, agg_ref, hidden_ref, slope_ref):
+    agg = total.astype(BF16)
+    agg_ref[...] = agg
+    pre = dot(agg, weight, ((1,), (0,)))
+    sig = jax.nn.sigmoid(pre)
+    hidden_ref[...] = (pre * sig).astype(BF16)
+    slope_ref[...] = sig * (1.0 + pre * (1.0 - sig))
+
+
+def hidden_kernel(*refs):
+    first, second, far_rest, feats, w_ref, agg_in, *outs = refs
+    step, wide = feats.shape
+    bundles = first, second, (None, far_rest)
+    for b, bundle in enumerate(bundles):
+        rest, start = (bundle[1], wide) if b == CORES else (bundle, 2 * wide)
+        columns = rest[:, at(place_of(CORES + 1), step, start)]
+        total = agg_in[b] + dot(columns, feats[...], ((1,), (0,)))
+        activate(total, w_ref[0], *(out.at[b] for out in outs))
+
+
 def layers_kernel(reps, scale, *refs):
-    bundles, (w_ref, back_ref, early_agg_ref), refs = refs[:4], refs[4:7], refs[7:]
-    emb_ref, gf_ref, gs_ref, af_s, hid_s, slope_s = refs
+    first, second, *far, w_ref, back_ref, early_agg, early_hidden, early_slope = refs[:11]
+    emb_ref, gf_ref, gs_ref, last_agg, last_hidden, last_slope = refs[11:]
+    bundles = first, second, tuple(far[:2]), tuple(far[2:])
     row, rep = lax.axis_index("row"), lax.axis_index("rep")
     chip = lax.div(row, CORES)
     height, width = emb_ref.shape
     wide = width * reps
     step = 2 * height
     count = len(bundles)
+    last = count - 1
     my_cols = at(rep, width)
     parts = [parts_of(bundle, wide, step) for bundle in bundles]
 
-    last = count - 1
     back_agg = back_aggregates(parts[last][1], w_ref[1])
-    for b in range(count):
-        a = parts[b][2]
-        if b < last:
-            total = early_agg_ref[b] + dot(a(last), parts[last][0], ((1,), (0,)))
-        else:
-            total = total_of(dot(a(k), parts[k][0], ((1,), (0,))) for k in range(count))
-        agg = total.astype(BF16)
-        af_s[b] = agg
-        pre = dot(agg, w_ref[0], ((1,), (0,)))
-        sig = jax.nn.sigmoid(pre)
-        hid_s[b] = (pre * sig).astype(BF16)
-        slope_s[b] = sig * (1.0 + pre * (1.0 - sig))
+    a = parts[last][2]
+    total = total_of(dot(a(k), parts[k][0], ((1,), (0,))) for k in range(count))
+    activate(total, w_ref[0], last_agg, last_hidden, last_slope)
+    agg_first, hidden, slope = (
+        [early.at[b] for b in range(last)] + [late]
+        for early, late in (
+            (early_agg, last_agg),
+            (early_hidden, last_hidden),
+            (early_slope, last_slope),
+        )
+    )
 
     for b in range(count):
         _, cotangent, a = parts[b]
         back_hidden = back_ref[b] + dot(parts[last][2](b), back_agg, ((0,), (0,)))
-        back_pre = (back_hidden * slope_s[b]).astype(BF16)
-        agg = total_of(dot(a(k), hid_s[k, :, my_cols], ((1,), (0,))) for k in range(count))
-        gf = dot(af_s[b, :, my_cols], back_pre, ((0,), (0,)))
+        back_pre = (back_hidden * slope[b][...]).astype(BF16)
+        agg = total_of(dot(a(k), hidden[k][:, my_cols], ((1,), (0,))) for k in range(count))
+        gf = dot(agg_first[b][:, my_cols], back_pre, ((0,), (0,)))
         gs = dot(agg.astype(BF16), cotangent, ((0,), (0,)))
         gf_ref[...] = gf if b == 0 else gf_ref[...] + gf
         gs_ref[...] = gs if b == 0 else gs_ref[...] + gs
@@ -297,7 +321,7 @@
 
     mine = at(lax.rem(chip, 2), height)
     agg = total_of(
-        dot(bundles[0][mine, at(place_of(k), step, 2 * wide)], hid_s[k], ((1,), (0,)))
+        dot(first[mine, at(place_of(k), step, 2 * wide)], hidden[k][...], ((1,), (0,)))
         for k in range(count)
     )
     emb_ref[...] = dot(agg.astype(BF16), w_ref[1, :, my_cols], ((1,), (0,))).astype(BF16)
@@ -344,12 +368,9 @@
     def swap(value, axis, size, d):
         return lax.ppermute(value, axis, [(i, i ^ d) for i in range(size)])
 
-    def spread(value, name):
-        values = [value]
-        for d in range(1, reps):
-            via, hop = hop_of(name, d)
-            values.append(swap(values[via], "rep", reps, hop))
-        return values
+    def spread(value):
+        arrived = [swap(value, "rep", reps, d) for d in range(1, reps)]
+        return [value, *arrived]
 
     def local(kernel, outs, *operands, scratch=()):
         return pl.pallas_call(
@@ -367,13 +388,14 @@
     third = swap(for_chips, "row", rows, CORES * 3)
     second = swap(for_chips, "row", rows, CORES * 2)
     from_next = swap(for_next, "row", rows, CORES)
-    own, third, second = spread(for_reps, "own"), spread(third, "third"), spread(second, "second")
+    own, third, second = spread(for_reps), spread(third), spread(second)
 
     outs = (rows_shape, shape((wide, wide), BF16), shape((reps - 1, height, share), BF16))
     own_rows, weight, peers = local(own_kernel, outs, *own, for_next)
     peers = swap(peers, "row", rows, CORES)
     (next_rows,) = local(next_kernel, (rows_shape,), from_next, peers)
-    (far_bundle,) = local(far_kernel, (bundle_shape,), *second, *third)
+    outs = (shape((step, wide), BF16), shape((step, wide + nodes), BF16))
+    far_feats, far_rest = local(far_kernel, outs, *second, *third)
     outs = (
         *(bundle_shape, bundle_shape),
         shape((2, wide, wide), BF16),
@@ -388,35 +410,26 @@
         *pair(weight),
         scratch=[pltpu.VMEM((CORES, step, wide), BF16)],
     )
-    far_pair = pair(far_bundle)
+    other_feats = swap(far_feats, "row", rows, 1)
+    other_rest = swap(far_rest, "row", rows, 1)
     back, agg = local(
         middle_kernel,
         (shape((2 * CORES, step, wide), F32), shape((CORES + 1, step, wide), F32)),
         *near_bundles,
-        far_bundle,
-        *(weights, back, agg),
-    )
+        *(far_feats, far_rest, weights, back, agg),
+    )
+    count = CORES + 1
+    outs = tuple(shape((count, step, wide), dtype) for dtype in (BF16, BF16, F32))
+    first_layer = local(hidden_kernel, outs, *near_bundles, far_rest, other_feats, weights, agg)
     outs = (shape((height, width), BF16), shape((width, wide), F32), shape((width, wide), F32))
     return local(
         functools.partial(layers_kernel, reps, 1.0 / math.sqrt(nodes)),
         outs,
         *near_bundles,
-        *far_pair,
-        *(weights, back, agg),
-        scratch=[
-            pltpu.VMEM((2 * CORES, step, wide), BF16),
-            pltpu.VMEM((2 * CORES, step, wide), BF16),
-            pltpu.VMEM((2 * CORES, step, wide), F32),
-        ],
-    )
-
-
-RELAYED = {}
-
-
-def hop_of(name, d):
-    hop = RELAYED.get(name, 0) & d
-    return (d ^ hop, hop) if hop and hop != d else (0, d)
+        *(far_feats, far_rest, other_feats, other_rest, weights, back),
+        *first_layer,
+        scratch=[pltpu.VMEM((step, wide), dtype) for dtype in (BF16, BF16, F32)],
+    )
 
 
 def fits_whole(features, edge_tiles, rows, reps):

time: 60.6 us -> 56.8 us (0.937)
  waiting for transfers between devices: 31.2 us -> 25.5 us
  starting transfers between devices: 18.3 us -> 20 us
    ppermute x17 -> x18, waiting for transfers between devices: 31.2 us -> 25.5 us  [swap(): return lax.ppermute(value, axis, [(i, i ^ d) for i in range(size)])]
    ppermute x17 -> x18, starting transfers between devices: 18.3 us -> 20 us  [swap(): return lax.ppermute(value, axis, [(i, i ^ d) for i in range(size)])]
    pallas_call x6 -> x7, Pallas kernels: 7.76 us -> 7.85 us  [local(): pl.pallas_call(kernel, out_shape=outs, in_specs=[vmem] * len(operands), o...]
  transfers between devices with their start and end apart: 17 -> 18, of which waited for: 8 -> 7; matrix products, arithmetic and copies ran while one was open for 0% -> 0% of each run, Pallas kernels for 5% -> 8%
where the time goes in v3:
time: 56.8 us; the launch traced here: 56.5 us
  waiting for transfers between devices  25.5 us (45%)
  starting transfers between devices  20 us (35%)
  Pallas kernels  9.6 us (17%)
  between operations  1.4 us (2%)
    ppermute x18, waiting for transfers between devices, swap(): return lax.ppermute(value, axis, [(i, i ^ d) for i in range(size)])  25.5 us
    ppermute x18, starting transfers between devices, swap(): return lax.ppermute(value, axis, [(i, i ^ d) for i in range(size)])  20 us
    pallas_call x7, Pallas kernels, local(): pl.pallas_call(kernel, out_shape=outs, in_specs=[vmem] * len(operands), o...  7.85 us
    pallas_call x1, Pallas kernels, whole_body(): pl.pallas_call(functools.partial(pack_kernel, chips, share // block), out...  1.76 us
  transfers between devices with their start and end apart: 18, of which 7 were waited for; matrix products, arithmetic and copies ran while one was open for 0% of the time, Pallas kernels for 8%

profile of v3, /device:TPU:0, one launch (start us, length us, event | category | flops | bytes accessed | tf_op | source)
XLA Modules:
  0.0 56.5 jit_solution(5529112883368643852)
XLA Ops:
  1.3 1.8 %pack.1 = (bf16[2,128,256]{2,1,0:T(8,128)(2,1)S(1)}, bf16[3,128,256]{2,1,0:T(8,128)(2,1)S(1)}, bf16[5,128,256]{2,1,0:T(8,128)(2,1)S(1)}) custom-call(s32[1]{0:T(128)S(6)} %copy.10.counts_ref, s32[1,8]{1,0:T(1,128)} %sources_hbm.1, bf16[128,128]{1,0:T(8,128)(2,1)} %feat_ref.1, bf16[128,128]{1,0:T(8,128)(2,1)} %cot_ref.1, bf16[1,8,128,128]{3,2,1,0:T(8,128)(2,1)} %tiles_ref.1, ...), custom_call_target="tpu_custom_call" | custom-call | tf_op jit(solution)/shard_map/pack/pallas_call | solution.py:350
  3.0 4.1 %collective-permute-start.8 = (bf16[2,128,256]{2,1,0:T(8,128)(2,1)S(1)}, bf16[2,128,256]{2,1,0:T(8,128)(2,1)S(1)}, u32[]{:S(2)}, u32[]{:S(2)}) collective-permute-start(bf16[2,128,256]{2,1,0:T(8,128)(2,1)S(1)} %get-tuple-element.28), channel_id=1, source_target_pairs={{0,16},{4,20},{8,24},{12,28},{16,0},{20,4},{24,8},{28,12},{1,17},{... | collective-permute-start | bytes 393224 | tf_op jit(solution)/shard_map/ppermute | solution.py:369
  7.1 1.3 %collective-permute-start.12 = (bf16[2,128,256]{2,1,0:T(8,128)(2,1)S(1)}, bf16[2,128,256]{2,1,0:T(8,128)(2,1)S(1)}, u32[]{:S(2)}, u32[]{:S(2)}) collective-permute-start(bf16[2,128,256]{2,1,0:T(8,128)(2,1)S(1)} %get-tuple-element.28), channel_id=1, source_target_pairs={{0,24},{4,28},{8,16},{12,20},{16,8},{20,12},{24,0},{28,4},{1,25},{... | collective-permute-start | bytes 393224 | tf_op jit(solution)/shard_map/ppermute | solution.py:369
  8.5 8.6 %collective-permute-done.8.refs_0_ = bf16[2,128,256]{2,1,0:T(8,128)(2,1)S(1)} collective-permute-done((bf16[2,128,256]{2,1,0:T(8,128)(2,1)S(1)}, bf16[2,128,256]{2,1,0:T(8,128)(2,1)S(1)}, u32[]{:S(2)}, u32[]{:S(2)}) %collective-permute-start.8) | collective-permute-done | bytes 131104 | tf_op jit(solution)/shard_map/ppermute | solution.py:369
  17.1 1.9 %collective-permute-start.10 = (bf16[2,128,256]{2,1,0:T(8,128)(2,1)S(1)}, bf16[2,128,256]{2,1,0:T(8,128)(2,1)S(1)}, u32[]{:S(2)}, u32[]{:S(2)}) collective-permute-start(bf16[2,128,256]{2,1,0:T(8,128)(2,1)S(1)} %collective-permute-done.8.refs_0_), channel_id=1, source_target_pairs={{0,2},{1,3},{2,0},{3,1},{4,6},{5,7},{6,4},{7,5},{8,10},{9,11},{10,... | collective-permute-start | bytes 393224 | tf_op jit(solution)/shard_map/ppermute | solution.py:369
  19.0 1.4 %collective-permute-start.11 = (bf16[2,128,256]{2,1,0:T(8,128)(2,1)S(1)}, bf16[2,128,256]{2,1,0:T(8,128)(2,1)S(1)}, u32[]{:S(2)}, u32[]{:S(2)}) collective-permute-start(bf16[2,128,256]{2,1,0:T(8,128)(2,1)S(1)} %collective-permute-done.8.refs_0_), channel_id=1, source_target_pairs={{0,3},{1,2},{2,1},{3,0},{4,7},{5,6},{6,5},{7,4},{8,11},{9,10},{10,... | collective-permute-start | bytes 393224 | tf_op jit(solution)/shard_map/ppermute | solution.py:369
  20.6 1.9 %collective-permute-start.14 = (bf16[2,128,256]{2,1,0:T(8,128)(2,1)S(1)}, bf16[2,128,256]{2,1,0:T(8,128)(2,1)S(1)}, u32[]{:S(2)}, u32[]{:S(2)}) collective-permute-start(bf16[2,128,256]{2,1,0:T(8,128)(2,1)S(1)} %collective-permute-done.12.refs_4_), channel_id=1, source_target_pairs={{0,2},{1,3},{2,0},{3,1},{4,6},{5,7},{6,4},{7,5},{8,10},{9,11},{10,... | collective-permute-start | bytes 393224 | tf_op jit(solution)/shard_map/ppermute | solution.py:369
  22.5 1.4 %collective-permute-start.15 = (bf16[2,128,256]{2,1,0:T(8,128)(2,1)S(1)}, bf16[2,128,256]{2,1,0:T(8,128)(2,1)S(1)}, u32[]{:S(2)}, u32[]{:S(2)}) collective-permute-start(bf16[2,128,256]{2,1,0:T(8,128)(2,1)S(1)} %collective-permute-done.12.refs_4_), channel_id=1, source_target_pairs={{0,3},{1,2},{2,1},{3,0},{4,7},{5,6},{6,5},{7,4},{8,11},{9,10},{10,... | collective-permute-start | bytes 393224 | tf_op jit(solution)/shard_map/ppermute | solution.py:369
  23.9 3.1 %collective-permute-done.10.refs_2_ = bf16[2,128,256]{2,1,0:T(8,128)(2,1)S(1)} collective-permute-done((bf16[2,128,256]{2,1,0:T(8,128)(2,1)S(1)}, bf16[2,128,256]{2,1,0:T(8,128)(2,1)S(1)}, u32[]{:S(2)}, u32[]{:S(2)}) %collective-permute-start.10) | collective-permute-done | bytes 131104 | tf_op jit(solution)/shard_map/ppermute | solution.py:369
  27.0 1.6 %collective-permute-start = (bf16[3,128,256]{2,1,0:T(8,128)(2,1)S(1)}, bf16[3,128,256]{2,1,0:T(8,128)(2,1)S(1)}, u32[]{:S(2)}, u32[]{:S(2)}) collective-permute-start(bf16[3,128,256]{2,1,0:T(8,128)(2,1)S(1)} %get-tuple-element.21.refs_0_), channel_id=1, source_target_pairs={{0,1},{1,0},{2,3},{3,2},{4,5},{5,4},{6,7},{7,6},{8,9},{9,8},{10,11... | collective-permute-start | bytes 589832 | tf_op jit(solution)/shard_map/ppermute | solution.py:369
  28.6 1.1 %collective-permute-start.1 = (bf16[3,128,256]{2,1,0:T(8,128)(2,1)S(1)}, bf16[3,128,256]{2,1,0:T(8,128)(2,1)S(1)}, u32[]{:S(2)}, u32[]{:S(2)}) collective-permute-start(bf16[3,128,256]{2,1,0:T(8,128)(2,1)S(1)} %get-tuple-element.21.refs_0_), channel_id=1, source_target_pairs={{0,2},{1,3},{2,0},{3,1},{4,6},{5,7},{6,4},{7,5},{8,10},{9,11},{10,... | collective-permute-start | bytes 589832 | tf_op jit(solution)/shard_map/ppermute | solution.py:369
  29.7 0.9 %collective-permute-start.2 = (bf16[3,128,256]{2,1,0:T(8,128)(2,1)S(1)}, bf16[3,128,256]{2,1,0:T(8,128)(2,1)S(1)}, u32[]{:S(2)}, u32[]{:S(2)}) collective-permute-start(bf16[3,128,256]{2,1,0:T(8,128)(2,1)S(1)} %get-tuple-element.21.refs_0_), channel_id=1, source_target_pairs={{0,3},{1,2},{2,1},{3,0},{4,7},{5,6},{6,5},{7,4},{8,11},{9,10},{10,... | collective-permute-start | bytes 589832 | tf_op jit(solution)/shard_map/ppermute | solution.py:369
  30.6 2.5 %collective-permute-done.14.refs_6_ = bf16[2,128,256]{2,1,0:T(8,128)(2,1)S(1)} collective-permute-done((bf16[2,128,256]{2,1,0:T(8,128)(2,1)S(1)}, bf16[2,128,256]{2,1,0:T(8,128)(2,1)S(1)}, u32[]{:S(2)}, u32[]{:S(2)}) %collective-permute-start.14) | collective-permute-done | bytes 131104 | tf_op jit(solution)/shard_map/ppermute | solution.py:369
  33.1 1.6 %collective-permute-start.9 = (bf16[2,128,256]{2,1,0:T(8,128)(2,1)S(1)}, bf16[2,128,256]{2,1,0:T(8,128)(2,1)S(1)}, u32[]{:S(2)}, u32[]{:S(2)}) collective-permute-start(bf16[2,128,256]{2,1,0:T(8,128)(2,1)S(1)} %collective-permute-done.8.refs_0_), channel_id=1, source_target_pairs={{0,1},{1,0},{2,3},{3,2},{4,5},{5,4},{6,7},{7,6},{8,9},{9,8},{10,11... | collective-permute-start | bytes 393224 | tf_op jit(solution)/shard_map/ppermute | solution.py:369
  34.8 4.4 %collective-permute-done.9.refs_1_ = bf16[2,128,256]{2,1,0:T(8,128)(2,1)S(1)} collective-permute-done((bf16[2,128,256]{2,1,0:T(8,128)(2,1)S(1)}, bf16[2,128,256]{2,1,0:T(8,128)(2,1)S(1)}, u32[]{:S(2)}, u32[]{:S(2)}) %collective-permute-start.9) | collective-permute-done | bytes 131104 | tf_op jit(solution)/shard_map/ppermute | solution.py:369
  39.6 1.5 %collective-permute-start.5 = (bf16[3,128,256]{2,1,0:T(8,128)(2,1)S(1)}, bf16[3,128,256]{2,1,0:T(8,128)(2,1)S(1)}, u32[]{:S(2)}, u32[]{:S(2)}) collective-permute-start(bf16[3,128,256]{2,1,0:T(8,128)(2,1)S(1)} %get-tuple-element.24), channel_id=1, source_target_pairs={{0,8},{4,12},{8,0},{12,4},{16,24},{20,28},{24,16},{28,20},{1,9},{5... | collective-permute-start | bytes 589832 | tf_op jit(solution)/shard_map/ppermute | solution.py:369
  41.3 0.3 collective-permute-start.7
  41.8 5.1 %collective-permute-done.5.peers = bf16[3,128,256]{2,1,0:T(8,128)(2,1)S(1)} collective-permute-done((bf16[3,128,256]{2,1,0:T(8,128)(2,1)S(1)}, bf16[3,128,256]{2,1,0:T(8,128)(2,1)S(1)}, u32[]{:S(2)}, u32[]{:S(2)}) %collective-permute-start.5) | collective-permute-done | bytes 196640 | tf_op jit(solution)/shard_map/ppermute | solution.py:369
  47.1 0.5 collective-permute-start.16
  47.6 1.4 %collective-permute-done.6.refs_3_ = bf16[128,2048]{1,0:T(8,128)(2,1)S(1)} collective-permute-done((bf16[128,2048]{1,0:T(8,128)(2,1)S(1)}, bf16[128,2048]{1,0:T(8,128)(2,1)S(1)}, u32[]{:S(2)}, u32[]{:S(2)}) %collective-permute-start.6) | collective-permute-done | bytes 524320 | tf_op jit(solution)/shard_map/ppermute | solution.py:369
  49.0 1.6 %shard_map.96 = (bf16[256,2048]{1,0:T(8,128)(2,1)S(1)}, bf16[256,2048]{1,0:T(8,128)(2,1)S(1)}, bf16[2,512,512]{2,1,0:T(8,128)(2,1)S(1)}, f32[4,256,512]{2,1,0:T(8,128)S(1)}, f32[2,256,512]{2,1,0:T(8,128)S(1)}) custom-call(bf16[128,2048]{1,0:T(8,128)(2,1)S(1)} %get-tuple-element.23.refs_0_, bf16[128,2048]{1,0:T(8,128)(2,1)S(1)} %collective-permute-done.3.refs_1_, ...), custom_call_target="tpu_custom_call" | custom-call | tf_op jit(solution)/shard_map/pallas_call | solution.py:376
  50.6 1.1 %shard_map.98 = (f32[4,256,512]{2,1,0:T(8,128)S(1)}, f32[3,256,512]{2,1,0:T(8,128)S(1)}) custom-call(bf16[256,2048]{1,0:T(8,128)(2,1)S(1)} %get-tuple-element.26.refs_0_, bf16[256,2048]{1,0:T(8,128)(2,1)S(1)} %get-tuple-element.27.refs_1_, bf16[256,512]{1,0:T(8,128)(2,1)S(1)} %get-tuple-element.29.refs_2_, ...), custom_call_target="tpu_custom_call" | custom-call | tf_op jit(solution)/shard_map/pallas_call | solution.py:376
  51.7 1.2 %shard_map.99 = (bf16[3,256,512]{2,1,0:T(8,128)(2,1)S(1)}, bf16[3,256,512]{2,1,0:T(8,128)(2,1)S(1)}, f32[3,256,512]{2,1,0:T(8,128)S(1)}) custom-call(bf16[256,2048]{1,0:T(8,128)(2,1)S(1)} %get-tuple-element.26.refs_0_, bf16[256,2048]{1,0:T(8,128)(2,1)S(1)} %get-tuple-element.27.refs_1_, bf16[256,1536]{1,0:T(8,128)(2,1)S(1)} %get-tuple-element.30.refs_3_.refs_2_, ...), custom_call_target="tpu_custom_call" | custom-call | tf_op jit(solution)/shard_map/pallas_call | solution.py:376
  53.0 3.6 %shard_map.100 = (bf16[128,128]{1,0:T(8,128)(2,1)}, f32[128,512]{1,0:T(8,128)}, f32[128,512]{1,0:T(8,128)}) custom-call(bf16[256,2048]{1,0:T(8,128)(2,1)S(1)} %get-tuple-element.26.refs_0_, bf16[256,2048]{1,0:T(8,128)(2,1)S(1)} %get-tuple-element.27.refs_1_, bf16[256,512]{1,0:T(8,128)(2,1)S(1)} %get-tuple-element.29.refs_2_, ...), custom_call_target="tpu_custom_call" | custom-call | tf_op jit(solution)/shard_map/pallas_call | solution.py:376
  (20 shorter events, 1.2 us)
Async XLA Ops:
  3.0 14.1 %collective-permute-start.8 = (bf16[2,128,256]{2,1,0:T(8,128)(2,1)S(1)}, bf16[2,128,256]{2,1,0:T(8,128)(2,1)S(1)}, u32[]{:S(2)}, u32[]{:S(2)}) collective-permute-start(bf16[2,128,256]{2,1,0:T(8,128)(2,1)S(1)} %get-tuple-element.28), channel_id=1, source_target_pairs={{0,16},{4,20},{8,24},{12,28},{16,0},{20,4},{24,8},{28,12},{1,17},{... | collective-permute-start | bytes 393224 | tf_op jit(solution)/shard_map/ppermute | solution.py:369
  7.1 13.3 %collective-permute-start.12 = (bf16[2,128,256]{2,1,0:T(8,128)(2,1)S(1)}, bf16[2,128,256]{2,1,0:T(8,128)(2,1)S(1)}, u32[]{:S(2)}, u32[]{:S(2)}) collective-permute-start(bf16[2,128,256]{2,1,0:T(8,128)(2,1)S(1)} %get-tuple-element.28), channel_id=1, source_target_pairs={{0,24},{4,28},{8,16},{12,20},{16,8},{20,12},{24,0},{28,4},{1,25},{... | collective-permute-start | bytes 393224 | tf_op jit(solution)/shard_map/ppermute | solution.py:369
  17.1 9.9 %collective-permute-start.10 = (bf16[2,128,256]{2,1,0:T(8,128)(2,1)S(1)}, bf16[2,128,256]{2,1,0:T(8,128)(2,1)S(1)}, u32[]{:S(2)}, u32[]{:S(2)}) collective-permute-start(bf16[2,128,256]{2,1,0:T(8,128)(2,1)S(1)} %collective-permute-done.8.refs_0_), channel_id=1, source_target_pairs={{0,2},{1,3},{2,0},{3,1},{4,6},{5,7},{6,4},{7,5},{8,10},{9,11},{10,... | collective-permute-start | bytes 393224 | tf_op jit(solution)/shard_map/ppermute | solution.py:369
  19.0 9.6 %collective-permute-start.11 = (bf16[2,128,256]{2,1,0:T(8,128)(2,1)S(1)}, bf16[2,128,256]{2,1,0:T(8,128)(2,1)S(1)}, u32[]{:S(2)}, u32[]{:S(2)}) collective-permute-start(bf16[2,128,256]{2,1,0:T(8,128)(2,1)S(1)} %collective-permute-done.8.refs_0_), channel_id=1, source_target_pairs={{0,3},{1,2},{2,1},{3,0},{4,7},{5,6},{6,5},{7,4},{8,11},{9,10},{10,... | collective-permute-start | bytes 393224 | tf_op jit(solution)/shard_map/ppermute | solution.py:369
  20.4 9.2 %collective-permute-start.13 = (bf16[2,128,256]{2,1,0:T(8,128)(2,1)S(1)}, bf16[2,128,256]{2,1,0:T(8,128)(2,1)S(1)}, u32[]{:S(2)}, u32[]{:S(2)}) collective-permute-start(bf16[2,128,256]{2,1,0:T(8,128)(2,1)S(1)} %collective-permute-done.12.refs_4_), channel_id=1, source_target_pairs={{0,1},{1,0},{2,3},{3,2},{4,5},{5,4},{6,7},{7,6},{8,9},{9,8},{10,11... | collective-permute-start | bytes 393224 | tf_op jit(solution)/shard_map/ppermute | solution.py:369
  20.6 12.5 %collective-permute-start.14 = (bf16[2,128,256]{2,1,0:T(8,128)(2,1)S(1)}, bf16[2,128,256]{2,1,0:T(8,128)(2,1)S(1)}, u32[]{:S(2)}, u32[]{:S(2)}) collective-permute-start(bf16[2,128,256]{2,1,0:T(8,128)(2,1)S(1)} %collective-permute-done.12.refs_4_), channel_id=1, source_target_pairs={{0,2},{1,3},{2,0},{3,1},{4,6},{5,7},{6,4},{7,5},{8,10},{9,11},{10,... | collective-permute-start | bytes 393224 | tf_op jit(solution)/shard_map/ppermute | solution.py:369
  22.5 12.3 %collective-permute-start.15 = (bf16[2,128,256]{2,1,0:T(8,128)(2,1)S(1)}, bf16[2,128,256]{2,1,0:T(8,128)(2,1)S(1)}, u32[]{:S(2)}, u32[]{:S(2)}) collective-permute-start(bf16[2,128,256]{2,1,0:T(8,128)(2,1)S(1)} %collective-permute-done.12.refs_4_), channel_id=1, source_target_pairs={{0,3},{1,2},{2,1},{3,0},{4,7},{5,6},{6,5},{7,4},{8,11},{9,10},{10,... | collective-permute-start | bytes 393224 | tf_op jit(solution)/shard_map/ppermute | solution.py:369
  27.0 12.4 %collective-permute-start = (bf16[3,128,256]{2,1,0:T(8,128)(2,1)S(1)}, bf16[3,128,256]{2,1,0:T(8,128)(2,1)S(1)}, u32[]{:S(2)}, u32[]{:S(2)}) collective-permute-start(bf16[3,128,256]{2,1,0:T(8,128)(2,1)S(1)} %get-tuple-element.21.refs_0_), channel_id=1, source_target_pairs={{0,1},{1,0},{2,3},{3,2},{4,5},{5,4},{6,7},{7,6},{8,9},{9,8},{10,11... | collective-permute-start | bytes 589832 | tf_op jit(solution)/shard_map/ppermute | solution.py:369
  28.6 10.8 %collective-permute-start.1 = (bf16[3,128,256]{2,1,0:T(8,128)(2,1)S(1)}, bf16[3,128,256]{2,1,0:T(8,128)(2,1)S(1)}, u32[]{:S(2)}, u32[]{:S(2)}) collective-permute-start(bf16[3,128,256]{2,1,0:T(8,128)(2,1)S(1)} %get-tuple-element.21.refs_0_), channel_id=1, source_target_pairs={{0,2},{1,3},{2,0},{3,1},{4,6},{5,7},{6,4},{7,5},{8,10},{9,11},{10,... | collective-permute-start | bytes 589832 | tf_op jit(solution)/shard_map/ppermute | solution.py:369
  29.7 9.8 %collective-permute-start.2 = (bf16[3,128,256]{2,1,0:T(8,128)(2,1)S(1)}, bf16[3,128,256]{2,1,0:T(8,128)(2,1)S(1)}, u32[]{:S(2)}, u32[]{:S(2)}) collective-permute-start(bf16[3,128,256]{2,1,0:T(8,128)(2,1)S(1)} %get-tuple-element.21.refs_0_), channel_id=1, source_target_pairs={{0,3},{1,2},{2,1},{3,0},{4,7},{5,6},{6,5},{7,4},{8,11},{9,10},{10,... | collective-permute-start | bytes 589832 | tf_op jit(solution)/shard_map/ppermute | solution.py:369
  33.1 6.0 %collective-permute-start.9 = (bf16[2,128,256]{2,1,0:T(8,128)(2,1)S(1)}, bf16[2,128,256]{2,1,0:T(8,128)(2,1)S(1)}, u32[]{:S(2)}, u32[]{:S(2)}) collective-permute-start(bf16[2,128,256]{2,1,0:T(8,128)(2,1)S(1)} %collective-permute-done.8.refs_0_), channel_id=1, source_target_pairs={{0,1},{1,0},{2,3},{3,2},{4,5},{5,4},{6,7},{7,6},{8,9},{9,8},{10,11... | collective-permute-start | bytes 393224 | tf_op jit(solution)/shard_map/ppermute | solution.py:369
  34.8 7.1 %collective-permute-start.4 = (bf16[5,128,256]{2,1,0:T(8,128)(2,1)S(1)}, bf16[5,128,256]{2,1,0:T(8,128)(2,1)S(1)}, u32[]{:S(2)}, u32[]{:S(2)}) collective-permute-start(bf16[5,128,256]{2,1,0:T(8,128)(2,1)S(1)} %get-tuple-element.22.refs_4_), channel_id=1, source_target_pairs={{0,8},{4,12},{8,0},{12,4},{16,24},{20,28},{24,16},{28,20},{1,9},{5... | collective-permute-start | bytes 983048 | tf_op jit(solution)/shard_map/ppermute | solution.py:369
  39.3 13.6 %collective-permute-start.17 = (bf16[256,1536]{1,0:T(8,128)(2,1)S(1)}, bf16[256,1536]{1,0:T(8,128)(2,1)S(1)}, u32[]{:S(2)}, u32[]{:S(2)}) collective-permute-start(bf16[256,1536]{1,0:T(8,128)(2,1)S(1)} %get-tuple-element.30.refs_3_.refs_2_), channel_id=1, source_target_pairs={{0,4},{4,0},{8,12},{12,8},{16,20},{20,16},{24,28},{28,24},{1,5},{5... | collective-permute-start | bytes 2359304 | tf_op jit(solution)/shard_map/ppermute | solution.py:369
  39.6 7.3 %collective-permute-start.5 = (bf16[3,128,256]{2,1,0:T(8,128)(2,1)S(1)}, bf16[3,128,256]{2,1,0:T(8,128)(2,1)S(1)}, u32[]{:S(2)}, u32[]{:S(2)}) collective-permute-start(bf16[3,128,256]{2,1,0:T(8,128)(2,1)S(1)} %get-tuple-element.24), channel_id=1, source_target_pairs={{0,8},{4,12},{8,0},{12,4},{16,24},{20,28},{24,16},{28,20},{1,9},{5... | collective-permute-start | bytes 589832 | tf_op jit(solution)/shard_map/ppermute | solution.py:369
  41.1 6.5 %collective-permute-start.3 = (bf16[128,2048]{1,0:T(8,128)(2,1)S(1)}, bf16[128,2048]{1,0:T(8,128)(2,1)S(1)}, u32[]{:S(2)}, u32[]{:S(2)}) collective-permute-start(bf16[128,2048]{1,0:T(8,128)(2,1)S(1)} %get-tuple-element.23.refs_0_), channel_id=1, source_target_pairs={{0,4},{4,0},{8,12},{12,8},{16,20},{20,16},{24,28},{28,24},{1,5},{5... | collective-permute-start | bytes 1572872 | tf_op jit(solution)/shard_map/ppermute | solution.py:369
  41.3 6.3 %collective-permute-start.7 = (bf16[512,512]{1,0:T(8,128)(2,1)S(1)}, bf16[512,512]{1,0:T(8,128)(2,1)S(1)}, u32[]{:S(2)}, u32[]{:S(2)}) collective-permute-start(bf16[512,512]{1,0:T(8,128)(2,1)S(1)} %get-tuple-element.25.refs_4_), channel_id=1, source_target_pairs={{0,4},{4,0},{8,12},{12,8},{16,20},{20,16},{24,28},{28,24},{1,5},{5... | collective-permute-start | bytes 1572872 | tf_op jit(solution)/shard_map/ppermute | solution.py:369
  47.0 2.0 %collective-permute-start.6 = (bf16[128,2048]{1,0:T(8,128)(2,1)S(1)}, bf16[128,2048]{1,0:T(8,128)(2,1)S(1)}, u32[]{:S(2)}, u32[]{:S(2)}) collective-permute-start(bf16[128,2048]{1,0:T(8,128)(2,1)S(1)} %shard_map.95.refs_2_), channel_id=1, source_target_pairs={{0,4},{4,0},{8,12},{12,8},{16,20},{20,16},{24,28},{28,24},{1,5},{5... | collective-permute-start | bytes 1572872 | tf_op jit(solution)/shard_map/ppermute | solution.py:369
  47.1 4.6 %collective-permute-start.16 = (bf16[256,512]{1,0:T(8,128)(2,1)S(1)}, bf16[256,512]{1,0:T(8,128)(2,1)S(1)}, u32[]{:S(2)}, u32[]{:S(2)}) collective-permute-start(bf16[256,512]{1,0:T(8,128)(2,1)S(1)} %get-tuple-element.29.refs_2_), channel_id=1, source_target_pairs={{0,4},{4,0},{8,12},{12,8},{16,20},{20,16},{24,28},{28,24},{1,5},{5... | collective-permute-start | bytes 786440 | tf_op jit(solution)/shard_map/ppermute | solution.py:369

commit v4 on v3

--- a/solution.py
+++ b/solution.py
@@ -150,12 +150,12 @@
         out_ref[rows, at(rep ^ d, width, width * reps)] = block[:, width:]
 
 
-def place_adjacency(out_ref, for_next):
+def place_adjacency(out_ref, rows, for_next):
     share = for_next.shape[2]
     count = for_next.shape[0] - 1
     start = out_ref.shape[1] - count * share
     for j in range(count):
-        out_ref[:, start + j * share : start + (j + 1) * share] = for_next[1 + j]
+        out_ref[rows, start + j * share : start + (j + 1) * share] = for_next[1 + j]
 
 
 def own_kernel(*refs):
@@ -164,21 +164,13 @@
     _, height, share = for_next.shape
     everything = pl.ds(0, height)
     place_features(rows_ref, everything, rep, [ref[0] for ref in own])
-    place_adjacency(rows_ref, for_next)
+    place_adjacency(rows_ref, everything, for_next)
     width = weight_ref.shape[0] // len(own)
     for d, ref in enumerate(own):
         for n in range(2):
             weight_ref[at(rep ^ d, width), n * share : (n + 1) * share] = ref[1 + n]
         if d:
             peers_ref[d - 1] = ref[0]
-
-
-def next_kernel(from_next, peers, rows_ref):
-    rep = lax.axis_index("rep")
-    everything = pl.ds(0, from_next.shape[1])
-    blocks = [from_next[0]] + [peers[d] for d in range(peers.shape[0])]
-    place_features(rows_ref, everything, rep, blocks)
-    place_adjacency(rows_ref, from_next)
 
 
 def far_kernel(*refs):
@@ -224,16 +216,20 @@
 
 
 def early_kernel(*refs):
-    own_rows, next_rows, weights, refs = refs[:2], refs[2:4], refs[4:6], refs[6:]
+    own_rows, from_next, peers, weights = (refs[n : n + 2] for n in range(0, 8, 2))
+    refs = refs[8:]
     first_bundle, second_bundle, w_ref, back_ref, agg_ref, ba_s = refs
     bundles = first_bundle, second_bundle
-    row = lax.axis_index("row")
+    row, rep = lax.axis_index("row"), lax.axis_index("rep")
     core, half = lax.rem(row, CORES), lax.rem(lax.div(row, CORES), 2)
     height = own_rows[0].shape[0]
+    mine, other = at(half, height), at(1 - half, height)
     wide = w_ref.shape[1]
     for c in range(CORES):
-        bundles[c][at(half, height), :] = own_rows[c][...]
-        bundles[c][at(1 - half, height), :] = next_rows[c][...]
+        bundles[c][mine, :] = own_rows[c][...]
+        blocks = [from_next[c][0]] + [peers[c][d] for d in range(peers[c].shape[0])]
+        place_features(bundles[c], other, rep, blocks)
+        place_adjacency(bundles[c], other, from_next[c])
         w_ref[core ^ c] = weights[c][...]
     parts = [parts_of(bundle, wide, 2 * height) for bundle in bundles]
     for k, (_, cotangent, _) in enumerate(parts):
@@ -307,17 +303,21 @@
         )
     )
 
+    back_pre, agg_second = [], []
     for b in range(count):
-        _, cotangent, a = parts[b]
+        a = parts[b][2]
         back_hidden = back_ref[b] + dot(parts[last][2](b), back_agg, ((0,), (0,)))
-        back_pre = (back_hidden * slope[b][...]).astype(BF16)
+        back_pre.append((back_hidden * slope[b][...]).astype(BF16))
+    gf = total_of(
+        dot(agg_first[b][:, my_cols], back_pre[b], ((0,), (0,))) for b in range(count)
+    )
+    gf_ref[...] = gf * scale
+    for b in range(count):
+        a = parts[b][2]
         agg = total_of(dot(a(k), hidden[k][:, my_cols], ((1,), (0,))) for k in range(count))
-        gf = dot(agg_first[b][:, my_cols], back_pre, ((0,), (0,)))
-        gs = dot(agg.astype(BF16), cotangent, ((0,), (0,)))
-        gf_ref[...] = gf if b == 0 else gf_ref[...] + gf
-        gs_ref[...] = gs if b == 0 else gs_ref[...] + gs
-    gf_ref[...] = gf_ref[...] * scale
-    gs_ref[...] = gs_ref[...] * scale
+        agg_second.append(agg.astype(BF16))
+    gs = total_of(dot(agg_second[b], parts[b][1], ((0,), (0,))) for b in range(count))
+    gs_ref[...] = gs * scale
 
     mine = at(lax.rem(chip, 2), height)
     agg = total_of(
@@ -393,7 +393,6 @@
     outs = (rows_shape, shape((wide, wide), BF16), shape((reps - 1, height, share), BF16))
     own_rows, weight, peers = local(own_kernel, outs, *own, for_next)
     peers = swap(peers, "row", rows, CORES)
-    (next_rows,) = local(next_kernel, (rows_shape,), from_next, peers)
     outs = (shape((step, wide), BF16), shape((step, wide + nodes), BF16))
     far_feats, far_rest = local(far_kernel, outs, *second, *third)
     outs = (
@@ -406,7 +405,8 @@
         early_kernel,
         outs,
         *pair(own_rows),
-        *pair(next_rows),
+        *pair(from_next),
+        *pair(peers),
         *pair(weight),
         scratch=[pltpu.VMEM((CORES, step, wide), BF16)],
     )

time: 56.8 us -> 57.3 us (level)
  starting transfers between devices: 20 us -> 20.9 us
    ppermute x18 -> x19, starting transfers between devices: 20 us -> 20.9 us  [swap(): return lax.ppermute(value, axis, [(i, i ^ d) for i in range(size)])]
    pallas_call x7 -> x6, Pallas kernels: 7.85 us -> 7.3 us  [local(): pl.pallas_call(kernel, out_shape=outs, in_specs=[vmem] * len(operands), o...]
    ppermute x18 -> x19, waiting for transfers between devices: 25.5 us -> 25.7 us  [swap(): return lax.ppermute(value, axis, [(i, i ^ d) for i in range(size)])]
  transfers between devices with their start and end apart: 18 -> 19, of which waited for: 7 -> 9; matrix products, arithmetic and copies ran while one was open for 0% -> 0% of each run, Pallas kernels for 8% -> 7%
where the time goes in v4:
time: 57.3 us; the launch traced here: 57 us
  waiting for transfers between devices  25.7 us (45%)
  starting transfers between devices  20.9 us (36%)
  Pallas kernels  9.06 us (16%)
  between operations  1.37 us (2%)
    ppermute x19, waiting for transfers between devices, swap(): return lax.ppermute(value, axis, [(i, i ^ d) for i in range(size)])  25.7 us
    ppermute x19, starting transfers between devices, swap(): return lax.ppermute(value, axis, [(i, i ^ d) for i in range(size)])  20.9 us
    pallas_call x6, Pallas kernels, local(): pl.pallas_call(kernel, out_shape=outs, in_specs=[vmem] * len(operands), o...  7.3 us
    pallas_call x1, Pallas kernels, whole_body(): pl.pallas_call(functools.partial(pack_kernel, chips, share // block), out...  1.76 us
  transfers between devices with their start and end apart: 19, of which 9 were waited for; matrix products, arithmetic and copies ran while one was open for 0% of the time, Pallas kernels for 7%

profile of v4, /device:TPU:0, one launch (start us, length us, event | category | flops | bytes accessed | tf_op | source)
XLA Modules:
  0.0 57.0 jit_solution(6405206552120400938)
XLA Ops:
  1.3 1.8 %pack.1 = (bf16[2,128,256]{2,1,0:T(8,128)(2,1)S(1)}, bf16[3,128,256]{2,1,0:T(8,128)(2,1)S(1)}, bf16[5,128,256]{2,1,0:T(8,128)(2,1)S(1)}) custom-call(s32[1]{0:T(128)S(6)} %copy.10.counts_ref, s32[1,8]{1,0:T(1,128)} %sources_hbm.1, bf16[128,128]{1,0:T(8,128)(2,1)} %feat_ref.1, bf16[128,128]{1,0:T(8,128)(2,1)} %cot_ref.1, bf16[1,8,128,128]{3,2,1,0:T(8,128)(2,1)} %tiles_ref.1, ...), custom_call_target="tpu_custom_call" | custom-call | tf_op jit(solution)/shard_map/pack/pallas_call | solution.py:350
  3.0 4.1 %collective-permute-start.9 = (bf16[2,128,256]{2,1,0:T(8,128)(2,1)S(1)}, bf16[2,128,256]{2,1,0:T(8,128)(2,1)S(1)}, u32[]{:S(2)}, u32[]{:S(2)}) collective-permute-start(bf16[2,128,256]{2,1,0:T(8,128)(2,1)S(1)} %get-tuple-element.28), channel_id=1, source_target_pairs={{0,16},{4,20},{8,24},{12,28},{16,0},{20,4},{24,8},{28,12},{1,17},{... | collective-permute-start | bytes 393224 | tf_op jit(solution)/shard_map/ppermute | solution.py:369
  7.1 1.3 %collective-permute-start.13 = (bf16[2,128,256]{2,1,0:T(8,128)(2,1)S(1)}, bf16[2,128,256]{2,1,0:T(8,128)(2,1)S(1)}, u32[]{:S(2)}, u32[]{:S(2)}) collective-permute-start(bf16[2,128,256]{2,1,0:T(8,128)(2,1)S(1)} %get-tuple-element.28), channel_id=1, source_target_pairs={{0,24},{4,28},{8,16},{12,20},{16,8},{20,12},{24,0},{28,4},{1,25},{... | collective-permute-start | bytes 393224 | tf_op jit(solution)/shard_map/ppermute | solution.py:369
  8.5 8.6 %collective-permute-done.9.refs_0_ = bf16[2,128,256]{2,1,0:T(8,128)(2,1)S(1)} collective-permute-done((bf16[2,128,256]{2,1,0:T(8,128)(2,1)S(1)}, bf16[2,128,256]{2,1,0:T(8,128)(2,1)S(1)}, u32[]{:S(2)}, u32[]{:S(2)}) %collective-permute-start.9) | collective-permute-done | bytes 131104 | tf_op jit(solution)/shard_map/ppermute | solution.py:369
  17.1 1.8 %collective-permute-start.10 = (bf16[2,128,256]{2,1,0:T(8,128)(2,1)S(1)}, bf16[2,128,256]{2,1,0:T(8,128)(2,1)S(1)}, u32[]{:S(2)}, u32[]{:S(2)}) collective-permute-start(bf16[2,128,256]{2,1,0:T(8,128)(2,1)S(1)} %collective-permute-done.9.refs_0_), channel_id=1, source_target_pairs={{0,1},{1,0},{2,3},{3,2},{4,5},{5,4},{6,7},{7,6},{8,9},{9,8},{10,11... | collective-permute-start | bytes 393224 | tf_op jit(solution)/shard_map/ppermute | solution.py:369
  18.9 1.5 %collective-permute-start.11 = (bf16[2,128,256]{2,1,0:T(8,128)(2,1)S(1)}, bf16[2,128,256]{2,1,0:T(8,128)(2,1)S(1)}, u32[]{:S(2)}, u32[]{:S(2)}) collective-permute-start(bf16[2,128,256]{2,1,0:T(8,128)(2,1)S(1)} %collective-permute-done.9.refs_0_), channel_id=1, source_target_pairs={{0,2},{1,3},{2,0},{3,1},{4,6},{5,7},{6,4},{7,5},{8,10},{9,11},{10,... | collective-permute-start | bytes 393224 | tf_op jit(solution)/shard_map/ppermute | solution.py:369
  20.6 1.8 %collective-permute-start.14 = (bf16[2,128,256]{2,1,0:T(8,128)(2,1)S(1)}, bf16[2,128,256]{2,1,0:T(8,128)(2,1)S(1)}, u32[]{:S(2)}, u32[]{:S(2)}) collective-permute-start(bf16[2,128,256]{2,1,0:T(8,128)(2,1)S(1)} %collective-permute-done.13.refs_4_), channel_id=1, source_target_pairs={{0,1},{1,0},{2,3},{3,2},{4,5},{5,4},{6,7},{7,6},{8,9},{9,8},{10,11... | collective-permute-start | bytes 393224 | tf_op jit(solution)/shard_map/ppermute | solution.py:369
  22.4 1.5 %collective-permute-start.15 = (bf16[2,128,256]{2,1,0:T(8,128)(2,1)S(1)}, bf16[2,128,256]{2,1,0:T(8,128)(2,1)S(1)}, u32[]{:S(2)}, u32[]{:S(2)}) collective-permute-start(bf16[2,128,256]{2,1,0:T(8,128)(2,1)S(1)} %collective-permute-done.13.refs_4_), channel_id=1, source_target_pairs={{0,2},{1,3},{2,0},{3,1},{4,6},{5,7},{6,4},{7,5},{8,10},{9,11},{10,... | collective-permute-start | bytes 393224 | tf_op jit(solution)/shard_map/ppermute | solution.py:369
  24.0 2.3 %collective-permute-start.16 = (bf16[2,128,256]{2,1,0:T(8,128)(2,1)S(1)}, bf16[2,128,256]{2,1,0:T(8,128)(2,1)S(1)}, u32[]{:S(2)}, u32[]{:S(2)}) collective-permute-start(bf16[2,128,256]{2,1,0:T(8,128)(2,1)S(1)} %collective-permute-done.13.refs_4_), channel_id=1, source_target_pairs={{0,3},{1,2},{2,1},{3,0},{4,7},{5,6},{6,5},{7,4},{8,11},{9,10},{10,... | collective-permute-start | bytes 393224 | tf_op jit(solution)/shard_map/ppermute | solution.py:369
  26.3 1.7 %collective-permute-done.11.refs_2_ = bf16[2,128,256]{2,1,0:T(8,128)(2,1)S(1)} collective-permute-done((bf16[2,128,256]{2,1,0:T(8,128)(2,1)S(1)}, bf16[2,128,256]{2,1,0:T(8,128)(2,1)S(1)}, u32[]{:S(2)}, u32[]{:S(2)}) %collective-permute-start.11) | collective-permute-done | bytes 131104 | tf_op jit(solution)/shard_map/ppermute | solution.py:369
  28.0 1.8 %collective-permute-start.1 = (bf16[3,128,256]{2,1,0:T(8,128)(2,1)S(1)}, bf16[3,128,256]{2,1,0:T(8,128)(2,1)S(1)}, u32[]{:S(2)}, u32[]{:S(2)}) collective-permute-start(bf16[3,128,256]{2,1,0:T(8,128)(2,1)S(1)} %get-tuple-element.21.refs_0_), channel_id=1, source_target_pairs={{0,2},{1,3},{2,0},{3,1},{4,6},{5,7},{6,4},{7,5},{8,10},{9,11},{10,... | collective-permute-start | bytes 589832 | tf_op jit(solution)/shard_map/ppermute | solution.py:369
  29.7 2.2 %collective-permute-start.2 = (bf16[3,128,256]{2,1,0:T(8,128)(2,1)S(1)}, bf16[3,128,256]{2,1,0:T(8,128)(2,1)S(1)}, u32[]{:S(2)}, u32[]{:S(2)}) collective-permute-start(bf16[3,128,256]{2,1,0:T(8,128)(2,1)S(1)} %get-tuple-element.21.refs_0_), channel_id=1, source_target_pairs={{0,3},{1,2},{2,1},{3,0},{4,7},{5,6},{6,5},{7,4},{8,11},{9,10},{10,... | collective-permute-start | bytes 589832 | tf_op jit(solution)/shard_map/ppermute | solution.py:369
  31.9 1.6 %collective-permute-done.16.refs_7_ = bf16[2,128,256]{2,1,0:T(8,128)(2,1)S(1)} collective-permute-done((bf16[2,128,256]{2,1,0:T(8,128)(2,1)S(1)}, bf16[2,128,256]{2,1,0:T(8,128)(2,1)S(1)}, u32[]{:S(2)}, u32[]{:S(2)}) %collective-permute-start.16) | collective-permute-done | bytes 131104 | tf_op jit(solution)/shard_map/ppermute | solution.py:369
  33.8 2.7 %collective-permute-done.refs_1_ = bf16[3,128,256]{2,1,0:T(8,128)(2,1)S(1)} collective-permute-done((bf16[3,128,256]{2,1,0:T(8,128)(2,1)S(1)}, bf16[3,128,256]{2,1,0:T(8,128)(2,1)S(1)}, u32[]{:S(2)}, u32[]{:S(2)}) %collective-permute-start) | collective-permute-done | bytes 196640 | tf_op jit(solution)/shard_map/ppermute | solution.py:369
  36.5 1.6 %collective-permute-done.1.refs_2_ = bf16[3,128,256]{2,1,0:T(8,128)(2,1)S(1)} collective-permute-done((bf16[3,128,256]{2,1,0:T(8,128)(2,1)S(1)}, bf16[3,128,256]{2,1,0:T(8,128)(2,1)S(1)}, u32[]{:S(2)}, u32[]{:S(2)}) %collective-permute-start.1) | collective-permute-done | bytes 196640 | tf_op jit(solution)/shard_map/ppermute | solution.py:369
  38.1 1.4 %collective-permute-done.2.refs_3_ = bf16[3,128,256]{2,1,0:T(8,128)(2,1)S(1)} collective-permute-done((bf16[3,128,256]{2,1,0:T(8,128)(2,1)S(1)}, bf16[3,128,256]{2,1,0:T(8,128)(2,1)S(1)}, u32[]{:S(2)}, u32[]{:S(2)}) %collective-permute-start.2) | collective-permute-done | bytes 196640 | tf_op jit(solution)/shard_map/ppermute | solution.py:369
  39.7 1.1 %collective-permute-start.6 = (bf16[3,128,256]{2,1,0:T(8,128)(2,1)S(1)}, bf16[3,128,256]{2,1,0:T(8,128)(2,1)S(1)}, u32[]{:S(2)}, u32[]{:S(2)}) collective-permute-start(bf16[3,128,256]{2,1,0:T(8,128)(2,1)S(1)} %get-tuple-element.24), channel_id=1, source_target_pairs={{0,8},{4,12},{8,0},{12,4},{16,24},{20,28},{24,16},{28,20},{1,9},{5... | collective-permute-start | bytes 589832 | tf_op jit(solution)/shard_map/ppermute | solution.py:369
  41.3 6.8 %collective-permute-done.6.refs_4_ = bf16[3,128,256]{2,1,0:T(8,128)(2,1)S(1)} collective-permute-done((bf16[3,128,256]{2,1,0:T(8,128)(2,1)S(1)}, bf16[3,128,256]{2,1,0:T(8,128)(2,1)S(1)}, u32[]{:S(2)}, u32[]{:S(2)}) %collective-permute-start.6) | collective-permute-done | bytes 196640 | tf_op jit(solution)/shard_map/ppermute | solution.py:369
  48.1 0.5 collective-permute-start.5
  48.6 0.9 %collective-permute-done.7.refs_5_ = bf16[3,128,256]{2,1,0:T(8,128)(2,1)S(1)} collective-permute-done((bf16[3,128,256]{2,1,0:T(8,128)(2,1)S(1)}, bf16[3,128,256]{2,1,0:T(8,128)(2,1)S(1)}, u32[]{:S(2)}, u32[]{:S(2)}) %collective-permute-start.7) | collective-permute-done | bytes 196640 | tf_op jit(solution)/shard_map/ppermute | solution.py:369
  50.0 1.6 %shard_map.95 = (bf16[256,2048]{1,0:T(8,128)(2,1)S(1)}, bf16[256,2048]{1,0:T(8,128)(2,1)S(1)}, bf16[2,512,512]{2,1,0:T(8,128)(2,1)S(1)}, f32[4,256,512]{2,1,0:T(8,128)S(1)}, f32[2,256,512]{2,1,0:T(8,128)S(1)}) custom-call(bf16[128,2048]{1,0:T(8,128)(2,1)S(1)} %get-tuple-element.23.refs_0_, bf16[128,2048]{1,0:T(8,128)(2,1)S(1)} %collective-permute-done.3.refs_1_, ...), custom_call_target="tpu_custom_call" | custom-call | tf_op jit(solution)/shard_map/pallas_call | solution.py:376
  51.6 1.1 %shard_map.97 = (f32[4,256,512]{2,1,0:T(8,128)S(1)}, f32[3,256,512]{2,1,0:T(8,128)S(1)}) custom-call(bf16[256,2048]{1,0:T(8,128)(2,1)S(1)} %get-tuple-element.26.refs_0_, bf16[256,2048]{1,0:T(8,128)(2,1)S(1)} %get-tuple-element.27.refs_1_, bf16[256,512]{1,0:T(8,128)(2,1)S(1)} %get-tuple-element.29.refs_2_, ...), custom_call_target="tpu_custom_call" | custom-call | tf_op jit(solution)/shard_map/pallas_call | solution.py:376
  52.7 1.2 %shard_map.98 = (bf16[3,256,512]{2,1,0:T(8,128)(2,1)S(1)}, bf16[3,256,512]{2,1,0:T(8,128)(2,1)S(1)}, f32[3,256,512]{2,1,0:T(8,128)S(1)}) custom-call(bf16[256,2048]{1,0:T(8,128)(2,1)S(1)} %get-tuple-element.26.refs_0_, bf16[256,2048]{1,0:T(8,128)(2,1)S(1)} %get-tuple-element.27.refs_1_, bf16[256,1536]{1,0:T(8,128)(2,1)S(1)} %get-tuple-element.30.refs_3_.refs_2_, ...), custom_call_target="tpu_custom_call" | custom-call | tf_op jit(solution)/shard_map/pallas_call | solution.py:376
  53.9 3.1 %shard_map.99 = (bf16[128,128]{1,0:T(8,128)(2,1)}, f32[128,512]{1,0:T(8,128)}, f32[128,512]{1,0:T(8,128)}) custom-call(bf16[256,2048]{1,0:T(8,128)(2,1)S(1)} %get-tuple-element.26.refs_0_, bf16[256,2048]{1,0:T(8,128)(2,1)S(1)} %get-tuple-element.27.refs_1_, bf16[256,512]{1,0:T(8,128)(2,1)S(1)} %get-tuple-element.29.refs_2_, ...), custom_call_target="tpu_custom_call" | custom-call | tf_op jit(solution)/shard_map/pallas_call | solution.py:376
  (21 shorter events, 1.6 us)
Async XLA Ops:
  3.0 14.1 %collective-permute-start.9 = (bf16[2,128,256]{2,1,0:T(8,128)(2,1)S(1)}, bf16[2,128,256]{2,1,0:T(8,128)(2,1)S(1)}, u32[]{:S(2)}, u32[]{:S(2)}) collective-permute-start(bf16[2,128,256]{2,1,0:T(8,128)(2,1)S(1)} %get-tuple-element.28), channel_id=1, source_target_pairs={{0,16},{4,20},{8,24},{12,28},{16,0},{20,4},{24,8},{28,12},{1,17},{... | collective-permute-start | bytes 393224 | tf_op jit(solution)/shard_map/ppermute | solution.py:369
  7.1 13.5 %collective-permute-start.13 = (bf16[2,128,256]{2,1,0:T(8,128)(2,1)S(1)}, bf16[2,128,256]{2,1,0:T(8,128)(2,1)S(1)}, u32[]{:S(2)}, u32[]{:S(2)}) collective-permute-start(bf16[2,128,256]{2,1,0:T(8,128)(2,1)S(1)} %get-tuple-element.28), channel_id=1, source_target_pairs={{0,24},{4,28},{8,16},{12,20},{16,8},{20,12},{24,0},{28,4},{1,25},{... | collective-permute-start | bytes 393224 | tf_op jit(solution)/shard_map/ppermute | solution.py:369
  17.1 6.9 %collective-permute-start.10 = (bf16[2,128,256]{2,1,0:T(8,128)(2,1)S(1)}, bf16[2,128,256]{2,1,0:T(8,128)(2,1)S(1)}, u32[]{:S(2)}, u32[]{:S(2)}) collective-permute-start(bf16[2,128,256]{2,1,0:T(8,128)(2,1)S(1)} %collective-permute-done.9.refs_0_), channel_id=1, source_target_pairs={{0,1},{1,0},{2,3},{3,2},{4,5},{5,4},{6,7},{7,6},{8,9},{9,8},{10,11... | collective-permute-start | bytes 393224 | tf_op jit(solution)/shard_map/ppermute | solution.py:369
  18.9 9.0 %collective-permute-start.11 = (bf16[2,128,256]{2,1,0:T(8,128)(2,1)S(1)}, bf16[2,128,256]{2,1,0:T(8,128)(2,1)S(1)}, u32[]{:S(2)}, u32[]{:S(2)}) collective-permute-start(bf16[2,128,256]{2,1,0:T(8,128)(2,1)S(1)} %collective-permute-done.9.refs_0_), channel_id=1, source_target_pairs={{0,2},{1,3},{2,0},{3,1},{4,6},{5,7},{6,4},{7,5},{8,10},{9,11},{10,... | collective-permute-start | bytes 393224 | tf_op jit(solution)/shard_map/ppermute | solution.py:369
  20.5 7.5 %collective-permute-start.12 = (bf16[2,128,256]{2,1,0:T(8,128)(2,1)S(1)}, bf16[2,128,256]{2,1,0:T(8,128)(2,1)S(1)}, u32[]{:S(2)}, u32[]{:S(2)}) collective-permute-start(bf16[2,128,256]{2,1,0:T(8,128)(2,1)S(1)} %collective-permute-done.9.refs_0_), channel_id=1, source_target_pairs={{0,3},{1,2},{2,1},{3,0},{4,7},{5,6},{6,5},{7,4},{8,11},{9,10},{10,... | collective-permute-start | bytes 393224 | tf_op jit(solution)/shard_map/ppermute | solution.py:369
  20.6 9.1 %collective-permute-start.14 = (bf16[2,128,256]{2,1,0:T(8,128)(2,1)S(1)}, bf16[2,128,256]{2,1,0:T(8,128)(2,1)S(1)}, u32[]{:S(2)}, u32[]{:S(2)}) collective-permute-start(bf16[2,128,256]{2,1,0:T(8,128)(2,1)S(1)} %collective-permute-done.13.refs_4_), channel_id=1, source_target_pairs={{0,1},{1,0},{2,3},{3,2},{4,5},{5,4},{6,7},{7,6},{8,9},{9,8},{10,11... | collective-permute-start | bytes 393224 | tf_op jit(solution)/shard_map/ppermute | solution.py:369
  22.4 9.5 %collective-permute-start.15 = (bf16[2,128,256]{2,1,0:T(8,128)(2,1)S(1)}, bf16[2,128,256]{2,1,0:T(8,128)(2,1)S(1)}, u32[]{:S(2)}, u32[]{:S(2)}) collective-permute-start(bf16[2,128,256]{2,1,0:T(8,128)(2,1)S(1)} %collective-permute-done.13.refs_4_), channel_id=1, source_target_pairs={{0,2},{1,3},{2,0},{3,1},{4,6},{5,7},{6,4},{7,5},{8,10},{9,11},{10,... | collective-permute-start | bytes 393224 | tf_op jit(solution)/shard_map/ppermute | solution.py:369
  24.0 9.5 %collective-permute-start.16 = (bf16[2,128,256]{2,1,0:T(8,128)(2,1)S(1)}, bf16[2,128,256]{2,1,0:T(8,128)(2,1)S(1)}, u32[]{:S(2)}, u32[]{:S(2)}) collective-permute-start(bf16[2,128,256]{2,1,0:T(8,128)(2,1)S(1)} %collective-permute-done.13.refs_4_), channel_id=1, source_target_pairs={{0,3},{1,2},{2,1},{3,0},{4,7},{5,6},{6,5},{7,4},{8,11},{9,10},{10,... | collective-permute-start | bytes 393224 | tf_op jit(solution)/shard_map/ppermute | solution.py:369
  27.9 8.5 %collective-permute-start = (bf16[3,128,256]{2,1,0:T(8,128)(2,1)S(1)}, bf16[3,128,256]{2,1,0:T(8,128)(2,1)S(1)}, u32[]{:S(2)}, u32[]{:S(2)}) collective-permute-start(bf16[3,128,256]{2,1,0:T(8,128)(2,1)S(1)} %get-tuple-element.21.refs_0_), channel_id=1, source_target_pairs={{0,1},{1,0},{2,3},{3,2},{4,5},{5,4},{6,7},{7,6},{8,9},{9,8},{10,11... | collective-permute-start | bytes 589832 | tf_op jit(solution)/shard_map/ppermute | solution.py:369
  28.0 10.2 %collective-permute-start.1 = (bf16[3,128,256]{2,1,0:T(8,128)(2,1)S(1)}, bf16[3,128,256]{2,1,0:T(8,128)(2,1)S(1)}, u32[]{:S(2)}, u32[]{:S(2)}) collective-permute-start(bf16[3,128,256]{2,1,0:T(8,128)(2,1)S(1)} %get-tuple-element.21.refs_0_), channel_id=1, source_target_pairs={{0,2},{1,3},{2,0},{3,1},{4,6},{5,7},{6,4},{7,5},{8,10},{9,11},{10,... | collective-permute-start | bytes 589832 | tf_op jit(solution)/shard_map/ppermute | solution.py:369
  29.7 9.8 %collective-permute-start.2 = (bf16[3,128,256]{2,1,0:T(8,128)(2,1)S(1)}, bf16[3,128,256]{2,1,0:T(8,128)(2,1)S(1)}, u32[]{:S(2)}, u32[]{:S(2)}) collective-permute-start(bf16[3,128,256]{2,1,0:T(8,128)(2,1)S(1)} %get-tuple-element.21.refs_0_), channel_id=1, source_target_pairs={{0,3},{1,2},{2,1},{3,0},{4,7},{5,6},{6,5},{7,4},{8,11},{9,10},{10,... | collective-permute-start | bytes 589832 | tf_op jit(solution)/shard_map/ppermute | solution.py:369
  33.6 20.3 %collective-permute-start.18 = (bf16[256,1536]{1,0:T(8,128)(2,1)S(1)}, bf16[256,1536]{1,0:T(8,128)(2,1)S(1)}, u32[]{:S(2)}, u32[]{:S(2)}) collective-permute-start(bf16[256,1536]{1,0:T(8,128)(2,1)S(1)} %get-tuple-element.30.refs_3_.refs_2_), channel_id=1, source_target_pairs={{0,4},{4,0},{8,12},{12,8},{16,20},{20,16},{24,28},{28,24},{1,5},{5... | collective-permute-start | bytes 2359304 | tf_op jit(solution)/shard_map/ppermute | solution.py:369
  33.7 14.3 %collective-permute-start.4 = (bf16[5,128,256]{2,1,0:T(8,128)(2,1)S(1)}, bf16[5,128,256]{2,1,0:T(8,128)(2,1)S(1)}, u32[]{:S(2)}, u32[]{:S(2)}) collective-permute-start(bf16[5,128,256]{2,1,0:T(8,128)(2,1)S(1)} %get-tuple-element.22.refs_4_), channel_id=1, source_target_pairs={{0,8},{4,12},{8,0},{12,4},{16,24},{20,28},{24,16},{28,20},{1,9},{5... | collective-permute-start | bytes 983048 | tf_op jit(solution)/shard_map/ppermute | solution.py:369
  39.7 8.4 %collective-permute-start.6 = (bf16[3,128,256]{2,1,0:T(8,128)(2,1)S(1)}, bf16[3,128,256]{2,1,0:T(8,128)(2,1)S(1)}, u32[]{:S(2)}, u32[]{:S(2)}) collective-permute-start(bf16[3,128,256]{2,1,0:T(8,128)(2,1)S(1)} %get-tuple-element.24), channel_id=1, source_target_pairs={{0,8},{4,12},{8,0},{12,4},{16,24},{20,28},{24,16},{28,20},{1,9},{5... | collective-permute-start | bytes 589832 | tf_op jit(solution)/shard_map/ppermute | solution.py:369
  40.7 9.2 %collective-permute-start.3 = (bf16[128,2048]{1,0:T(8,128)(2,1)S(1)}, bf16[128,2048]{1,0:T(8,128)(2,1)S(1)}, u32[]{:S(2)}, u32[]{:S(2)}) collective-permute-start(bf16[128,2048]{1,0:T(8,128)(2,1)S(1)} %get-tuple-element.23.refs_0_), channel_id=1, source_target_pairs={{0,4},{4,0},{8,12},{12,8},{16,20},{20,16},{24,28},{28,24},{1,5},{5... | collective-permute-start | bytes 1572872 | tf_op jit(solution)/shard_map/ppermute | solution.py:369
  40.7 9.2 %collective-permute-start.8 = (bf16[512,512]{1,0:T(8,128)(2,1)S(1)}, bf16[512,512]{1,0:T(8,128)(2,1)S(1)}, u32[]{:S(2)}, u32[]{:S(2)}) collective-permute-start(bf16[512,512]{1,0:T(8,128)(2,1)S(1)} %get-tuple-element.25.refs_6_), channel_id=1, source_target_pairs={{0,4},{4,0},{8,12},{12,8},{16,20},{20,16},{24,28},{28,24},{1,5},{5... | collective-permute-start | bytes 1572872 | tf_op jit(solution)/shard_map/ppermute | solution.py:369
  48.1 1.4 %collective-permute-start.7 = (bf16[3,128,256]{2,1,0:T(8,128)(2,1)S(1)}, bf16[3,128,256]{2,1,0:T(8,128)(2,1)S(1)}, u32[]{:S(2)}, u32[]{:S(2)}) collective-permute-start(bf16[3,128,256]{2,1,0:T(8,128)(2,1)S(1)} %collective-permute-done.6.refs_4_), channel_id=1, source_target_pairs={{0,4},{4,0},{8,12},{12,8},{16,20},{20,16},{24,28},{28,24},{1,5},{5... | collective-permute-start | bytes 589832 | tf_op jit(solution)/shard_map/ppermute | solution.py:369
  48.1 1.9 %collective-permute-start.5 = (bf16[5,128,256]{2,1,0:T(8,128)(2,1)S(1)}, bf16[5,128,256]{2,1,0:T(8,128)(2,1)S(1)}, u32[]{:S(2)}, u32[]{:S(2)}) collective-permute-start(bf16[5,128,256]{2,1,0:T(8,128)(2,1)S(1)} %collective-permute-done.4.refs_2_), channel_id=1, source_target_pairs={{0,4},{4,0},{8,12},{12,8},{16,20},{20,16},{24,28},{28,24},{1,5},{5... | collective-permute-start | bytes 983048 | tf_op jit(solution)/shard_map/ppermute | solution.py:369
  49.5 3.2 %collective-permute-start.17 = (bf16[256,512]{1,0:T(8,128)(2,1)S(1)}, bf16[256,512]{1,0:T(8,128)(2,1)S(1)}, u32[]{:S(2)}, u32[]{:S(2)}) collective-permute-start(bf16[256,512]{1,0:T(8,128)(2,1)S(1)} %get-tuple-element.29.refs_2_), channel_id=1, source_target_pairs={{0,4},{4,0},{8,12},{12,8},{16,20},{20,16},{24,28},{28,24},{1,5},{5... | collective-permute-start | bytes 786440 | tf_op jit(solution)/shard_map/ppermute | solution.py:369

commit v5 on v4

--- a/solution.py
+++ b/solution.py
@@ -92,10 +92,16 @@
 def pack_kernel(
     chips, parts, counts_ref, sources_hbm, feat_ref, cot_ref, tiles_ref, w1_ref, w2_ref, *outs
 ):
-    for_chips, for_reps, for_next, sems, sources_ref, index_sem = outs
+    for_chips, for_reps, for_next, sems, sources_ref, index_sem, tiles_s = outs
     index_copy = pltpu.make_async_copy(sources_hbm, sources_ref, index_sem)
     index_copy.start()
     _, slots, block, _ = tiles_ref.shape
+
+    def tile_copy(k):
+        return pltpu.make_async_copy(tiles_ref.at[0, k], tiles_s.at[k], sems.at[k])
+
+    for k in range(slots):
+        pl.when(k < counts_ref[0])(lambda k=k: tile_copy(k).start())
     width = feat_ref.shape[1]
     core = lax.rem(lax.axis_index("row"), CORES)
     moves = [
@@ -115,23 +121,21 @@
         for n in range(2):
             pl.when(core == c)(lambda ref=ref, n=n: weight_copy(ref, n).start())
     for_next[1:] = jnp.zeros_like(for_next[1:])
-    index_copy.wait()
-
-    def tile_copy(k):
-        source = sources_ref[0, k]
-        position = lax.rem(source, CORES) * chips + lax.div(source, CORES)
-        columns = pl.ds(pl.multiple_of(lax.rem(position, parts) * block, block), block)
-        target = for_next.at[1 + lax.div(position, parts), :, columns]
-        return pltpu.make_async_copy(tiles_ref.at[0, k], target, sems.at[k])
-
-    for k in range(slots):
-        pl.when(k < counts_ref[0])(lambda k=k: tile_copy(k).start())
     for copy in copies:
         copy.wait()
     for_chips[0] = for_reps[0]
     for_next[0] = for_reps[0]
+    index_copy.wait()
+
+    def place(k):
+        tile_copy(k).wait()
+        source = sources_ref[0, k]
+        position = lax.rem(source, CORES) * chips + lax.div(source, CORES)
+        columns = at(lax.rem(position, parts), block)
+        for_next[1 + lax.div(position, parts), :, columns] = tiles_s[k]
+
     for k in range(slots):
-        pl.when(k < counts_ref[0])(lambda k=k: tile_copy(k).wait())
+        pl.when(k < counts_ref[0])(lambda k=k: place(k))
     for_chips[1] = for_next[1 + lax.axis_index("rep")]
     for c, ref in enumerate((w1_ref, w2_ref)):
         for n in range(2):
@@ -234,12 +238,12 @@
     parts = [parts_of(bundle, wide, 2 * height) for bundle in bundles]
     for k, (_, cotangent, _) in enumerate(parts):
         ba_s[k] = back_aggregates(cotangent, w_ref[1])
+    for b, (_, _, a) in enumerate(parts):
+        terms = (dot(a(k), feats, ((1,), (0,))) for k, (feats, _, _) in enumerate(parts))
+        agg_ref[b] = total_of(terms)
     for b in range(2 * CORES):
         terms = (dot(a(b), ba_s[k], ((0,), (0,))) for k, (_, _, a) in enumerate(parts))
         back_ref[b] = total_of(terms)
-    for b, (_, _, a) in enumerate(parts):
-        terms = (dot(a(k), feats, ((1,), (0,))) for k, (feats, _, _) in enumerate(parts))
-        agg_ref[b] = total_of(terms)
 
 
 def middle_kernel(*refs):
@@ -249,11 +253,11 @@
     parts = [parts_of(bundle, w_ref.shape[1], step) for bundle in bundles]
     feats, cotangent, a = parts[CORES]
     back_agg = back_aggregates(cotangent, w_ref[1])
-    for b in range(2 * CORES):
-        back_ref[b] = back_in[b] + dot(a(b), back_agg, ((0,), (0,)))
     for b in range(CORES):
         agg_ref[b] = agg_in[b] + dot(parts[b][2](CORES), feats, ((1,), (0,)))
     agg_ref[CORES] = total_of(dot(a(k), parts[k][0], ((1,), (0,))) for k in range(CORES + 1))
+    for b in range(2 * CORES):
+        back_ref[b] = back_in[b] + dot(a(b), back_agg, ((0,), (0,)))
 
 
 def activate(total, weight, agg_ref, hidden_ref, slope_ref):
@@ -306,16 +310,14 @@
     back_pre, agg_second = [], []
     for b in range(count):
         a = parts[b][2]
+        agg = total_of(dot(a(k), hidden[k][:, my_cols], ((1,), (0,))) for k in range(count))
+        agg_second.append(agg.astype(BF16))
         back_hidden = back_ref[b] + dot(parts[last][2](b), back_agg, ((0,), (0,)))
         back_pre.append((back_hidden * slope[b][...]).astype(BF16))
     gf = total_of(
         dot(agg_first[b][:, my_cols], back_pre[b], ((0,), (0,))) for b in range(count)
     )
     gf_ref[...] = gf * scale
-    for b in range(count):
-        a = parts[b][2]
-        agg = total_of(dot(a(k), hidden[k][:, my_cols], ((1,), (0,))) for k in range(count))
-        agg_second.append(agg.astype(BF16))
     gs = total_of(dot(agg_second[b], parts[b][1], ((0,), (0,))) for b in range(count))
     gs_ref[...] = gs * scale
 
@@ -360,6 +362,7 @@
             pltpu.SemaphoreType.DMA((slots + 4,)),
             pltpu.SMEM(sources.shape, sources.dtype),
             pltpu.SemaphoreType.DMA,
+            pltpu.VMEM(edge_tiles.shape[1:], BF16),
         ],
         compiler_params=limit,
         name="pack",

time: 57.3 us -> 56.2 us (0.981)
  Pallas kernels: 9.06 us -> 8.05 us
    pallas_call x1, Pallas kernels: 1.76 us -> 1.09 us  [whole_body(): pl.pallas_call(functools.partial(pack_kernel, chips, share // block), out...]
where the time goes in v5:
time: 56.2 us; the launch traced here: 56 us
  waiting for transfers between devices  25.7 us (46%)
  starting transfers between devices  20.9 us (37%)
  Pallas kernels  8.05 us (14%)
  between operations  1.37 us (2%)
    ppermute x19, waiting for transfers between devices, swap(): return lax.ppermute(value, axis, [(i, i ^ d) for i in range(size)])  25.7 us
    ppermute x19, starting transfers between devices, swap(): return lax.ppermute(value, axis, [(i, i ^ d) for i in range(size)])  20.9 us
    pallas_call x6, Pallas kernels, local(): pl.pallas_call(kernel, out_shape=outs, in_specs=[vmem] * len(operands), o...  6.96 us
  transfers between devices with their start and end apart: 19, of which 9 were waited for; matrix products, arithmetic and copies ran while one was open for 0% of the time, Pallas kernels for 7%

profile of v5, /device:TPU:0, one launch (start us, length us, event | category | flops | bytes accessed | tf_op | source)
XLA Modules:
  0.0 56.0 jit_solution(10564723300616950315)
XLA Ops:
  1.3 1.1 %pack.1 = (bf16[2,128,256]{2,1,0:T(8,128)(2,1)S(1)}, bf16[3,128,256]{2,1,0:T(8,128)(2,1)S(1)}, bf16[5,128,256]{2,1,0:T(8,128)(2,1)S(1)}) custom-call(s32[1]{0:T(128)S(6)} %copy.10.counts_ref, s32[1,8]{1,0:T(1,128)} %sources_hbm.1, bf16[128,128]{1,0:T(8,128)(2,1)} %feat_ref.1, bf16[128,128]{1,0:T(8,128)(2,1)} %cot_ref.1, bf16[1,8,128,128]{3,2,1,0:T(8,128)(2,1)} %tiles_ref.1, ...), custom_call_target="tpu_custom_call" | custom-call | tf_op jit(solution)/shard_map/pack/pallas_call | solution.py:352
  2.4 4.1 %collective-permute-start.9 = (bf16[2,128,256]{2,1,0:T(8,128)(2,1)S(1)}, bf16[2,128,256]{2,1,0:T(8,128)(2,1)S(1)}, u32[]{:S(2)}, u32[]{:S(2)}) collective-permute-start(bf16[2,128,256]{2,1,0:T(8,128)(2,1)S(1)} %get-tuple-element.28), channel_id=1, source_target_pairs={{0,16},{4,20},{8,24},{12,28},{16,0},{20,4},{24,8},{28,12},{1,17},{... | collective-permute-start | bytes 393224 | tf_op jit(solution)/shard_map/ppermute | solution.py:372
  6.5 1.3 %collective-permute-start.13 = (bf16[2,128,256]{2,1,0:T(8,128)(2,1)S(1)}, bf16[2,128,256]{2,1,0:T(8,128)(2,1)S(1)}, u32[]{:S(2)}, u32[]{:S(2)}) collective-permute-start(bf16[2,128,256]{2,1,0:T(8,128)(2,1)S(1)} %get-tuple-element.28), channel_id=1, source_target_pairs={{0,24},{4,28},{8,16},{12,20},{16,8},{20,12},{24,0},{28,4},{1,25},{... | collective-permute-start | bytes 393224 | tf_op jit(solution)/shard_map/ppermute | solution.py:372
  7.8 8.6 %collective-permute-done.9.refs_0_ = bf16[2,128,256]{2,1,0:T(8,128)(2,1)S(1)} collective-permute-done((bf16[2,128,256]{2,1,0:T(8,128)(2,1)S(1)}, bf16[2,128,256]{2,1,0:T(8,128)(2,1)S(1)}, u32[]{:S(2)}, u32[]{:S(2)}) %collective-permute-start.9) | collective-permute-done | bytes 131104 | tf_op jit(solution)/shard_map/ppermute | solution.py:372
  16.4 1.8 %collective-permute-start.10 = (bf16[2,128,256]{2,1,0:T(8,128)(2,1)S(1)}, bf16[2,128,256]{2,1,0:T(8,128)(2,1)S(1)}, u32[]{:S(2)}, u32[]{:S(2)}) collective-permute-start(bf16[2,128,256]{2,1,0:T(8,128)(2,1)S(1)} %collective-permute-done.9.refs_0_), channel_id=1, source_target_pairs={{0,1},{1,0},{2,3},{3,2},{4,5},{5,4},{6,7},{7,6},{8,9},{9,8},{10,11... | collective-permute-start | bytes 393224 | tf_op jit(solution)/shard_map/ppermute | solution.py:372
  18.3 1.5 %collective-permute-start.11 = (bf16[2,128,256]{2,1,0:T(8,128)(2,1)S(1)}, bf16[2,128,256]{2,1,0:T(8,128)(2,1)S(1)}, u32[]{:S(2)}, u32[]{:S(2)}) collective-permute-start(bf16[2,128,256]{2,1,0:T(8,128)(2,1)S(1)} %collective-permute-done.9.refs_0_), channel_id=1, source_target_pairs={{0,2},{1,3},{2,0},{3,1},{4,6},{5,7},{6,4},{7,5},{8,10},{9,11},{10,... | collective-permute-start | bytes 393224 | tf_op jit(solution)/shard_map/ppermute | solution.py:372
  19.9 1.8 %collective-permute-start.14 = (bf16[2,128,256]{2,1,0:T(8,128)(2,1)S(1)}, bf16[2,128,256]{2,1,0:T(8,128)(2,1)S(1)}, u32[]{:S(2)}, u32[]{:S(2)}) collective-permute-start(bf16[2,128,256]{2,1,0:T(8,128)(2,1)S(1)} %collective-permute-done.13.refs_4_), channel_id=1, source_target_pairs={{0,1},{1,0},{2,3},{3,2},{4,5},{5,4},{6,7},{7,6},{8,9},{9,8},{10,11... | collective-permute-start | bytes 393224 | tf_op jit(solution)/shard_map/ppermute | solution.py:372
  21.8 1.5 %collective-permute-start.15 = (bf16[2,128,256]{2,1,0:T(8,128)(2,1)S(1)}, bf16[2,128,256]{2,1,0:T(8,128)(2,1)S(1)}, u32[]{:S(2)}, u32[]{:S(2)}) collective-permute-start(bf16[2,128,256]{2,1,0:T(8,128)(2,1)S(1)} %collective-permute-done.13.refs_4_), channel_id=1, source_target_pairs={{0,2},{1,3},{2,0},{3,1},{4,6},{5,7},{6,4},{7,5},{8,10},{9,11},{10,... | collective-permute-start | bytes 393224 | tf_op jit(solution)/shard_map/ppermute | solution.py:372
  23.3 2.3 %collective-permute-start.16 = (bf16[2,128,256]{2,1,0:T(8,128)(2,1)S(1)}, bf16[2,128,256]{2,1,0:T(8,128)(2,1)S(1)}, u32[]{:S(2)}, u32[]{:S(2)}) collective-permute-start(bf16[2,128,256]{2,1,0:T(8,128)(2,1)S(1)} %collective-permute-done.13.refs_4_), channel_id=1, source_target_pairs={{0,3},{1,2},{2,1},{3,0},{4,7},{5,6},{6,5},{7,4},{8,11},{9,10},{10,... | collective-permute-start | bytes 393224 | tf_op jit(solution)/shard_map/ppermute | solution.py:372
  25.6 1.7 %collective-permute-done.11.refs_2_ = bf16[2,128,256]{2,1,0:T(8,128)(2,1)S(1)} collective-permute-done((bf16[2,128,256]{2,1,0:T(8,128)(2,1)S(1)}, bf16[2,128,256]{2,1,0:T(8,128)(2,1)S(1)}, u32[]{:S(2)}, u32[]{:S(2)}) %collective-permute-start.11) | collective-permute-done | bytes 131104 | tf_op jit(solution)/shard_map/ppermute | solution.py:372
  27.3 1.8 %collective-permute-start.1 = (bf16[3,128,256]{2,1,0:T(8,128)(2,1)S(1)}, bf16[3,128,256]{2,1,0:T(8,128)(2,1)S(1)}, u32[]{:S(2)}, u32[]{:S(2)}) collective-permute-start(bf16[3,128,256]{2,1,0:T(8,128)(2,1)S(1)} %get-tuple-element.21.refs_0_), channel_id=1, source_target_pairs={{0,2},{1,3},{2,0},{3,1},{4,6},{5,7},{6,4},{7,5},{8,10},{9,11},{10,... | collective-permute-start | bytes 589832 | tf_op jit(solution)/shard_map/ppermute | solution.py:372
  29.1 2.2 %collective-permute-start.2 = (bf16[3,128,256]{2,1,0:T(8,128)(2,1)S(1)}, bf16[3,128,256]{2,1,0:T(8,128)(2,1)S(1)}, u32[]{:S(2)}, u32[]{:S(2)}) collective-permute-start(bf16[3,128,256]{2,1,0:T(8,128)(2,1)S(1)} %get-tuple-element.21.refs_0_), channel_id=1, source_target_pairs={{0,3},{1,2},{2,1},{3,0},{4,7},{5,6},{6,5},{7,4},{8,11},{9,10},{10,... | collective-permute-start | bytes 589832 | tf_op jit(solution)/shard_map/ppermute | solution.py:372
  31.3 1.6 %collective-permute-done.16.refs_7_ = bf16[2,128,256]{2,1,0:T(8,128)(2,1)S(1)} collective-permute-done((bf16[2,128,256]{2,1,0:T(8,128)(2,1)S(1)}, bf16[2,128,256]{2,1,0:T(8,128)(2,1)S(1)}, u32[]{:S(2)}, u32[]{:S(2)}) %collective-permute-start.16) | collective-permute-done | bytes 131104 | tf_op jit(solution)/shard_map/ppermute | solution.py:372
  33.1 2.7 %collective-permute-done.refs_1_ = bf16[3,128,256]{2,1,0:T(8,128)(2,1)S(1)} collective-permute-done((bf16[3,128,256]{2,1,0:T(8,128)(2,1)S(1)}, bf16[3,128,256]{2,1,0:T(8,128)(2,1)S(1)}, u32[]{:S(2)}, u32[]{:S(2)}) %collective-permute-start) | collective-permute-done | bytes 196640 | tf_op jit(solution)/shard_map/ppermute | solution.py:372
  35.8 1.7 %collective-permute-done.1.refs_2_ = bf16[3,128,256]{2,1,0:T(8,128)(2,1)S(1)} collective-permute-done((bf16[3,128,256]{2,1,0:T(8,128)(2,1)S(1)}, bf16[3,128,256]{2,1,0:T(8,128)(2,1)S(1)}, u32[]{:S(2)}, u32[]{:S(2)}) %collective-permute-start.1) | collective-permute-done | bytes 196640 | tf_op jit(solution)/shard_map/ppermute | solution.py:372
  37.5 1.4 %collective-permute-done.2.refs_3_ = bf16[3,128,256]{2,1,0:T(8,128)(2,1)S(1)} collective-permute-done((bf16[3,128,256]{2,1,0:T(8,128)(2,1)S(1)}, bf16[3,128,256]{2,1,0:T(8,128)(2,1)S(1)}, u32[]{:S(2)}, u32[]{:S(2)}) %collective-permute-start.2) | collective-permute-done | bytes 196640 | tf_op jit(solution)/shard_map/ppermute | solution.py:372
  39.0 1.0 %collective-permute-start.6 = (bf16[3,128,256]{2,1,0:T(8,128)(2,1)S(1)}, bf16[3,128,256]{2,1,0:T(8,128)(2,1)S(1)}, u32[]{:S(2)}, u32[]{:S(2)}) collective-permute-start(bf16[3,128,256]{2,1,0:T(8,128)(2,1)S(1)} %get-tuple-element.24), channel_id=1, source_target_pairs={{0,8},{4,12},{8,0},{12,4},{16,24},{20,28},{24,16},{28,20},{1,9},{5... | collective-permute-start | bytes 589832 | tf_op jit(solution)/shard_map/ppermute | solution.py:372
  40.6 6.8 %collective-permute-done.6.refs_4_ = bf16[3,128,256]{2,1,0:T(8,128)(2,1)S(1)} collective-permute-done((bf16[3,128,256]{2,1,0:T(8,128)(2,1)S(1)}, bf16[3,128,256]{2,1,0:T(8,128)(2,1)S(1)}, u32[]{:S(2)}, u32[]{:S(2)}) %collective-permute-start.6) | collective-permute-done | bytes 196640 | tf_op jit(solution)/shard_map/ppermute | solution.py:372
  47.4 0.5 collective-permute-start.5
  47.9 0.9 %collective-permute-done.7.refs_5_ = bf16[3,128,256]{2,1,0:T(8,128)(2,1)S(1)} collective-permute-done((bf16[3,128,256]{2,1,0:T(8,128)(2,1)S(1)}, bf16[3,128,256]{2,1,0:T(8,128)(2,1)S(1)}, u32[]{:S(2)}, u32[]{:S(2)}) %collective-permute-start.7) | collective-permute-done | bytes 196640 | tf_op jit(solution)/shard_map/ppermute | solution.py:372
  49.3 1.5 %shard_map.95 = (bf16[256,2048]{1,0:T(8,128)(2,1)S(1)}, bf16[256,2048]{1,0:T(8,128)(2,1)S(1)}, bf16[2,512,512]{2,1,0:T(8,128)(2,1)S(1)}, f32[4,256,512]{2,1,0:T(8,128)S(1)}, f32[2,256,512]{2,1,0:T(8,128)S(1)}) custom-call(bf16[128,2048]{1,0:T(8,128)(2,1)S(1)} %get-tuple-element.23.refs_0_, bf16[128,2048]{1,0:T(8,128)(2,1)S(1)} %collective-permute-done.3.refs_1_, ...), custom_call_target="tpu_custom_call" | custom-call | tf_op jit(solution)/shard_map/pallas_call | solution.py:379
  50.8 1.0 %shard_map.97 = (f32[4,256,512]{2,1,0:T(8,128)S(1)}, f32[3,256,512]{2,1,0:T(8,128)S(1)}) custom-call(bf16[256,2048]{1,0:T(8,128)(2,1)S(1)} %get-tuple-element.26.refs_0_, bf16[256,2048]{1,0:T(8,128)(2,1)S(1)} %get-tuple-element.27.refs_1_, bf16[256,512]{1,0:T(8,128)(2,1)S(1)} %get-tuple-element.29.refs_2_, ...), custom_call_target="tpu_custom_call" | custom-call | tf_op jit(solution)/shard_map/pallas_call | solution.py:379
  51.7 1.2 %shard_map.98 = (bf16[3,256,512]{2,1,0:T(8,128)(2,1)S(1)}, bf16[3,256,512]{2,1,0:T(8,128)(2,1)S(1)}, f32[3,256,512]{2,1,0:T(8,128)S(1)}) custom-call(bf16[256,2048]{1,0:T(8,128)(2,1)S(1)} %get-tuple-element.26.refs_0_, bf16[256,2048]{1,0:T(8,128)(2,1)S(1)} %get-tuple-element.27.refs_1_, bf16[256,1536]{1,0:T(8,128)(2,1)S(1)} %get-tuple-element.30.refs_3_.refs_2_, ...), custom_call_target="tpu_custom_call" | custom-call | tf_op jit(solution)/shard_map/pallas_call | solution.py:379
  53.0 3.0 %shard_map.99 = (bf16[128,128]{1,0:T(8,128)(2,1)}, f32[128,512]{1,0:T(8,128)}, f32[128,512]{1,0:T(8,128)}) custom-call(bf16[256,2048]{1,0:T(8,128)(2,1)S(1)} %get-tuple-element.26.refs_0_, bf16[256,2048]{1,0:T(8,128)(2,1)S(1)} %get-tuple-element.27.refs_1_, bf16[256,512]{1,0:T(8,128)(2,1)S(1)} %get-tuple-element.29.refs_2_, ...), custom_call_target="tpu_custom_call" | custom-call | tf_op jit(solution)/shard_map/pallas_call | solution.py:379
  (21 shorter events, 1.5 us)
Async XLA Ops:
  2.4 14.1 %collective-permute-start.9 = (bf16[2,128,256]{2,1,0:T(8,128)(2,1)S(1)}, bf16[2,128,256]{2,1,0:T(8,128)(2,1)S(1)}, u32[]{:S(2)}, u32[]{:S(2)}) collective-permute-start(bf16[2,128,256]{2,1,0:T(8,128)(2,1)S(1)} %get-tuple-element.28), channel_id=1, source_target_pairs={{0,16},{4,20},{8,24},{12,28},{16,0},{20,4},{24,8},{28,12},{1,17},{... | collective-permute-start | bytes 393224 | tf_op jit(solution)/shard_map/ppermute | solution.py:372
  6.5 13.5 %collective-permute-start.13 = (bf16[2,128,256]{2,1,0:T(8,128)(2,1)S(1)}, bf16[2,128,256]{2,1,0:T(8,128)(2,1)S(1)}, u32[]{:S(2)}, u32[]{:S(2)}) collective-permute-start(bf16[2,128,256]{2,1,0:T(8,128)(2,1)S(1)} %get-tuple-element.28), channel_id=1, source_target_pairs={{0,24},{4,28},{8,16},{12,20},{16,8},{20,12},{24,0},{28,4},{1,25},{... | collective-permute-start | bytes 393224 | tf_op jit(solution)/shard_map/ppermute | solution.py:372
  16.4 6.9 %collective-permute-start.10 = (bf16[2,128,256]{2,1,0:T(8,128)(2,1)S(1)}, bf16[2,128,256]{2,1,0:T(8,128)(2,1)S(1)}, u32[]{:S(2)}, u32[]{:S(2)}) collective-permute-start(bf16[2,128,256]{2,1,0:T(8,128)(2,1)S(1)} %collective-permute-done.9.refs_0_), channel_id=1, source_target_pairs={{0,1},{1,0},{2,3},{3,2},{4,5},{5,4},{6,7},{7,6},{8,9},{9,8},{10,11... | collective-permute-start | bytes 393224 | tf_op jit(solution)/shard_map/ppermute | solution.py:372
  18.3 9.0 %collective-permute-start.11 = (bf16[2,128,256]{2,1,0:T(8,128)(2,1)S(1)}, bf16[2,128,256]{2,1,0:T(8,128)(2,1)S(1)}, u32[]{:S(2)}, u32[]{:S(2)}) collective-permute-start(bf16[2,128,256]{2,1,0:T(8,128)(2,1)S(1)} %collective-permute-done.9.refs_0_), channel_id=1, source_target_pairs={{0,2},{1,3},{2,0},{3,1},{4,6},{5,7},{6,4},{7,5},{8,10},{9,11},{10,... | collective-permute-start | bytes 393224 | tf_op jit(solution)/shard_map/ppermute | solution.py:372
  19.8 7.5 %collective-permute-start.12 = (bf16[2,128,256]{2,1,0:T(8,128)(2,1)S(1)}, bf16[2,128,256]{2,1,0:T(8,128)(2,1)S(1)}, u32[]{:S(2)}, u32[]{:S(2)}) collective-permute-start(bf16[2,128,256]{2,1,0:T(8,128)(2,1)S(1)} %collective-permute-done.9.refs_0_), channel_id=1, source_target_pairs={{0,3},{1,2},{2,1},{3,0},{4,7},{5,6},{6,5},{7,4},{8,11},{9,10},{10,... | collective-permute-start | bytes 393224 | tf_op jit(solution)/shard_map/ppermute | solution.py:372
  19.9 9.2 %collective-permute-start.14 = (bf16[2,128,256]{2,1,0:T(8,128)(2,1)S(1)}, bf16[2,128,256]{2,1,0:T(8,128)(2,1)S(1)}, u32[]{:S(2)}, u32[]{:S(2)}) collective-permute-start(bf16[2,128,256]{2,1,0:T(8,128)(2,1)S(1)} %collective-permute-done.13.refs_4_), channel_id=1, source_target_pairs={{0,1},{1,0},{2,3},{3,2},{4,5},{5,4},{6,7},{7,6},{8,9},{9,8},{10,11... | collective-permute-start | bytes 393224 | tf_op jit(solution)/shard_map/ppermute | solution.py:372
  21.8 9.5 %collective-permute-start.15 = (bf16[2,128,256]{2,1,0:T(8,128)(2,1)S(1)}, bf16[2,128,256]{2,1,0:T(8,128)(2,1)S(1)}, u32[]{:S(2)}, u32[]{:S(2)}) collective-permute-start(bf16[2,128,256]{2,1,0:T(8,128)(2,1)S(1)} %collective-permute-done.13.refs_4_), channel_id=1, source_target_pairs={{0,2},{1,3},{2,0},{3,1},{4,6},{5,7},{6,4},{7,5},{8,10},{9,11},{10,... | collective-permute-start | bytes 393224 | tf_op jit(solution)/shard_map/ppermute | solution.py:372
  23.3 9.5 %collective-permute-start.16 = (bf16[2,128,256]{2,1,0:T(8,128)(2,1)S(1)}, bf16[2,128,256]{2,1,0:T(8,128)(2,1)S(1)}, u32[]{:S(2)}, u32[]{:S(2)}) collective-permute-start(bf16[2,128,256]{2,1,0:T(8,128)(2,1)S(1)} %collective-permute-done.13.refs_4_), channel_id=1, source_target_pairs={{0,3},{1,2},{2,1},{3,0},{4,7},{5,6},{6,5},{7,4},{8,11},{9,10},{10,... | collective-permute-start | bytes 393224 | tf_op jit(solution)/shard_map/ppermute | solution.py:372
  27.3 8.6 %collective-permute-start = (bf16[3,128,256]{2,1,0:T(8,128)(2,1)S(1)}, bf16[3,128,256]{2,1,0:T(8,128)(2,1)S(1)}, u32[]{:S(2)}, u32[]{:S(2)}) collective-permute-start(bf16[3,128,256]{2,1,0:T(8,128)(2,1)S(1)} %get-tuple-element.21.refs_0_), channel_id=1, source_target_pairs={{0,1},{1,0},{2,3},{3,2},{4,5},{5,4},{6,7},{7,6},{8,9},{9,8},{10,11... | collective-permute-start | bytes 589832 | tf_op jit(solution)/shard_map/ppermute | solution.py:372
  27.3 10.2 %collective-permute-start.1 = (bf16[3,128,256]{2,1,0:T(8,128)(2,1)S(1)}, bf16[3,128,256]{2,1,0:T(8,128)(2,1)S(1)}, u32[]{:S(2)}, u32[]{:S(2)}) collective-permute-start(bf16[3,128,256]{2,1,0:T(8,128)(2,1)S(1)} %get-tuple-element.21.refs_0_), channel_id=1, source_target_pairs={{0,2},{1,3},{2,0},{3,1},{4,6},{5,7},{6,4},{7,5},{8,10},{9,11},{10,... | collective-permute-start | bytes 589832 | tf_op jit(solution)/shard_map/ppermute | solution.py:372
  29.1 9.8 %collective-permute-start.2 = (bf16[3,128,256]{2,1,0:T(8,128)(2,1)S(1)}, bf16[3,128,256]{2,1,0:T(8,128)(2,1)S(1)}, u32[]{:S(2)}, u32[]{:S(2)}) collective-permute-start(bf16[3,128,256]{2,1,0:T(8,128)(2,1)S(1)} %get-tuple-element.21.refs_0_), channel_id=1, source_target_pairs={{0,3},{1,2},{2,1},{3,0},{4,7},{5,6},{6,5},{7,4},{8,11},{9,10},{10,... | collective-permute-start | bytes 589832 | tf_op jit(solution)/shard_map/ppermute | solution.py:372
  33.0 20.0 %collective-permute-start.18 = (bf16[256,1536]{1,0:T(8,128)(2,1)S(1)}, bf16[256,1536]{1,0:T(8,128)(2,1)S(1)}, u32[]{:S(2)}, u32[]{:S(2)}) collective-permute-start(bf16[256,1536]{1,0:T(8,128)(2,1)S(1)} %get-tuple-element.30.refs_3_.refs_2_), channel_id=1, source_target_pairs={{0,4},{4,0},{8,12},{12,8},{16,20},{20,16},{24,28},{28,24},{1,5},{5... | collective-permute-start | bytes 2359304 | tf_op jit(solution)/shard_map/ppermute | solution.py:372
  33.1 14.3 %collective-permute-start.4 = (bf16[5,128,256]{2,1,0:T(8,128)(2,1)S(1)}, bf16[5,128,256]{2,1,0:T(8,128)(2,1)S(1)}, u32[]{:S(2)}, u32[]{:S(2)}) collective-permute-start(bf16[5,128,256]{2,1,0:T(8,128)(2,1)S(1)} %get-tuple-element.22.refs_4_), channel_id=1, source_target_pairs={{0,8},{4,12},{8,0},{12,4},{16,24},{20,28},{24,16},{28,20},{1,9},{5... | collective-permute-start | bytes 983048 | tf_op jit(solution)/shard_map/ppermute | solution.py:372
  39.0 8.3 %collective-permute-start.6 = (bf16[3,128,256]{2,1,0:T(8,128)(2,1)S(1)}, bf16[3,128,256]{2,1,0:T(8,128)(2,1)S(1)}, u32[]{:S(2)}, u32[]{:S(2)}) collective-permute-start(bf16[3,128,256]{2,1,0:T(8,128)(2,1)S(1)} %get-tuple-element.24), channel_id=1, source_target_pairs={{0,8},{4,12},{8,0},{12,4},{16,24},{20,28},{24,16},{28,20},{1,9},{5... | collective-permute-start | bytes 589832 | tf_op jit(solution)/shard_map/ppermute | solution.py:372
  40.1 9.2 %collective-permute-start.3 = (bf16[128,2048]{1,0:T(8,128)(2,1)S(1)}, bf16[128,2048]{1,0:T(8,128)(2,1)S(1)}, u32[]{:S(2)}, u32[]{:S(2)}) collective-permute-start(bf16[128,2048]{1,0:T(8,128)(2,1)S(1)} %get-tuple-element.23.refs_0_), channel_id=1, source_target_pairs={{0,4},{4,0},{8,12},{12,8},{16,20},{20,16},{24,28},{28,24},{1,5},{5... | collective-permute-start | bytes 1572872 | tf_op jit(solution)/shard_map/ppermute | solution.py:372
  40.1 9.2 %collective-permute-start.8 = (bf16[512,512]{1,0:T(8,128)(2,1)S(1)}, bf16[512,512]{1,0:T(8,128)(2,1)S(1)}, u32[]{:S(2)}, u32[]{:S(2)}) collective-permute-start(bf16[512,512]{1,0:T(8,128)(2,1)S(1)} %get-tuple-element.25.refs_6_), channel_id=1, source_target_pairs={{0,4},{4,0},{8,12},{12,8},{16,20},{20,16},{24,28},{28,24},{1,5},{5... | collective-permute-start | bytes 1572872 | tf_op jit(solution)/shard_map/ppermute | solution.py:372
  47.4 1.4 %collective-permute-start.7 = (bf16[3,128,256]{2,1,0:T(8,128)(2,1)S(1)}, bf16[3,128,256]{2,1,0:T(8,128)(2,1)S(1)}, u32[]{:S(2)}, u32[]{:S(2)}) collective-permute-start(bf16[3,128,256]{2,1,0:T(8,128)(2,1)S(1)} %collective-permute-done.6.refs_4_), channel_id=1, source_target_pairs={{0,4},{4,0},{8,12},{12,8},{16,20},{20,16},{24,28},{28,24},{1,5},{5... | collective-permute-start | bytes 589832 | tf_op jit(solution)/shard_map/ppermute | solution.py:372
  47.4 1.9 %collective-permute-start.5 = (bf16[5,128,256]{2,1,0:T(8,128)(2,1)S(1)}, bf16[5,128,256]{2,1,0:T(8,128)(2,1)S(1)}, u32[]{:S(2)}, u32[]{:S(2)}) collective-permute-start(bf16[5,128,256]{2,1,0:T(8,128)(2,1)S(1)} %collective-permute-done.4.refs_2_), channel_id=1, source_target_pairs={{0,4},{4,0},{8,12},{12,8},{16,20},{20,16},{24,28},{28,24},{1,5},{5... | collective-permute-start | bytes 983048 | tf_op jit(solution)/shard_map/ppermute | solution.py:372
  48.8 2.9 %collective-permute-start.17 = (bf16[256,512]{1,0:T(8,128)(2,1)S(1)}, bf16[256,512]{1,0:T(8,128)(2,1)S(1)}, u32[]{:S(2)}, u32[]{:S(2)}) collective-permute-start(bf16[256,512]{1,0:T(8,128)(2,1)S(1)} %get-tuple-element.29.refs_2_), channel_id=1, source_target_pairs={{0,4},{4,0},{8,12},{12,8},{16,20},{20,16},{24,28},{28,24},{1,5},{5... | collective-permute-start | bytes 786440 | tf_op jit(solution)/shard_map/ppermute | solution.py:372
